TPU v7x, 512 devices: a whole 4x4x16 slice. The times are simulated.
512 devices in a mesh: client: 32 (over z, core), param: 16 (over x, y).
Axes of the slice: x: 4, y: 4, z: 16, core: 2. Of those that a mesh axis runs over, the one named last changes fastest.
Arguments:
- inputs: bfloat16 [32, 384, 2304], P('client', None, 'param'), may hold values from -6 to 6
- targets: bfloat16 [32, 384, 2304], P('client', None, 'param'), may hold values from -35 to 35
- norm_gain: float32 [2304], replicated, may hold values from 0.1 to 1.9
- gate_weight: bfloat16 [2304, 4608], P(None, 'param'), may hold values from -0.125 to 0.125
- up_weight: bfloat16 [2304, 4608], P(None, 'param'), may hold values from -0.125 to 0.125
- down_weight: bfloat16 [4608, 2304], P('param'), may hold values from -0.09375 to 0.09375
- neighbours: int32 [32], replicated, may hold values from 9 to 30
Outputs:
- update_gate: float32 [2304, 4608], P('client', 'param')
- update_up: float32 [2304, 4608], P('client', 'param')
- update_down: float32 [2304, 4608], P('client', 'param')
- relative_weight: float32 [32], replicated
All inputs are finite; a program needn't handle non-finite values.
Results may differ from a plain program's by a relative error of at most 0.0095.
Values may be sent and summed in bfloat16 or wider, within the bound.
No kernel may reach another device: no remote copies, remote signals or barrier semaphores. Data moves between devices by JAX's collectives and lax.ppermute only.
A program may use at most 64 MiB of HBM per device.

v0:
```python
import math

import jax
import jax.numpy as jnp
from jax import lax
from jax.sharding import PartitionSpec as P


def gelu_tanh(values):
    return jax.nn.gelu(values, approximate=True)


def rms_normed(gathered, norm_gain):
    widened = gathered.astype(jnp.float32)
    inverse_rms = lax.rsqrt(jnp.mean(widened * widened, axis=-1, keepdims=True) + 1e-06)
    return (widened * inverse_rms * norm_gain).astype(jnp.bfloat16)


def krum_weights(gram, neighbours):
    client_count = gram.shape[0]
    diagonal = jnp.diagonal(gram)
    distance = diagonal[:, None] + diagonal[None, :] - 2.0 * gram
    row_index = lax.broadcasted_iota(jnp.int32, (client_count, client_count), 0)
    col_index = lax.broadcasted_iota(jnp.int32, (client_count, client_count), 1)
    distance = jnp.where(row_index == col_index, jnp.asarray(1e30, gram.dtype), distance)
    ordered = jnp.sort(distance, axis=1)
    scores = jnp.sum(
        jnp.where(col_index < neighbours[:, None], ordered, jnp.zeros_like(ordered)), axis=1
    )
    scaled = scores / jnp.mean(scores)
    exponent = jnp.exp(-4.0 * scaled)
    return exponent / jnp.sum(exponent)


def token_contract(left, right):
    return lax.dot_general(
        left, right, (((0,), (0,)), ((), ())), preferred_element_type=jnp.float32
    )


def pair_products(exchanged):
    flattened = exchanged.reshape(exchanged.shape[0], -1)
    return lax.dot_general(
        flattened, flattened, (((1,), (1,)), ((), ())), preferred_element_type=jnp.float32
    )


def weighted_sum(weights, exchanged):
    return jnp.sum(weights[:, None, None] * exchanged.astype(jnp.float32), axis=0)


def on_device(inputs, targets, norm_gain, gate_weight, up_weight, down_weight, neighbours):
    token_count = inputs.shape[1]
    factor = 1.0 / math.sqrt(token_count)
    gathered, target_rows = (
        lax.all_gather(inputs, "param", axis=2, tiled=True),
        lax.all_gather(targets, "param", axis=2, tiled=True),
    )
    normed = rms_normed(gathered[0], norm_gain)
    gate_value = jnp.dot(normed, gate_weight, preferred_element_type=jnp.float32)
    up_value = jnp.dot(normed, up_weight, preferred_element_type=jnp.float32)
    activated, gelu_back = jax.vjp(gelu_tanh, gate_value)
    hidden = (activated * up_value).astype(jnp.bfloat16)
    partial_out = jnp.dot(hidden, down_weight, preferred_element_type=jnp.float32)
    summed = lax.psum(partial_out.astype(jnp.bfloat16), "param").astype(jnp.float32)
    residual = ((summed - target_rows[0].astype(jnp.float32)) * factor).astype(jnp.bfloat16)
    down_delta = (-token_contract(residual, hidden)).astype(jnp.bfloat16)
    back_hidden = lax.dot_general(
        residual, down_weight, (((1,), (1,)), ((), ())), preferred_element_type=jnp.float32
    )
    back_gate = gelu_back(back_hidden * up_value)[0].astype(jnp.bfloat16)
    back_up = (back_hidden * activated).astype(jnp.bfloat16)
    gate_delta = (-token_contract(normed, back_gate)).astype(jnp.bfloat16)
    up_delta = (-token_contract(normed, back_up)).astype(jnp.bfloat16)
    owned_gate, owned_up, owned_down = (
        lax.all_to_all(gate_delta[None], "client", split_axis=1, concat_axis=0, tiled=True),
        lax.all_to_all(up_delta[None], "client", split_axis=1, concat_axis=0, tiled=True),
        lax.all_to_all(down_delta[None], "client", split_axis=1, concat_axis=0, tiled=True),
    )
    partial_gram = pair_products(owned_gate) + pair_products(owned_up) + pair_products(owned_down)
    gram = lax.psum(partial_gram, ("client", "param"))
    weights = krum_weights(gram, neighbours)
    client_count = lax.axis_size("client")
    update_gate = weighted_sum(weights, owned_gate)
    update_up = weighted_sum(weights, owned_up)
    update_down = weighted_sum(weights, owned_down)
    return (update_gate, update_up, update_down, client_count * weights)


def solution(mesh):
    in_specs = (
        P("client", None, "param"),
        P("client", None, "param"),
        P(),
        P(None, "param"),
        P(None, "param"),
        P("param", None),
        P(),
    )
    out_specs = (P("client", "param"), P("client", "param"), P("client", "param"), P())
    return jax.shard_map(
        on_device, mesh=mesh, in_specs=in_specs, out_specs=out_specs, check_vma=False
    )
```

profile of v0, /device:TPU:1, one launch (start us, length us, event | category | flops | bytes accessed | tf_op | source)
XLA Modules:
  0.0 651.7 jit_solution(12808052381832234853)
XLA Ops:
  7.2 0.7 all-gather.3.cloned.1.call-update
  8.0 0.7 all-gather.5.cloned.1.call-update
  8.7 65.9 %all-gather.3.cloned.1.call-done = bf16[1,384,2304]{1,2,0:T(8,128)(2,1)} async-done(((bf16[1,384,144]{1,2,0:T(8,128)(2,1)}), bf16[1,384,2304]{1,2,0:T(8,128)(2,1)}) %all-gather.3.cloned.1.call-update) | async-done | bytes 1769488 | tf_op jit(solution)/shard_map/all_gather | solution.py:56
  74.6 2.1 fusion.6
  76.7 2.4 fusion.66
  79.1 1.7 multiply_convert_fusion.1
  80.9 2.3 convolution_convert_fusion
  83.2 53.5 %all-gather.5.cloned.1.call-done = bf16[1,384,2304]{1,2,0:T(8,128)(2,1)} async-done(((bf16[1,384,144]{1,2,0:T(8,128)(2,1)}), bf16[1,384,2304]{1,2,0:T(8,128)(2,1)}) %all-gather.5.cloned.1.call-update) | async-done | bytes 1769488 | tf_op jit(solution)/shard_map/all_gather | solution.py:57
  136.7 2.6 copy.29
  139.3 120.3 %all-reduce.2.cloned.1.call-done = bf16[384,2304]{1,0:T(8,128)(2,1)} async-done(((bf16[384,2304]{1,0:T(8,128)(2,1)}), bf16[384,2304]{1,0:T(8,128)(2,1)}) %all-reduce.2.cloned.1.call-update) | async-done | bytes 1769488 | tf_op jit(solution)/shard_map/psum | solution.py:65
  259.6 2.5 fusion.33
  262.2 0.8 copy-done.11
  262.9 2.2 fusion.4
  265.1 8.5 %copy.33 = bf16[1,2304,288]{2,0,1:T(2,128)(2,1)} copy(bf16[1,2304,288]{1,2,0:T(8,128)(2,1)} %fusion.4) | data formatting | bytes 2654208 | tf_op jit(solution)/shard_map/broadcast_in_dim | solution.py:77
  274.1 15.4 %reduce.3 = bf16[2304,288]{1,0:T(8,128)(2,1)S(1)} reduce(bf16[2304,1,288]{2,1,0:T(2,128)(2,1)} %bitcast.48, bf16[]{:T(256)} %broadcast.132), dimensions={1}, to_apply=%bitcast.38.reduce_sub_computation | reduce | bytes 2654210
  289.5 3.7 reshape.93
  293.2 14.8 %all-to-all-start.1 = ((bf16[32,2,10368]{2,1,0:T(2,128)(2,1)}), bf16[32,2,10368]{2,1,0:T(2,128)(2,1)}, u32[]{:S(2)}, u32[]{:S(2)}) async-start(bf16[32,2,10368]{2,1,0:T(2,128)(2,1)} %reshape.93), calls=%async_computation.1 | async-start | bytes 2654208 | tf_op jit(solution)/shard_map/all_to_all | solution.py:77
  308.0 3.6 fusion.5
  311.6 8.5 %copy.30 = bf16[1,2304,288]{2,0,1:T(2,128)(2,1)} copy(bf16[1,2304,288]{1,2,0:T(8,128)(2,1)} %fusion.5) | data formatting | bytes 2654208 | tf_op jit(solution)/shard_map/broadcast_in_dim | solution.py:76
  320.1 15.4 %reduce.2 = bf16[2304,288]{1,0:T(8,128)(2,1)S(1)} reduce(bf16[2304,1,288]{2,1,0:T(2,128)(2,1)} %bitcast.50, bf16[]{:T(256)} %broadcast.132), dimensions={1}, to_apply=%bitcast.36.reduce_sub_computation | reduce | bytes 2654210
  335.5 3.7 reshape.91
  339.2 36.4 %all-to-all-done.1 = bf16[32,2,10368]{2,1,0:T(2,128)(2,1)} async-done(((bf16[32,2,10368]{2,1,0:T(2,128)(2,1)}), bf16[32,2,10368]{2,1,0:T(2,128)(2,1)}, u32[]{:S(2)}, u32[]{:S(2)}) %all-to-all-start.1) | async-done | bytes 1327136 | tf_op jit(solution)/shard_map/all_to_all | solution.py:77
  375.6 4.8 all-to-all-start
  380.4 3.4 fusion.3
  383.8 8.5 %copy.36 = bf16[1,2304,288]{2,0,1:T(2,128)(2,1)} copy(bf16[1,2304,288]{1,2,0:T(8,128)(2,1)} %fusion.3) | data formatting | bytes 2654208 | tf_op jit(solution)/shard_map/broadcast_in_dim | solution.py:78
  392.3 15.4 %reduce.1 = bf16[2304,288]{1,0:T(8,128)(2,1)S(1)} reduce(bf16[2304,1,288]{2,1,0:T(2,128)(2,1)} %bitcast.49, bf16[]{:T(256)} %broadcast.132), dimensions={1}, to_apply=%bitcast.34.reduce_sub_computation | reduce | bytes 2654210
  407.7 3.7 reshape.89
  411.4 36.6 %all-to-all-done = bf16[32,2,10368]{2,1,0:T(2,128)(2,1)} async-done(((bf16[32,2,10368]{2,1,0:T(2,128)(2,1)}), bf16[32,2,10368]{2,1,0:T(2,128)(2,1)}, u32[]{:S(2)}, u32[]{:S(2)}) %all-to-all-start) | async-done | bytes 1327136 | tf_op jit(solution)/shard_map/all_to_all | solution.py:76
  448.0 5.5 all-to-all-start.2
  453.5 11.1 %reshape.94 = bf16[2304,1,288]{2,1,0:T(2,128)(2,1)} reshape(bf16[32,2,10368]{2,1,0:T(2,128)(2,1)} %all-to-all-done.1) | data formatting | bytes 2654208
  464.6 2.3 copy.41
  466.9 11.1 %reshape.92 = bf16[2304,1,288]{2,1,0:T(2,128)(2,1)} reshape(bf16[32,2,10368]{2,1,0:T(2,128)(2,1)} %all-to-all-done) | data formatting | bytes 2654208
  478.1 2.3 copy.40
  480.4 1.2 copy-done.1
  481.6 0.6 fusion.17
  482.2 38.9 %all-to-all-done.2 = bf16[32,2,10368]{2,1,0:T(2,128)(2,1)} async-done(((bf16[32,2,10368]{2,1,0:T(2,128)(2,1)}), bf16[32,2,10368]{2,1,0:T(2,128)(2,1)}, u32[]{:S(2)}, u32[]{:S(2)}) %all-to-all-start.2) | async-done | bytes 1327136 | tf_op jit(solution)/shard_map/all_to_all | solution.py:78
  521.1 11.1 %reshape.90 = bf16[2304,1,288]{2,1,0:T(2,128)(2,1)} reshape(bf16[32,2,10368]{2,1,0:T(2,128)(2,1)} %all-to-all-done.2) | data formatting | bytes 2654208
  532.2 2.3 copy.42
  534.5 0.6 fusion.29
  535.2 0.6 copy-done.2
  535.8 0.6 fusion.26
  536.4 100.0 %psum.15 = f32[32,32]{1,0:T(8,128)S(1)} all-reduce(f32[32,32]{1,0:T(8,128)S(1)} %fusion.26), channel_id=1, replica_groups=mesh['client'=32,'param'=16] {'client','param'}, use_global_device_ids=true, to_apply=%region_2.0 | all-reduce | flops 1024 | bytes 8192 | tf_op jit(solution)/shard_map/psum | solution.py:81
  636.3 0.7 gather_fusion
  637.2 0.9 sort.15
  638.1 0.6 fusion.50
  639.4 0.6 fusion.70
  640.0 1.2 broadcast_multiply_fusion
  641.2 4.0 multiply_reduce_fusion
  (35 shorter events, 0.9 us)
Async XLA Ops:
  7.2 73.7 %copy-start = (bf16[288,2304]{1,0:T(8,128)(2,1)S(1)}, bf16[288,2304]{1,0:T(8,128)(2,1)}, u32[]{:S(2)}) copy-start(bf16[288,2304]{1,0:T(8,128)(2,1)} %param.12) | copy-start | bytes 3981316
  7.2 69.5 %copy-start.10 = (f32[2304]{0:T(1024)S(1)}, f32[2304]{0:T(1024)}, u32[]{:S(2)}) copy-start(f32[2304]{0:T(1024)} %param.9) | copy-start | bytes 27652
  7.2 67.4 %all-gather.3.cloned.1.call-start = ((), (), s32[]{:S(2)}) async-start(), calls=%async_computation.3 | async-start | bytes 1880064 | tf_op jit(solution)/shard_map/all_gather | solution.py:56
  7.9 128.8 %all-gather.5.cloned.1.call-start = ((), (), s32[]{:S(2)}) async-start(), calls=%async_computation.5 | async-start | bytes 1880064 | tf_op jit(solution)/shard_map/all_gather | solution.py:57
  8.7 250.9 %all-reduce.2.cloned.1.call-start = ((), (), s32[]{:S(2)}) async-start(), calls=%async_computation.4 | async-start | bytes 3538944 | tf_op jit(solution)/shard_map/psum | solution.py:65
  74.6 2.1 copy-start.5
  76.7 2.4 copy-start.9
  79.1 1.7 copy-start.12
  139.3 122.8 %copy-start.3 = (bf16[1,384,2304]{2,1,0:T(8,128)(2,1)}, bf16[1,384,2304]{2,1,0:T(8,128)(2,1)S(1)}, u32[]{:S(2)}) copy-start(bf16[1,384,2304]{2,1,0:T(8,128)(2,1)S(1)} %copy.29) | copy-start | bytes 5308420
  259.6 3.3 copy-start.6
  259.6 3.3 copy-start.13
  262.1 0.8 copy-start.11
  293.2 14.8 %copy-start.7 = (bf16[1,384,2304]{1,2,0:T(8,128)(2,1)S(1)}, bf16[1,384,2304]{1,2,0:T(8,128)(2,1)}, u32[]{:S(2)}) copy-start(bf16[1,384,2304]{1,2,0:T(8,128)(2,1)} %all-gather.3.cloned.1.call-done) | copy-start | bytes 5308420
  293.2 82.4 %all-to-all-start.1 = ((bf16[32,2,10368]{2,1,0:T(2,128)(2,1)}), bf16[32,2,10368]{2,1,0:T(2,128)(2,1)}, u32[]{:S(2)}, u32[]{:S(2)}) async-start(bf16[32,2,10368]{2,1,0:T(2,128)(2,1)} %reshape.93), calls=%async_computation.1 | async-start | bytes 2654208 | tf_op jit(solution)/shard_map/all_to_all | solution.py:77
  339.2 41.2 %copy-start.4 = (bf16[1,384,2304]{2,1,0:T(8,128)(2,1)S(1)}, bf16[1,384,2304]{2,1,0:T(8,128)(2,1)}, u32[]{:S(2)}) copy-start(bf16[1,384,2304]{2,1,0:T(8,128)(2,1)} %copy-done.3) | copy-start | bytes 5308420
  375.6 72.4 %all-to-all-start = ((bf16[32,2,10368]{2,1,0:T(2,128)(2,1)}), bf16[32,2,10368]{2,1,0:T(2,128)(2,1)}, u32[]{:S(2)}, u32[]{:S(2)}) async-start(bf16[32,2,10368]{2,1,0:T(2,128)(2,1)} %reshape.91), calls=%async_computation | async-start | bytes 2654208 | tf_op jit(solution)/shard_map/all_to_all | solution.py:76
  448.0 73.1 %all-to-all-start.2 = ((bf16[32,2,10368]{2,1,0:T(2,128)(2,1)}), bf16[32,2,10368]{2,1,0:T(2,128)(2,1)}, u32[]{:S(2)}, u32[]{:S(2)}) async-start(bf16[32,2,10368]{2,1,0:T(2,128)(2,1)} %reshape.89), calls=%async_computation.2 | async-start | bytes 2654208 | tf_op jit(solution)/shard_map/all_to_all | solution.py:78
  480.4 1.2 copy-start.1
  534.5 1.2 copy-start.2
  535.2 103.0 %copy-start.8 = (s32[32]{0:T(128)S(1)}, s32[32]{0:T(128)}, u32[]{:S(2)}) copy-start(s32[32]{0:T(128)} %param.13) | copy-start | bytes 388
Sparse Core Ops, SparseCore 0:
  11.1 63.5 all-gather.2
  77.7 58.9 all-gather.4
  140.0 119.5 all-reduce.1
where the time goes:
time: 655 us; the launch traced here: 652 us
  waiting for transfers between devices  353 us (54%)
  blocking collectives  100 us (15%)
  local copies, waits for them, and re-layouts  83.4 us (13%)
  other arithmetic  55.6 us (8%)
  starting transfers between devices  25.1 us (4%)
  matrix products  19.9 us (3%)
  between operations  14.6 us (2%)
    psum x1, waiting for transfers between devices, on_device(): lax.psum(partial_out.astype(jnp.bfloat16), 'param').astype(jnp.float32)  120 us
    psum x1, blocking collectives, on_device(): gram = lax.psum(partial_gram, ('client', 'param'))  100 us
    all_gather x1, waiting for transfers between devices, on_device(): lax.all_gather(inputs, 'param', axis=2, tiled=True)  65.9 us
    unnamed x38, local copies, waits for them, and re-layouts  54.6 us
    all_gather x1, waiting for transfers between devices, on_device(): lax.all_gather(targets, 'param', axis=2, tiled=True)  53.5 us
    unnamed x3, other arithmetic  46.2 us
    all_to_all x1, waiting for transfers between devices, on_device(): lax.all_to_all(down_delta[None], 'client', split_axis=1, concat_axis=0, t...  38.9 us
    all_to_all x1, waiting for transfers between devices, on_device(): lax.all_to_all(gate_delta[None], 'client', split_axis=1, concat_axis=0, t...  36.6 us
  transfers between devices with their start and end apart: 6, of which 6 were waited for; matrix products, arithmetic and copies ran while one was open for 15% of the time, Pallas kernels for 0%

commit v1 on v0

v1 whole, which is shorter than its diff:
```python
import math

import jax
import jax.numpy as jnp
from jax import lax
from jax.experimental import pallas as pl
from jax.experimental.pallas import tpu as pltpu
from jax.sharding import Mesh, PartitionSpec as P

XY = ("x", "y")
ZC = ("z", "core")


def gelu_tanh(values):
    return jax.nn.gelu(values, approximate=True)


def exchange(blocks, axes):
    return lax.all_to_all(blocks, axes, split_axis=0, concat_axis=0, tiled=True)


def gather_rows(shard, axes, count):
    copies = jnp.broadcast_to(shard[None], (count,) + shard.shape)
    return exchange(copies, axes).reshape((count * shard.shape[0],) + shard.shape[1:])


def contract(left, right, left_dim, right_dim):
    return lax.dot_general(
        left, right, (((left_dim,), (right_dim,)), ((), ())), preferred_element_type=jnp.float32
    )


def krum_weights(gram, neighbours):
    client_count = gram.shape[0]
    row_index = lax.broadcasted_iota(jnp.int32, (client_count, client_count), 0)
    col_index = lax.broadcasted_iota(jnp.int32, (client_count, client_count), 1)
    diagonal = jnp.sum(jnp.where(row_index == col_index, gram, 0.0), axis=1)
    distance = diagonal[:, None] + diagonal[None, :] - 2.0 * gram
    distance = jnp.where(row_index == col_index, jnp.asarray(1e30, gram.dtype), distance)
    ordered = jnp.sort(distance, axis=1)
    scores = jnp.sum(
        jnp.where(col_index < neighbours[:, None], ordered, jnp.zeros_like(ordered)), axis=1
    )
    scaled = scores / jnp.mean(scores)
    exponent = jnp.exp(-4.0 * scaled)
    return exponent / jnp.sum(exponent)


def gram_kernel(block_ref, gram_ref, total_ref):
    clients, rows, columns = block_ref.shape
    step = 8
    total_ref[...] = jnp.zeros_like(total_ref)

    @pl.loop(0, rows // step)
    def _(index):
        start = pl.multiple_of(index * step, step)
        tile = block_ref[:, pl.ds(start, step), :].reshape(clients * step, columns)
        total_ref[...] += contract(tile, tile, 1, 1)

    size = clients * step
    row_index = lax.broadcasted_iota(jnp.int32, (size, size), 0)
    col_index = lax.broadcasted_iota(jnp.int32, (size, size), 1)
    kept = jnp.where(row_index % step == col_index % step, total_ref[...], 0.0)
    pick_client = lax.broadcasted_iota(jnp.int32, (clients, size), 0)
    pick_row = lax.broadcasted_iota(jnp.int32, (clients, size), 1)
    pick = (pick_row // step == pick_client).astype(jnp.float32)
    half = lax.dot_general(
        pick, kept, (((1,), (0,)), ((), ())),
        precision=lax.Precision.HIGHEST, preferred_element_type=jnp.float32,
    )
    gram_ref[...] = lax.dot_general(
        half, pick, (((1,), (1,)), ((), ())),
        precision=lax.Precision.HIGHEST, preferred_element_type=jnp.float32,
    )


def pair_products(exchanged):
    clients, rows, columns = exchanged.shape
    return pl.pallas_call(
        gram_kernel,
        out_shape=jax.ShapeDtypeStruct((clients, clients), jnp.float32),
        in_specs=[pl.BlockSpec(memory_space=pltpu.VMEM)],
        out_specs=pl.BlockSpec(memory_space=pltpu.VMEM),
        scratch_shapes=[pltpu.VMEM((clients * 8, clients * 8), jnp.float32)],
        cost_estimate=pl.CostEstimate(
            flops=2 * rows * clients * clients * 8 * columns,
            bytes_accessed=2 * clients * rows * columns,
            transcendentals=0,
        ),
        name="pair_products",
    )(exchanged)


def sum_over(values, axes, count):
    copies = jnp.broadcast_to(values[None], (count,) + values.shape)
    return jnp.sum(exchange(copies, axes), axis=0)


def on_device(inputs, targets, norm_gain, gate_weight, up_weight, down_weight, neighbours):
    token_count = inputs.shape[1]
    param_count = lax.axis_size(XY)
    client_count = lax.axis_size(ZC)
    z_count = lax.axis_size("z")
    factor = 1.0 / math.sqrt(token_count)
    features = param_count * inputs.shape[2]
    hidden_units = gate_weight.shape[1]

    gathered = gather_rows(inputs[0].T, XY, param_count).astype(jnp.float32)
    inverse_rms = lax.rsqrt(jnp.mean(gathered * gathered, axis=0, keepdims=True) + 1e-06)
    normed = (gathered * inverse_rms * norm_gain[:, None]).astype(jnp.bfloat16)
    gate_value = contract(gate_weight, normed, 0, 0)
    up_value = contract(up_weight, normed, 0, 0)
    activated, gelu_back = jax.vjp(gelu_tanh, gate_value)
    hidden = (activated * up_value).astype(jnp.bfloat16)
    partial_out = contract(down_weight, hidden, 0, 0).astype(jnp.bfloat16)
    parts = exchange(partial_out.reshape(param_count, features // param_count, token_count), XY)
    summed = jnp.sum(parts.astype(jnp.float32), axis=0)
    own_residual = ((summed - targets[0].T.astype(jnp.float32)) * factor).astype(jnp.bfloat16)
    residual = gather_rows(own_residual, XY, param_count)
    back_hidden = contract(down_weight, residual, 1, 0)
    back_gate = gelu_back(back_hidden * up_value)[0].astype(jnp.bfloat16)
    back_up = (back_hidden * activated).astype(jnp.bfloat16)

    width = -(-3 * hidden_units // 128) * 128
    zeros = jnp.zeros((hidden_units, token_count), jnp.bfloat16)
    rest = jnp.zeros((width - 3 * hidden_units, 2 * token_count), jnp.bfloat16)
    left = jnp.concatenate([normed, residual], axis=1)
    right = jnp.concatenate(
        [
            jnp.concatenate([back_gate, zeros], axis=1),
            jnp.concatenate([back_up, zeros], axis=1),
            jnp.concatenate([zeros, hidden], axis=1),
            rest,
        ],
        axis=0,
    )
    deltas = (-contract(left, right, 1, 1)).astype(jnp.bfloat16)
    owned = exchange(deltas.reshape(client_count, features // client_count, width), ZC)

    gram = pair_products(owned).reshape(8, -1)
    gram = lax.psum(gram, "core")
    gram = sum_over(gram, XY, param_count)
    gram = sum_over(gram, "z", z_count).reshape(client_count, client_count)
    weights = krum_weights(gram, neighbours)
    update = jnp.sum(weights[:, None, None] * owned.astype(jnp.float32), axis=0)
    return (
        update[:, :hidden_units],
        update[:, hidden_units : 2 * hidden_units],
        update[:, 2 * hidden_units : 3 * hidden_units],
        client_count * weights,
    )


def solution(mesh):
    torus = Mesh(mesh.devices.reshape(16, 2, 4, 4), ("z", "core", "x", "y"))
    in_specs = (
        P(ZC, None, XY),
        P(ZC, None, XY),
        P(),
        P(None, XY),
        P(None, XY),
        P(XY, None),
        P(),
    )
    out_specs = (P(ZC, XY), P(ZC, XY), P(ZC, XY), P())
    return jax.shard_map(
        on_device, mesh=torus, in_specs=in_specs, out_specs=out_specs, check_vma=False
    )
```

time: 655 us -> 355 us (0.54)
  waiting for transfers between devices: 353 us -> 20.5 us
  blocking collectives: 100 us -> 293 us
  local copies, waits for them, and re-layouts: 83.4 us -> 9.98 us
  other arithmetic: 55.6 us -> 7.73 us
  starting transfers between devices: 25.1 us -> 3.71 us
  between operations: 14.6 us -> 1.37 us
  matrix products: 19.9 us -> 11.2 us
    all_to_all x0 -> x5, blocking collectives: none -> 291 us  [exchange(): return lax.all_to_all(blocks, axes, split_axis=0, concat_axis=0, tiled=True)]
    psum x1 -> x0, waiting for transfers between devices: 120 us -> none  [on_device(): lax.psum(partial_out.astype(jnp.bfloat16), 'param').astype(jnp.float32)]
    all_gather x2 -> x0, waiting for transfers between devices: 119 us -> none  [the longest x1 65.9 us: on_device(): lax.all_gather(inputs, 'param', axis=2, tiled=True)]
    psum x1, blocking collectives: 100 us -> 2.62 us  [on_device(): gram = lax.psum(gram, 'core')]
    all_to_all x3 -> x1, waiting for transfers between devices: 112 us -> 20.5 us  [exchange(): return lax.all_to_all(blocks, axes, split_axis=0, concat_axis=0, tiled=True)]
    unnamed x38 -> x18, local copies, waits for them, and re-layouts: 54.6 us -> 2.86 us
    unnamed x3 -> x0, other arithmetic: 46.2 us -> none
    broadcast_in_dim x3 -> x5, local copies, waits for them, and re-layouts: 25.4 us -> 2.53 us  [the longest x2 2.51 us: gather_rows(): copies = jnp.broadcast_to(shard[None], (count,) + shard.shape)]
  transfers between devices with their start and end apart: 6 -> 1, of which waited for: 6 -> 1; matrix products, arithmetic and copies ran while one was open for 15% -> 0% of each run, Pallas kernels for 0% -> 0%
where the time goes in v1:
time: 355 us; the launch traced here: 354 us
  blocking collectives  293 us (83%)
  waiting for transfers between devices  20.5 us (6%)
  matrix products  11.2 us (3%)
  local copies, waits for them, and re-layouts  9.98 us (3%)
  other arithmetic  7.73 us (2%)
  Pallas kernels  6.27 us (2%)
  starting transfers between devices  3.71 us (1%)
    all_to_all x5, blocking collectives, exchange(): return lax.all_to_all(blocks, axes, split_axis=0, concat_axis=0, tiled=True)  291 us
    all_to_all x1, waiting for transfers between devices, exchange(): return lax.all_to_all(blocks, axes, split_axis=0, concat_axis=0, tiled=True)  20.5 us
    dot_general x5, matrix products, contract(): lax.dot_general(left, right, (((left_dim,), (right_dim,)), ((), ())), pre...  11.2 us
  transfers between devices with their start and end apart: 1, of which 1 were waited for; matrix products, arithmetic and copies ran while one was open for 0% of the time, Pallas kernels for 0%

profile of v1, /device:TPU:1, one launch (start us, length us, event | category | flops | bytes accessed | tf_op | source)
XLA Modules:
  0.0 354.1 jit_solution(7804485307363102841)
XLA Ops:
  0.6 0.0 copy-start
  0.6 1.2 broadcast_in_dim.17
  1.8 29.9 %all_to_all.30 = bf16[16,144,384]{2,1,0:T(8,128)(2,1)S(1)} all-to-all(bf16[16,144,384]{2,1,0:T(8,128)(2,1)S(1)} %broadcast_in_dim.17), channel_id=1, replica_groups=mesh['z'=16,'core'=2,'x'=4,'y'=4] {'x','y'}, dimensions={0} | all-to-all | bytes 3538944 | tf_op jit(solution)/shard_map/all_to_all | solution.py:19
  31.7 0.0 copy-start.4
  31.7 0.5 multiply_reduce_fusion.1
  32.2 0.2 copy-done.4
  32.4 0.0 copy-start.6
  32.4 0.5 fusion.5
  32.9 0.8 copy-done.6
  33.8 0.0 copy-start.1
  33.8 0.0 copy-start.7
  33.8 0.9 convolution_bitcast_fusion.2
  34.6 0.4 copy-done.1
  35.0 0.7 copy-done.7
  35.7 0.0 copy-start.8
  35.7 1.6 multiply_convert_fusion.1
  37.4 0.0 copy-done.8
  37.4 0.0 copy-done
  37.4 2.3 fusion
  39.7 2.8 copy.15
  42.4 24.7 %all_to_all.31 = bf16[16,144,384]{2,1,0:T(8,128)(2,1)S(1)} all-to-all(bf16[16,144,384]{2,1,0:T(8,128)(2,1)S(1)} %bitcast.39), channel_id=1, replica_groups=mesh['z'=16,'core'=2,'x'=4,'y'=4] {'x','y'}, dimensions={0} | all-to-all | bytes 3538944 | tf_op jit(solution)/shard_map/all_to_all | solution.py:19
  67.1 0.0 copy-start.3
  67.1 0.3 convert_reduce_fusion
  67.4 0.6 copy-done.3
  68.1 1.4 broadcast_in_dim.18
  69.4 3.7 %all-to-all-start.2 = ((bf16[16,144,384]{2,1,0:T(8,128)(2,1)}), bf16[16,144,384]{2,1,0:T(8,128)(2,1)S(1)}, u32[]{:S(2)}, u32[]{:S(2)}) async-start(bf16[16,144,384]{2,1,0:T(8,128)(2,1)} %broadcast_in_dim.18), calls=%async_computation.2 | async-start | bytes 3538944 | tf_op jit(solution)/shard_map/all_to_all | solution.py:19
  73.1 0.1 pad.6.clone
  73.2 20.5 %all-to-all-done.2 = bf16[16,144,384]{2,1,0:T(8,128)(2,1)S(1)} async-done(((bf16[16,144,384]{2,1,0:T(8,128)(2,1)}), bf16[16,144,384]{2,1,0:T(8,128)(2,1)S(1)}, u32[]{:S(2)}, u32[]{:S(2)}) %all-to-all-start.2) | async-done | bytes 1769504 | tf_op jit(solution)/shard_map/all_to_all | solution.py:19
  93.7 0.0 copy-start.2
  93.7 2.4 fusion.31
  96.1 0.0 copy-done.2
  96.1 4.0 %negate_convert_fusion = bf16[2304,896]{1,0:T(8,128)(2,1)S(1)} fusion(bf16[2304,384]{1,0:T(8,128)(2,1)S(1)} %bitcast.42, bf16[2304,384]{1,0:T(8,128)(2,1)S(1)} %copy-done.2, bf16[288,384]{1,0:T(8,128)(2,1)S(1)} %get-tuple-element.18, bf16[288,384]{1,0:T(8,128)(2,1)S(1)} %get-tuple-element.14, bf16[288,384]{1,0:T(8,128)(2,1)S(1)} %get-tuple-element.13, ...), kind=kOutput, calls=%fused_computation.1 | convolution fusion | flops 3194486784 | bytes 8333056 | tf_op jit(solution)/shard_map/dot_general | solution.py:28
  100.1 211.4 %all_to_all.32.block_ref = bf16[32,72,896]{2,1,0:T(8,128)(2,1)} all-to-all(bf16[32,72,896]{2,1,0:T(8,128)(2,1)S(1)} %bitcast.40), channel_id=1, replica_groups=mesh['z'=16,'core'=2,'x'=4,'y'=4] {'z','core'}, dimensions={0} | all-to-all | bytes 8257536 | tf_op jit(solution)/shard_map/all_to_all | solution.py:19
  311.5 6.3 %pair_products.1 = f32[32,32]{1,0:T(8,128)} custom-call(bf16[32,72,896]{2,1,0:T(8,128)(2,1)} %all_to_all.32.block_ref), custom_call_target="tpu_custom_call" | custom-call | flops 1056964608 | bytes 4128768 | tf_op jit(solution)/shard_map/pair_products/pallas_call | solution.py:79
  317.8 0.8 reshape.53
  318.6 2.6 psum.7
  321.2 10.5 %all_to_all.33 = f32[16,8,128]{2,1,0:T(8,128)S(1)} all-to-all(f32[16,8,128]{2,1,0:T(8,128)S(1)} %broadcast_in_dim.20), channel_id=1, replica_groups=mesh['z'=16,'core'=2,'x'=4,'y'=4] {'x','y'}, dimensions={0} | all-to-all | bytes 131072 | tf_op jit(solution)/shard_map/all_to_all | solution.py:19
  331.7 14.2 %all_to_all.34 = f32[16,8,128]{2,1,0:T(8,128)S(1)} all-to-all(f32[16,8,128]{2,1,0:T(8,128)S(1)} %broadcast_in_dim.21), channel_id=1, replica_groups=mesh['z'=16,'core'=2,'x'=4,'y'=4] {'z'}, dimensions={0} | all-to-all | bytes 131072 | tf_op jit(solution)/shard_map/all_to_all | solution.py:19
  346.0 0.1 reshape.54
  346.1 0.1 copy.16
  346.2 0.1 subtract_select_fusion
  346.3 0.9 sort.15
  347.2 0.0 copy-done.5
  347.2 0.6 fusion.36
  348.4 0.6 fusion.43
  349.0 1.2 broadcast_multiply_fusion
  350.2 3.1 multiply_reduce_fusion
  353.3 0.8 fusion.44
  (10 shorter events, 0.1 us)
Async XLA Ops:
  0.6 36.7 %copy-start = (bf16[288,2304]{1,0:T(8,128)(2,1)S(1)}, bf16[288,2304]{1,0:T(8,128)(2,1)}, u32[]{:S(2)}) copy-start(bf16[288,2304]{1,0:T(8,128)(2,1)} %param.12) | copy-start | bytes 3981316
  31.7 0.7 copy-start.4
  32.4 1.3 copy-start.6
  33.8 1.2 copy-start.1
  33.8 2.0 copy-start.7
  35.7 1.6 copy-start.8
  67.1 0.9 copy-start.3
  69.4 24.3 %all-to-all-start.2 = ((bf16[16,144,384]{2,1,0:T(8,128)(2,1)}), bf16[16,144,384]{2,1,0:T(8,128)(2,1)S(1)}, u32[]{:S(2)}, u32[]{:S(2)}) async-start(bf16[16,144,384]{2,1,0:T(8,128)(2,1)} %broadcast_in_dim.18), calls=%async_computation.2 | async-start | bytes 3538944 | tf_op jit(solution)/shard_map/all_to_all | solution.py:19
  93.7 2.4 copy-start.2
  311.5 35.7 %copy-start.5 = (s32[32]{0:T(128)S(1)}, s32[32]{0:T(128)}, u32[]{:S(2)}) copy-start(s32[32]{0:T(128)} %param.13) | copy-start | bytes 388

commit v2 on v1

--- a/solution.py
+++ b/solution.py
@@ -6,6 +6,7 @@
 from jax.experimental import pallas as pl
 from jax.experimental.pallas import tpu as pltpu
 from jax.sharding import Mesh, PartitionSpec as P
+
 
 XY = ("x", "y")
 ZC = ("z", "core")
@@ -96,58 +97,89 @@
     return jnp.sum(exchange(copies, axes), axis=0)
 
 
+def rms_normed(raw, norm_gain):
+    widened = raw.astype(jnp.float32)
+    inverse_rms = lax.rsqrt(jnp.mean(widened * widened, axis=0, keepdims=True) + 1e-06)
+    return (widened * inverse_rms * norm_gain[:, None]).astype(jnp.bfloat16)
+
+
+def swap_blocks(shard, z_count, core_count):
+    pairs = [
+        ((z * core_count + core) * z_count + p, (p * core_count + core) * z_count + z)
+        for z in range(z_count)
+        for core in range(core_count)
+        for p in range(z_count)
+    ]
+    return lax.ppermute(shard, ZC + XY, pairs)
+
+
 def on_device(inputs, targets, norm_gain, gate_weight, up_weight, down_weight, neighbours):
     token_count = inputs.shape[1]
     param_count = lax.axis_size(XY)
-    client_count = lax.axis_size(ZC)
     z_count = lax.axis_size("z")
+    core_count = lax.axis_size("core")
+    client_count = z_count * core_count
     factor = 1.0 / math.sqrt(token_count)
     features = param_count * inputs.shape[2]
+    slice_rows = features // client_count
     hidden_units = gate_weight.shape[1]
 
-    gathered = gather_rows(inputs[0].T, XY, param_count).astype(jnp.float32)
-    inverse_rms = lax.rsqrt(jnp.mean(gathered * gathered, axis=0, keepdims=True) + 1e-06)
-    normed = (gathered * inverse_rms * norm_gain[:, None]).astype(jnp.bfloat16)
+    own_inputs = inputs[0].T
+    met_inputs = swap_blocks(own_inputs, z_count, core_count)
+    met_inputs = lax.all_gather(met_inputs, "z", axis=0, tiled=True)
+    gathered = gather_rows(own_inputs, XY, param_count)
+    normed = rms_normed(gathered, norm_gain)
     gate_value = contract(gate_weight, normed, 0, 0)
     up_value = contract(up_weight, normed, 0, 0)
     activated, gelu_back = jax.vjp(gelu_tanh, gate_value)
     hidden = (activated * up_value).astype(jnp.bfloat16)
     partial_out = contract(down_weight, hidden, 0, 0).astype(jnp.bfloat16)
-    parts = exchange(partial_out.reshape(param_count, features // param_count, token_count), XY)
+    parts = exchange(
+        partial_out.reshape(param_count, features // param_count, token_count), XY
+    )
     summed = jnp.sum(parts.astype(jnp.float32), axis=0)
     own_residual = ((summed - targets[0].T.astype(jnp.float32)) * factor).astype(jnp.bfloat16)
+    met_residual = swap_blocks(own_residual, z_count, core_count)
+    met_residual = lax.all_gather(met_residual, "z", axis=0, tiled=True)
     residual = gather_rows(own_residual, XY, param_count)
     back_hidden = contract(down_weight, residual, 1, 0)
     back_gate = gelu_back(back_hidden * up_value)[0].astype(jnp.bfloat16)
     back_up = (back_hidden * activated).astype(jnp.bfloat16)
 
-    width = -(-3 * hidden_units // 128) * 128
-    zeros = jnp.zeros((hidden_units, token_count), jnp.bfloat16)
-    rest = jnp.zeros((width - 3 * hidden_units, 2 * token_count), jnp.bfloat16)
-    left = jnp.concatenate([normed, residual], axis=1)
-    right = jnp.concatenate(
-        [
-            jnp.concatenate([back_gate, zeros], axis=1),
-            jnp.concatenate([back_up, zeros], axis=1),
-            jnp.concatenate([zeros, hidden], axis=1),
-            rest,
-        ],
-        axis=0,
-    )
-    deltas = (-contract(left, right, 1, 1)).astype(jnp.bfloat16)
-    owned = exchange(deltas.reshape(client_count, features // client_count, width), ZC)
+    height = -(-3 * hidden_units // (8 * z_count)) * 8
+    rest = jnp.zeros((height * z_count - 3 * hidden_units, token_count), jnp.bfloat16)
+    rows = jnp.concatenate([back_gate, back_up, hidden, rest], axis=0)
+    rows, met_inputs = lax.optimization_barrier((rows, met_inputs))
+    rows = exchange(rows.reshape(z_count, height, token_count), "z")
+    rows = exchange(rows, XY)
+    place = lax.axis_index("z") * height + lax.broadcasted_iota(jnp.int32, (1, height, 1), 1)
+    of_down = place >= 2 * hidden_units
+    left = jnp.concatenate(
+        [jnp.where(of_down, 0, rows), jnp.where(of_down, rows, 0)], axis=2
+    ).reshape(param_count * height, 2 * token_count)
+    right = jnp.concatenate([rms_normed(met_inputs, norm_gain), met_residual], axis=1)
+    right = right.reshape(z_count, core_count, slice_rows, 2 * token_count)
+    half = z_count * slice_rows
+    deltas = [
+        (-contract(left, right[:, core].reshape(half, 2 * token_count), 1, 1))
+        .astype(jnp.bfloat16)
+        .reshape(param_count, height, half)
+        for core in range(core_count)
+    ]
+    owned = exchange(jnp.concatenate(deltas, axis=0), ("core",) + XY)
 
     gram = pair_products(owned).reshape(8, -1)
-    gram = lax.psum(gram, "core")
-    gram = sum_over(gram, XY, param_count)
+    gram = sum_over(gram, ("core",) + XY, core_count * param_count)
     gram = sum_over(gram, "z", z_count).reshape(client_count, client_count)
-    weights = krum_weights(gram, neighbours)
+    weights = krum_weights(gram, neighbours.reshape(z_count, core_count).T.reshape(-1))
     update = jnp.sum(weights[:, None, None] * owned.astype(jnp.float32), axis=0)
+    update = update.astype(jnp.bfloat16).reshape(height, z_count, slice_rows).swapaxes(0, 1)
+    update = exchange(update, "z").reshape(z_count * height, slice_rows).T.astype(jnp.float32)
     return (
         update[:, :hidden_units],
         update[:, hidden_units : 2 * hidden_units],
         update[:, 2 * hidden_units : 3 * hidden_units],
-        client_count * weights,
+        client_count * weights.reshape(core_count, z_count).T.reshape(-1),
     )
 
 

time: 355 us -> 395 us (1.11); the launches traced: 354 us -> 390 us
  blocking collectives: 293 us -> 106 us
  waiting for transfers between devices: 20.5 us -> 187 us
  starting transfers between devices: 3.71 us -> 36.5 us
  between operations: 1.37 us -> 14.9 us
  other arithmetic: 7.73 us -> 14.4 us
  local copies, waits for them, and re-layouts: 9.98 us -> 15.3 us
    all_to_all x5 -> x3, blocking collectives: 291 us -> 106 us  [exchange(): return lax.all_to_all(blocks, axes, split_axis=0, concat_axis=0, tiled=True)]
    all_to_all x1 -> x6, waiting for transfers between devices: 20.5 us -> 112 us  [exchange(): return lax.all_to_all(blocks, axes, split_axis=0, concat_axis=0, tiled=True)]
    all_gather x0 -> x2, waiting for transfers between devices: none -> 74.9 us  [the longest x1 40.6 us: on_device(): met_residual = lax.all_gather(met_residual, 'z', axis=0, tiled=True)]
    all_to_all x1 -> x6, starting transfers between devices: 3.71 us -> 34.1 us  [exchange(): return lax.all_to_all(blocks, axes, split_axis=0, concat_axis=0, tiled=True)]
    dot_general x5 -> x6, matrix products: 11.2 us -> 9.78 us  [contract(): lax.dot_general(left, right, (((left_dim,), (right_dim,)), ((), ())), pre...]
  transfers between devices with their start and end apart: 1 -> 10, of which waited for: 1 -> 7; matrix products, arithmetic and copies ran while one was open for 0% -> 3% of each run, Pallas kernels for 0% -> 0%
where the time goes in v2:
time: 395 us; the launch traced here: 390 us
  waiting for transfers between devices  187 us (47%)
  blocking collectives  106 us (27%)
  starting transfers between devices  36.5 us (9%)
  local copies, waits for them, and re-layouts  15.3 us (4%)
  between operations  14.9 us (4%)
  other arithmetic  14.4 us (4%)
  matrix products  9.78 us (2%)
  Pallas kernels  5.85 us (1%)
    all_to_all x6, waiting for transfers between devices, exchange(): return lax.all_to_all(blocks, axes, split_axis=0, concat_axis=0, tiled=True)  112 us
    all_to_all x3, blocking collectives, exchange(): return lax.all_to_all(blocks, axes, split_axis=0, concat_axis=0, tiled=True)  106 us
    all_gather x1, waiting for transfers between devices, on_device(): met_residual = lax.all_gather(met_residual, 'z', axis=0, tiled=True)  40.6 us
    all_gather x1, waiting for transfers between devices, on_device(): met_inputs = lax.all_gather(met_inputs, 'z', axis=0, tiled=True)  34.3 us
    all_to_all x6, starting transfers between devices, exchange(): return lax.all_to_all(blocks, axes, split_axis=0, concat_axis=0, tiled=True)  34.1 us
    dot_general x6, matrix products, contract(): lax.dot_general(left, right, (((left_dim,), (right_dim,)), ((), ())), pre...  9.78 us
  transfers between devices with their start and end apart: 10, of which 7 were waited for; matrix products, arithmetic and copies ran while one was open for 3% of the time, Pallas kernels for 0%

profile of v2, /device:TPU:1, one launch (start us, length us, event | category | flops | bytes accessed | tf_op | source)
XLA Modules:
  0.0 389.5 jit_solution(4903751285351583076)
XLA Ops:
  7.2 1.2 broadcast_in_dim.43
  8.3 29.9 %all_to_all.45 = bf16[16,144,384]{2,1,0:T(8,128)(2,1)S(1)} all-to-all(bf16[16,144,384]{2,1,0:T(8,128)(2,1)S(1)} %broadcast_in_dim.43), channel_id=1, replica_groups=mesh['z'=16,'core'=2,'x'=4,'y'=4] {'x','y'}, dimensions={0} | all-to-all | bytes 3538944 | tf_op jit(solution)/shard_map/all_to_all | solution.py:20
  39.4 0.8 copy-done.8
  40.3 0.8 convolution_bitcast_fusion.2
  41.6 1.6 multiply_convert_fusion.1
  43.3 1.1 fusion
  44.4 2.2 copy.31
  46.6 3.7 all-to-all-start.1
  50.4 1.6 collective-permute-start
  52.0 0.6 copy-done.5
  52.6 33.3 %all-to-all-done.1 = bf16[16,144,384]{2,1,0:T(8,128)(2,1)S(1)} async-done(((bf16[16,144,384]{2,1,0:T(8,128)(2,1)}), bf16[16,144,384]{2,1,0:T(8,128)(2,1)S(1)}, u32[]{:S(2)}, u32[]{:S(2)}) %all-to-all-start.1) | async-done | bytes 1769504 | tf_op jit(solution)/shard_map/all_to_all | solution.py:20
  86.2 1.4 broadcast_in_dim.68
  87.6 7.1 %all-to-all-start.2 = ((bf16[16,144,384]{2,1,0:T(8,128)(2,1)}), bf16[16,144,384]{2,1,0:T(8,128)(2,1)S(1)}, u32[]{:S(2)}, u32[]{:S(2)}) async-start(bf16[16,144,384]{2,1,0:T(8,128)(2,1)} %broadcast_in_dim.68), calls=%async_computation.2 | async-start | bytes 3538944 | tf_op jit(solution)/shard_map/all_to_all | solution.py:20
  94.7 0.7 collective-permute-start.1
  95.4 0.6 copy-done.4
  96.2 33.3 %all-to-all-done.2 = bf16[16,144,384]{2,1,0:T(8,128)(2,1)S(1)} async-done(((bf16[16,144,384]{2,1,0:T(8,128)(2,1)}), bf16[16,144,384]{2,1,0:T(8,128)(2,1)S(1)}, u32[]{:S(2)}, u32[]{:S(2)}) %all-to-all-start.2) | async-done | bytes 1769504 | tf_op jit(solution)/shard_map/all_to_all | solution.py:20
  129.5 2.2 fusion.12
  131.7 1.0 maximum_maximum_fusion
  132.8 34.3 %all-gather.3.cloned.1.call-done = bf16[2304,384]{1,0:T(8,128)(2,1)} async-done(((bf16[144,384]{1,0:T(8,128)(2,1)}), bf16[2304,384]{1,0:T(8,128)(2,1)}) %all-gather.3.cloned.1.call-update) | async-done | bytes 1769488 | tf_op jit(solution)/shard_map/all_gather | solution.py:129
  167.1 6.5 %all-to-all-start.3 = ((bf16[16,56,384]{2,1,0:T(8,128)(2,1)}), bf16[16,56,384]{2,1,0:T(8,128)(2,1)}, u32[]{:S(2)}, u32[]{:S(2)}) async-start(bf16[16,56,384]{2,1,0:T(8,128)(2,1)} %bitcast.13), calls=%async_computation.3 | async-start | bytes 1376256 | tf_op jit(solution)/shard_map/all_to_all | solution.py:20
  173.6 2.1 fusion.1
  175.7 0.5 fusion.3
  176.2 22.3 %all-to-all-done.3 = bf16[16,56,384]{2,1,0:T(8,128)(2,1)} async-done(((bf16[16,56,384]{2,1,0:T(8,128)(2,1)}), bf16[16,56,384]{2,1,0:T(8,128)(2,1)}, u32[]{:S(2)}, u32[]{:S(2)}) %all-to-all-start.3) | async-done | bytes 688160 | tf_op jit(solution)/shard_map/all_to_all | solution.py:20
  198.5 6.2 %all-to-all-start.4 = ((bf16[16,56,384]{2,1,0:T(8,128)(2,1)}), bf16[16,56,384]{2,1,0:T(8,128)(2,1)}, u32[]{:S(2)}, u32[]{:S(2)}) async-start(bf16[16,56,384]{2,1,0:T(8,128)(2,1)} %all-to-all-done.3), calls=%async_computation.4 | async-start | bytes 1376256 | tf_op jit(solution)/shard_map/all_to_all | solution.py:20
  204.7 40.6 %all-gather.5.cloned.1.call-done = bf16[2304,384]{1,0:T(8,128)(2,1)} async-done(((bf16[144,384]{1,0:T(8,128)(2,1)}), bf16[2304,384]{1,0:T(8,128)(2,1)}) %all-gather.5.cloned.1.call-update) | async-done | bytes 1769488 | tf_op jit(solution)/shard_map/all_gather | solution.py:143
  245.2 1.8 pad_maximum_fusion.1
  247.0 1.4 fusion.20
  248.5 1.3 broadcast_select_fusion.1
  249.9 1.3 copy-done.2
  251.2 2.0 negate_convert_fusion.1
  253.2 2.0 negate_convert_fusion
  255.6 64.0 %all_to_all.46.block_ref = bf16[32,56,1152]{2,1,0:T(8,128)(2,1)} all-to-all(bf16[32,56,1152]{2,1,0:T(8,128)(2,1)S(1)} %pad_maximum_fusion), channel_id=1, replica_groups=mesh['z'=16,'core'=2,'x'=4,'y'=4] {'core','x','y'}, dimensions={0} | all-to-all | bytes 8257536 | tf_op jit(solution)/shard_map/all_to_all | solution.py:20
  319.6 5.8 %pair_products.1 = f32[32,32]{1,0:T(8,128)} custom-call(bf16[32,56,1152]{2,1,0:T(8,128)(2,1)} %all_to_all.46.block_ref), custom_call_target="tpu_custom_call" | custom-call | flops 1056964608 | bytes 4128768 | tf_op jit(solution)/shard_map/pair_products/pallas_call | solution.py:80
  325.4 0.8 broadcast_in_dim.70
  326.2 12.0 %all_to_all.47 = f32[32,8,128]{2,1,0:T(8,128)S(1)} all-to-all(f32[32,8,128]{2,1,0:T(8,128)S(1)} %broadcast_in_dim.71), channel_id=1, replica_groups=mesh['z'=16,'core'=2,'x'=4,'y'=4] {'core','x','y'}, dimensions={0} | all-to-all | bytes 262144 | tf_op jit(solution)/shard_map/all_to_all | solution.py:20
  338.2 0.6 broadcast_in_dim.72
  338.9 6.9 %all-to-all-start.7 = ((f32[16,8,128]{2,1,0:T(8,128)}), f32[16,8,128]{2,1,0:T(8,128)S(1)}, u32[]{:S(2)}, u32[]{:S(2)}) async-start(f32[16,8,128]{2,1,0:T(8,128)} %broadcast_in_dim.72), calls=%async_computation.7 | async-start | bytes 131072 | tf_op jit(solution)/shard_map/all_to_all | solution.py:20
  346.1 11.3 %all-to-all-done.7 = f32[16,8,128]{2,1,0:T(8,128)S(1)} async-done(((f32[16,8,128]{2,1,0:T(8,128)}), f32[16,8,128]{2,1,0:T(8,128)S(1)}, u32[]{:S(2)}, u32[]{:S(2)}) %all-to-all-start.7) | async-done | bytes 65568 | tf_op jit(solution)/shard_map/all_to_all | solution.py:20
  357.7 0.9 sort.15
  358.6 0.6 fusion.17
  359.8 0.6 fusion.19
  360.4 0.6 broadcast_multiply_fusion
  361.1 3.0 multiply_reduce_fusion
  364.6 0.7 copy.34
  365.3 3.8 all-to-all-start.8
  369.3 0.6 mul.176
  369.9 11.7 %all-to-all-done.8 = bf16[16,56,72]{2,1,0:T(8,128)(2,1)S(1)} async-done(((bf16[16,56,72]{2,1,0:T(8,128)(2,1)}), bf16[16,56,72]{2,1,0:T(8,128)(2,1)S(1)}, u32[]{:S(2)}, u32[]{:S(2)}) %all-to-all-start.8) | async-done | bytes 129056 | tf_op jit(solution)/shard_map/all_to_all | solution.py:20
  381.8 0.8 fusion.21
  (52 shorter events, 4.1 us)
Async XLA Ops:
  7.2 36.1 %copy-start = (bf16[288,2304]{1,0:T(8,128)(2,1)S(1)}, bf16[288,2304]{1,0:T(8,128)(2,1)}, u32[]{:S(2)}) copy-start(bf16[288,2304]{1,0:T(8,128)(2,1)} %param.12) | copy-start | bytes 3981316
  38.3 0.7 copy-start.6
  39.0 1.3 copy-start.8
  40.3 1.3 copy-start.9
  41.6 1.7 copy-start.10
  46.6 39.3 %all-to-all-start.1 = ((bf16[16,144,384]{2,1,0:T(8,128)(2,1)}), bf16[16,144,384]{2,1,0:T(8,128)(2,1)S(1)}, u32[]{:S(2)}, u32[]{:S(2)}) async-start(bf16[16,144,384]{2,1,0:T(8,128)(2,1)} %bitcast.7), calls=%async_computation.1 | async-start | bytes 3538944 | tf_op jit(solution)/shard_map/all_to_all | solution.py:20
  50.3 35.8 %copy-start.3 = (bf16[1,384,144]{1,2,0:T(8,128)(2,1)S(1)}, bf16[1,384,144]{1,2,0:T(8,128)(2,1)}, u32[]{:S(2)}) copy-start(bf16[1,384,144]{1,2,0:T(8,128)(2,1)} %param.8) | copy-start | bytes 331780
  50.3 116.8 %all-gather.3.cloned.1.call-start = ((), (), s32[]{:S(2)}) async-start(), calls=%async_computation.9 | async-start | bytes 1880064 | tf_op jit(solution)/shard_map/all_gather | solution.py:129
  50.4 1.6 collective-permute-start
  52.0 0.6 copy-start.5
  87.6 41.9 %all-to-all-start.2 = ((bf16[16,144,384]{2,1,0:T(8,128)(2,1)}), bf16[16,144,384]{2,1,0:T(8,128)(2,1)S(1)}, u32[]{:S(2)}, u32[]{:S(2)}) async-start(bf16[16,144,384]{2,1,0:T(8,128)(2,1)} %broadcast_in_dim.68), calls=%async_computation.2 | async-start | bytes 3538944 | tf_op jit(solution)/shard_map/all_to_all | solution.py:20
  94.7 150.6 %all-gather.5.cloned.1.call-start = ((), (), s32[]{:S(2)}) async-start(), calls=%async_computation.10 | async-start | bytes 1880064 | tf_op jit(solution)/shard_map/all_gather | solution.py:143
  94.7 0.7 collective-permute-start.1
  95.4 0.6 copy-start.4
  167.1 31.4 %all-to-all-start.3 = ((bf16[16,56,384]{2,1,0:T(8,128)(2,1)}), bf16[16,56,384]{2,1,0:T(8,128)(2,1)}, u32[]{:S(2)}, u32[]{:S(2)}) async-start(bf16[16,56,384]{2,1,0:T(8,128)(2,1)} %bitcast.13), calls=%async_computation.3 | async-start | bytes 1376256 | tf_op jit(solution)/shard_map/all_to_all | solution.py:20
  173.6 2.1 copy-start.1
  198.5 50.0 %all-to-all-start.4 = ((bf16[16,56,384]{2,1,0:T(8,128)(2,1)}), bf16[16,56,384]{2,1,0:T(8,128)(2,1)}, u32[]{:S(2)}, u32[]{:S(2)}) async-start(bf16[16,56,384]{2,1,0:T(8,128)(2,1)} %all-to-all-done.3), calls=%async_computation.4 | async-start | bytes 1376256 | tf_op jit(solution)/shard_map/all_to_all | solution.py:20
  249.8 1.5 copy-start.2
  319.6 26.2 %copy-start.7 = (s32[32]{0:T(128)S(1)}, s32[32]{0:T(128)}, u32[]{:S(2)}) copy-start(s32[32]{0:T(128)} %param.13) | copy-start | bytes 388
  338.9 18.5 %all-to-all-start.7 = ((f32[16,8,128]{2,1,0:T(8,128)}), f32[16,8,128]{2,1,0:T(8,128)S(1)}, u32[]{:S(2)}, u32[]{:S(2)}) async-start(f32[16,8,128]{2,1,0:T(8,128)} %broadcast_in_dim.72), calls=%async_computation.7 | async-start | bytes 131072 | tf_op jit(solution)/shard_map/all_to_all | solution.py:20
  365.3 16.3 %all-to-all-start.8 = ((bf16[16,56,72]{2,1,0:T(8,128)(2,1)}), bf16[16,56,72]{2,1,0:T(8,128)(2,1)S(1)}, u32[]{:S(2)}, u32[]{:S(2)}) async-start(bf16[16,56,72]{2,1,0:T(8,128)(2,1)} %copy.34), calls=%async_computation.8 | async-start | bytes 458752 | tf_op jit(solution)/shard_map/all_to_all | solution.py:20
Sparse Core Ops, SparseCore 0:
  53.8 113.2 all-gather.2
  169.8 75.4 all-gather.4

commit v3 on v1

v3 whole, which is shorter than its diff:
```python
import math

import jax
import jax.numpy as jnp
from jax import lax
from jax.experimental import pallas as pl
from jax.experimental.pallas import tpu as pltpu
from jax.sharding import Mesh, PartitionSpec as P

XY = ("x", "y")
ZC = ("z", "core")


def exchange(blocks, axes):
    return lax.all_to_all(blocks, axes, split_axis=0, concat_axis=0, tiled=True)


def gather_rows(shard, axes, count):
    copies = jnp.broadcast_to(shard[None], (count,) + shard.shape)
    return exchange(copies, axes).reshape((count * shard.shape[0],) + shard.shape[1:])


def contract(left, right, left_dim, right_dim):
    return lax.dot_general(
        left, right, (((left_dim,), (right_dim,)), ((), ())), preferred_element_type=jnp.float32
    )


def gelu_parts(values):
    scale = math.sqrt(2.0 / math.pi)
    square = values * values
    bend = jnp.tanh(scale * (values + 0.044715 * (square * values)))
    slope = 0.5 * (1.0 + bend) + (0.5 * values) * (1.0 - bend * bend) * (
        scale * (1.0 + (3.0 * 0.044715) * square)
    )
    return 0.5 * values * (1.0 + bend), slope


def forward_kernel(
    normed_ref, gate_ref, up_ref, down_ref,
    out_ref, hidden_ref, activated_ref, slope_ref,
    gate_total, up_total,
):
    step = pl.program_id(0)
    half = pl.num_programs(0) // 2

    @pl.when(step == 0)
    def _():
        gate_total[...] = jnp.zeros_like(gate_total)
        up_total[...] = jnp.zeros_like(up_total)

    @pl.when(step < half)
    def _():
        rows = normed_ref[...]
        gate_total[...] += contract(gate_ref[...], rows, 1, 0)
        up_total[...] += contract(up_ref[...], rows, 1, 0)

    @pl.when(step == half - 1)
    def _():
        activated, slope = gelu_parts(gate_total[...])
        up_value = up_total[...]
        activated_ref[...] = activated
        slope_ref[...] = slope * up_value
        hidden_ref[...] = (activated * up_value).astype(hidden_ref.dtype)

    @pl.when(step >= half)
    def _():
        out_ref[...] = contract(down_ref[...], hidden_ref[...], 0, 0).astype(out_ref.dtype)


def forward(normed, gate_weight, up_weight, down_weight):
    features, tokens = normed.shape
    units = down_weight.shape[0]
    chunks = 3
    rows = features // chunks
    early = lambda step: jnp.minimum(step, chunks - 1)
    late = lambda step: jnp.maximum(step - chunks, 0)
    whole = pl.BlockSpec((units, tokens), lambda step: (0, 0))
    return pl.pallas_call(
        forward_kernel,
        grid=(2 * chunks,),
        in_specs=[
            pl.BlockSpec((rows, tokens), lambda step: (early(step), 0)),
            pl.BlockSpec((units, rows), lambda step: (0, early(step))),
            pl.BlockSpec((units, rows), lambda step: (0, early(step))),
            pl.BlockSpec((units, rows), lambda step: (0, late(step))),
        ],
        out_specs=[pl.BlockSpec((rows, tokens), lambda step: (late(step), 0)), whole, whole, whole],
        out_shape=[
            jax.ShapeDtypeStruct((features, tokens), jnp.bfloat16),
            jax.ShapeDtypeStruct((units, tokens), jnp.bfloat16),
            jax.ShapeDtypeStruct((units, tokens), jnp.float32),
            jax.ShapeDtypeStruct((units, tokens), jnp.float32),
        ],
        scratch_shapes=[pltpu.VMEM((units, tokens), jnp.float32)] * 2,
        cost_estimate=pl.CostEstimate(
            flops=6 * features * tokens * units,
            bytes_accessed=2 * features * (3 * units + 2 * tokens) + 10 * units * tokens,
            transcendentals=units * tokens,
        ),
        name="forward",
    )(normed, gate_weight.T, up_weight.T, down_weight)


def exact_dot(left, right, left_dim, right_dim):
    return lax.dot_general(
        left, right, (((left_dim,), (right_dim,)), ((), ())),
        precision=lax.Precision.HIGHEST, preferred_element_type=jnp.float32,
    )


def lane_place(index, size, lanes):
    row = lax.broadcasted_iota(jnp.int32, (size, lanes), 0)
    column = lax.broadcasted_iota(jnp.int32, (size, lanes), 1)
    return (column == row + index * size).astype(jnp.float32)


def gram_kernel(core_ref, own_ref, other_ref, copies_ref, total_ref):
    step = pl.program_id(0)
    half, _, rows, columns = own_ref.shape
    clients, tall = 2 * half, 8
    size = clients * tall

    @pl.when(step == 0)
    def _():
        total_ref[...] = jnp.zeros_like(total_ref)

    for start in range(0, rows, tall):
        tile = jnp.concatenate(
            [own_ref[:, 0, start : start + tall, :], other_ref[:, start : start + tall, :]], axis=0
        ).reshape(size, columns)
        total_ref[...] += contract(tile, tile, 1, 1)

    @pl.when(step == pl.num_programs(0) - 1)
    def _():
        row_index = lax.broadcasted_iota(jnp.int32, (size, size), 0)
        col_index = lax.broadcasted_iota(jnp.int32, (size, size), 1)
        kept = jnp.where(row_index % tall == col_index % tall, total_ref[...], 0.0)
        pick_client = lax.broadcasted_iota(jnp.int32, (clients, size), 0)
        pick_row = lax.broadcasted_iota(jnp.int32, (clients, size), 1) // tall
        pick_row = (pick_row + half * core_ref[0]) % clients
        pick = (pick_row == pick_client).astype(jnp.float32)
        gram = exact_dot(exact_dot(pick, kept, 1, 0), pick, 1, 1)
        packed = jnp.zeros(copies_ref.shape[1:], jnp.float32)
        for index in range(clients // tall):
            packed += exact_dot(
                gram[index * tall : (index + 1) * tall],
                lane_place(index, clients, copies_ref.shape[2]), 1, 0,
            )
        copies_ref[...] = jnp.broadcast_to(packed[None], copies_ref.shape)


def pair_products(core, own, other, copies):
    half, _, rows, columns = own.shape
    chunks = 3
    return pl.pallas_call(
        gram_kernel,
        grid_spec=pltpu.PrefetchScalarGridSpec(
            num_scalar_prefetch=1,
            grid=(chunks,),
            in_specs=[
                pl.BlockSpec(
                    (half, 1, rows // chunks, columns), lambda step, core_ref: (0, core_ref[0], step, 0)
                ),
                pl.BlockSpec((half, rows // chunks, columns), lambda step, core_ref: (0, step, 0)),
            ],
            out_specs=pl.BlockSpec((copies, 8, 128), lambda step, core_ref: (0, 0, 0)),
            scratch_shapes=[pltpu.VMEM((half * 16, half * 16), jnp.float32)],
        ),
        out_shape=jax.ShapeDtypeStruct((copies, 8, 128), jnp.float32),
        cost_estimate=pl.CostEstimate(
            flops=2 * rows * 4 * half * half * 8 * columns,
            bytes_accessed=4 * half * rows * columns,
            transcendentals=0,
        ),
        name="pair_products",
    )(core, own, other)


def finish_kernel(
    core_ref, parts_ref, neighbours_ref, own_ref, other_ref,
    gate_ref, up_ref, down_ref, relative_ref, weight_ref,
):
    step = pl.program_id(0)
    half, _, rows, _ = own_ref.shape
    clients, tall = 2 * half, 8
    units = gate_ref.shape[1]

    @pl.when(step == 0)
    def _():
        packed = jnp.sum(parts_ref[...], axis=0)
        gram = jnp.concatenate(
            [
                exact_dot(packed, lane_place(index, clients, packed.shape[1]), 1, 1)
                for index in range(clients // tall)
            ],
            axis=0,
        )
        row_index = lax.broadcasted_iota(jnp.int32, (clients, clients), 0)
        col_index = lax.broadcasted_iota(jnp.int32, (clients, clients), 1)
        same = row_index == col_index
        diagonal = jnp.where(same, gram, 0.0)
        distance = (
            jnp.sum(diagonal, axis=1, keepdims=True)
            + jnp.sum(diagonal, axis=0, keepdims=True)
            - 2.0 * gram
        )
        distance = jnp.where(same, 1e30, distance)
        rank = jnp.zeros((clients, clients), jnp.float32)
        for index in range(clients):
            rival = distance[:, index : index + 1]
            ahead = (rival < distance) | ((rival == distance) & (index < col_index))
            rank += jnp.where(ahead, 1.0, 0.0)
        count = jnp.sum(
            jnp.where(same, neighbours_ref[...].astype(jnp.float32), 0.0), axis=1, keepdims=True
        )
        scores = jnp.sum(jnp.where(rank < count, distance, 0.0), axis=1, keepdims=True)
        mean = jnp.sum(scores, axis=0, keepdims=True) / clients
        exponent = jnp.exp(-4.0 * (scores / mean))
        weights = exponent / jnp.sum(exponent, axis=0, keepdims=True)
        relative_ref[...] = clients * jnp.sum(
            jnp.where(same, weights, 0.0), axis=0, keepdims=True
        )
        weight_ref[...] = jnp.broadcast_to(weights, weight_ref.shape)

    core = core_ref[0]
    own_weight = weight_ref[pl.ds(pl.multiple_of(core * half, half), half), :]
    other_weight = weight_ref[pl.ds(pl.multiple_of((1 - core) * half, half), half), :]
    for start in range(0, rows, tall):
        total = jnp.zeros((tall, own_ref.shape[3]), jnp.float32)
        for index in range(half):
            total += own_weight[index : index + 1, :1] * own_ref[
                index, 0, start : start + tall, :
            ].astype(jnp.float32)
            total += other_weight[index : index + 1, :1] * other_ref[
                index, start : start + tall, :
            ].astype(jnp.float32)
        gate_ref[start : start + tall, :] = total[:, :units]
        up_ref[start : start + tall, :] = total[:, units : 2 * units]
        down_ref[start : start + tall, :] = total[:, 2 * units : 3 * units]


def finish(core, parts, neighbours, own, other, units):
    half, _, rows, columns = own.shape
    chunks = 3
    tall = rows // chunks
    block = pl.BlockSpec((tall, units), lambda step, core_ref: (step, 0))
    return pl.pallas_call(
        finish_kernel,
        grid_spec=pltpu.PrefetchScalarGridSpec(
            num_scalar_prefetch=1,
            grid=(chunks,),
            in_specs=[
                pl.BlockSpec(parts.shape, lambda step, core_ref: (0, 0, 0)),
                pl.BlockSpec(neighbours.shape, lambda step, core_ref: (0, 0)),
                pl.BlockSpec(
                    (half, 1, tall, columns), lambda step, core_ref: (0, core_ref[0], step, 0)
                ),
                pl.BlockSpec((half, tall, columns), lambda step, core_ref: (0, step, 0)),
            ],
            out_specs=[
                block, block, block, pl.BlockSpec((1, 2 * half), lambda step, core_ref: (0, 0))
            ],
            scratch_shapes=[pltpu.VMEM((2 * half, 128), jnp.float32)],
        ),
        out_shape=[jax.ShapeDtypeStruct((rows, units), jnp.float32)] * 3
        + [jax.ShapeDtypeStruct((1, 2 * half), jnp.float32)],
        cost_estimate=pl.CostEstimate(
            flops=4 * half * rows * columns,
            bytes_accessed=4 * half * rows * columns + 12 * rows * units,
            transcendentals=2 * half,
        ),
        name="finish",
    )(core, parts, neighbours, own, other)


def on_device(inputs, targets, norm_gain, gate_weight, up_weight, down_weight, neighbours):
    token_count = inputs.shape[1]
    param_count = lax.axis_size(XY)
    z_count = lax.axis_size("z")
    core_count = lax.axis_size("core")
    client_count = z_count * core_count
    factor = 1.0 / math.sqrt(token_count)
    features = param_count * inputs.shape[2]
    hidden_units = gate_weight.shape[1]
    core = lax.axis_index("core")

    gathered = gather_rows(inputs[0].T, XY, param_count).astype(jnp.float32)
    inverse_rms = lax.rsqrt(jnp.mean(gathered * gathered, axis=0, keepdims=True) + 1e-06)
    normed = (gathered * inverse_rms * norm_gain[:, None]).astype(jnp.bfloat16)
    partial_out, hidden, activated, slope = forward(normed, gate_weight, up_weight, down_weight)
    parts = exchange(partial_out.reshape(param_count, features // param_count, token_count), XY)
    summed = jnp.sum(parts.astype(jnp.float32), axis=0)
    own_residual = ((summed - targets[0].T.astype(jnp.float32)) * factor).astype(jnp.bfloat16)
    residual = gather_rows(own_residual, XY, param_count)
    back_hidden = contract(down_weight, residual, 1, 0)
    back_gate = (back_hidden * slope).astype(jnp.bfloat16)
    back_up = (back_hidden * activated).astype(jnp.bfloat16)

    width = -(-3 * hidden_units // 128) * 128
    zeros = jnp.zeros((hidden_units, token_count), jnp.bfloat16)
    rest = jnp.zeros((width - 3 * hidden_units, 2 * token_count), jnp.bfloat16)
    left = jnp.concatenate([normed, residual], axis=1)
    right = jnp.concatenate(
        [
            jnp.concatenate([back_gate, zeros], axis=1),
            jnp.concatenate([back_up, zeros], axis=1),
            jnp.concatenate([zeros, hidden], axis=1),
            rest,
        ],
        axis=0,
    )
    deltas = (-contract(left, right, 1, 1)).astype(jnp.bfloat16)
    met = exchange(deltas.reshape(z_count, features // z_count, width), "z")
    met = met.reshape(z_count, core_count, features // client_count, width)
    other = lax.dynamic_index_in_dim(met, 1 - core, axis=1, keepdims=False)
    other = lax.ppermute(other, "core", [(0, 1), (1, 0)])

    core = core.reshape(1)
    gram = pair_products(core, met, other, core_count * param_count)
    gram = jnp.sum(exchange(gram, ("core",) + XY), axis=0)
    gram = exchange(jnp.broadcast_to(gram[None], (z_count,) + gram.shape), "z")
    order = neighbours.reshape(z_count, core_count).T.reshape(1, -1)
    update_gate, update_up, update_down, relative = finish(
        core, gram, order, met, other, hidden_units
    )
    return (
        update_gate,
        update_up,
        update_down,
        relative.reshape(core_count, z_count).T.reshape(-1),
    )


def solution(mesh):
    torus = Mesh(mesh.devices.reshape(16, 2, 4, 4), ("z", "core", "x", "y"))
    in_specs = (
        P(ZC, None, XY),
        P(ZC, None, XY),
        P(),
        P(None, XY),
        P(None, XY),
        P(XY, None),
        P(),
    )
    out_specs = (P(ZC, XY), P(ZC, XY), P(ZC, XY), P())
    return jax.shard_map(
        on_device, mesh=torus, in_specs=in_specs, out_specs=out_specs, check_vma=False
    )
```

time: 355 us -> 359 us (1.011)
  blocking collectives: 293 us -> 68.2 us
  waiting for transfers between devices: 20.5 us -> 214 us
  starting transfers between devices: 3.71 us -> 36.2 us
  Pallas kernels: 6.27 us -> 18 us
  other arithmetic: 7.73 us -> 3.78 us
    all_to_all x5 -> x3, blocking collectives: 291 us -> 68.2 us  [exchange(): return lax.all_to_all(blocks, axes, split_axis=0, concat_axis=0, tiled=True)]
    all_to_all x1 -> x3, waiting for transfers between devices: 20.5 us -> 210 us  [exchange(): return lax.all_to_all(blocks, axes, split_axis=0, concat_axis=0, tiled=True)]
    all_to_all x1 -> x3, starting transfers between devices: 3.71 us -> 32.9 us  [exchange(): return lax.all_to_all(blocks, axes, split_axis=0, concat_axis=0, tiled=True)]
    pallas_call x1 -> x3, Pallas kernels: 6.27 us -> 18 us  [the longest x1 8.13 us: forward(): pl.pallas_call(forward_kernel, grid=(2 * chunks,), in_specs=[pl.BlockSpec...]
    reduce_sum x6 -> x1, other arithmetic: 4.36 us -> 0.04 us  [on_device(): gram = jnp.sum(exchange(gram, ('core',) + XY), axis=0)]
    ppermute x0 -> x1, waiting for transfers between devices: none -> 3.72 us  [on_device(): other = lax.ppermute(other, 'core', [(0, 1), (1, 0)])]
    dot_general x5 -> x2, matrix products: 11.2 us -> 7.93 us  [contract(): lax.dot_general(left, right, (((left_dim,), (right_dim,)), ((), ())), pre...]
  transfers between devices with their start and end apart: 1 -> 4, of which waited for: 1 -> 4; matrix products, arithmetic and copies ran while one was open for 0% -> 0% of each run, Pallas kernels for 0% -> 0%
where the time goes in v3:
time: 359 us; the launch traced here: 358 us
  waiting for transfers between devices  214 us (60%)
  blocking collectives  68.2 us (19%)
  starting transfers between devices  36.2 us (10%)
  Pallas kernels  18 us (5%)
  local copies, waits for them, and re-layouts  8.94 us (2%)
  matrix products  7.93 us (2%)
  other arithmetic  3.78 us (1%)
    all_to_all x3, waiting for transfers between devices, exchange(): return lax.all_to_all(blocks, axes, split_axis=0, concat_axis=0, tiled=True)  210 us
    all_to_all x3, blocking collectives, exchange(): return lax.all_to_all(blocks, axes, split_axis=0, concat_axis=0, tiled=True)  68.2 us
    all_to_all x3, starting transfers between devices, exchange(): return lax.all_to_all(blocks, axes, split_axis=0, concat_axis=0, tiled=True)  32.9 us
    pallas_call x1, Pallas kernels, forward(): pl.pallas_call(forward_kernel, grid=(2 * chunks,), in_specs=[pl.BlockSpec...  8.13 us
    dot_general x2, matrix products, contract(): lax.dot_general(left, right, (((left_dim,), (right_dim,)), ((), ())), pre...  7.93 us
  transfers between devices with their start and end apart: 4, of which 4 were waited for; matrix products, arithmetic and copies ran while one was open for 0% of the time, Pallas kernels for 0%

profile of v3, /device:TPU:1, one launch (start us, length us, event | category | flops | bytes accessed | tf_op | source)
XLA Modules:
  0.0 357.8 jit_solution(299056421388577623)
XLA Ops:
  0.6 1.1 broadcast_in_dim.8
  1.7 0.0 copy-start.6
  1.7 29.9 %all_to_all.30 = bf16[16,144,384]{2,1,0:T(8,128)(2,1)S(1)} all-to-all(bf16[16,144,384]{2,1,0:T(8,128)(2,1)S(1)} %broadcast_in_dim.8), channel_id=1, replica_groups=mesh['z'=16,'core'=2,'x'=4,'y'=4] {'x','y'}, dimensions={0} | all-to-all | bytes 3538944 | tf_op jit(solution)/shard_map/all_to_all | solution.py:15
  31.6 0.5 multiply_reduce_fusion
  32.1 0.0 copy-done.6
  32.1 1.7 fusion.4.normed_ref
  33.8 8.1 %forward.1 = (bf16[2304,384]{1,0:T(8,128)(2,1)}, bf16[288,384]{1,0:T(8,128)(2,1)}, f32[288,384]{1,0:T(8,128)}, f32[288,384]{1,0:T(8,128)}) custom-call(bf16[2304,384]{1,0:T(8,128)(2,1)} %fusion.4.normed_ref, bf16[288,2304]{1,0:T(8,128)(2,1)} %bitcast.39, bf16[288,2304]{1,0:T(8,128)(2,1)} %bitcast.40, bf16[288,2304]{1,0:T(8,128)(2,1)} %down_ref.1), custom_call_target="tpu_custom_call" | custom-call | flops 1528823808 | bytes 8626176 | tf_op jit(solution)/shard_map/forward/pallas_call | solution.py:79
  41.9 0.0 copy-start.5
  41.9 25.1 %all_to_all.31 = bf16[16,144,384]{2,1,0:T(8,128)(2,1)S(1)} all-to-all(bf16[16,144,384]{2,1,0:T(8,128)(2,1)} %bitcast.38), channel_id=1, replica_groups=mesh['z'=16,'core'=2,'x'=4,'y'=4] {'x','y'}, dimensions={0} | all-to-all | bytes 3538944 | tf_op jit(solution)/shard_map/all_to_all | solution.py:15
  67.0 0.3 convert_reduce_fusion
  67.3 0.0 copy-done.5
  67.3 1.4 broadcast_in_dim.9
  68.7 0.0 copy-start.1
  68.7 0.0 copy-start.3
  68.7 3.9 %all-to-all-start.2 = ((bf16[16,144,384]{2,1,0:T(8,128)(2,1)}), bf16[16,144,384]{2,1,0:T(8,128)(2,1)S(1)}, u32[]{:S(2)}, u32[]{:S(2)}) async-start(bf16[16,144,384]{2,1,0:T(8,128)(2,1)} %broadcast_in_dim.9), calls=%async_computation.2 | async-start | bytes 3538944 | tf_op jit(solution)/shard_map/all_to_all | solution.py:15
  72.6 0.1 pad.6.clone
  72.7 20.4 %all-to-all-done.2 = bf16[16,144,384]{2,1,0:T(8,128)(2,1)S(1)} async-done(((bf16[16,144,384]{2,1,0:T(8,128)(2,1)}), bf16[16,144,384]{2,1,0:T(8,128)(2,1)S(1)}, u32[]{:S(2)}, u32[]{:S(2)}) %all-to-all-start.2) | async-done | bytes 1769504 | tf_op jit(solution)/shard_map/all_to_all | solution.py:15
  93.1 0.0 copy-done.1
  93.1 0.0 copy-done.3
  93.1 0.0 copy-start.2
  93.1 0.0 copy-start.8
  93.1 2.0 multiply_convert_fusion.1
  95.1 0.0 copy-done.2
  95.1 0.0 copy-done.8
  95.1 5.9 %negate_convert_fusion = bf16[2304,896]{1,0:T(8,128)(2,1)} fusion(bf16[2304,384]{1,0:T(8,128)(2,1)S(1)} %bitcast.36, bf16[2304,384]{1,0:T(8,128)(2,1)S(1)} %copy-done.2, bf16[288,384]{1,0:T(8,128)(2,1)S(1)} %copy-done.8, bf16[288,384]{1,0:T(8,128)(2,1)S(1)} %get-tuple-element.21, bf16[288,384]{1,0:T(8,128)(2,1)S(1)} %get-tuple-element.20, ...), kind=kOutput, calls=%fused_computation | convolution fusion | flops 3194486784 | bytes 8333056 | tf_op jit(solution)/shard_map/dot_general | solution.py:24
  101.0 18.8 %all-to-all-start.3 = ((bf16[16,144,896]{2,1,0:T(8,128)(2,1)}), bf16[16,144,896]{2,1,0:T(8,128)(2,1)}, u32[]{:S(2)}, u32[]{:S(2)}) async-start(bf16[16,144,896]{2,1,0:T(8,128)(2,1)} %bitcast.37), calls=%async_computation.3 | async-start | bytes 8257536 | tf_op jit(solution)/shard_map/all_to_all | solution.py:15
  119.9 179.1 %all-to-all-done.3 = bf16[16,144,896]{2,1,0:T(8,128)(2,1)} async-done(((bf16[16,144,896]{2,1,0:T(8,128)(2,1)}), bf16[16,144,896]{2,1,0:T(8,128)(2,1)}, u32[]{:S(2)}, u32[]{:S(2)}) %all-to-all-start.3) | async-done | bytes 4128800 | tf_op jit(solution)/shard_map/all_to_all | solution.py:15
  298.9 1.7 dynamic-slice_bitcast_fusion
  300.7 3.3 collective-permute-start
  304.0 3.7 %collective-permute-done.other_ref = bf16[16,72,896]{2,1,0:T(8,128)(2,1)S(1)} collective-permute-done((bf16[16,72,896]{2,1,0:T(8,128)(2,1)S(1)}, bf16[16,72,896]{2,1,0:T(8,128)(2,1)S(1)}, u32[]{:S(2)}, u32[]{:S(2)}) %collective-permute-start) | collective-permute-done | bytes 2064416 | tf_op jit(solution)/shard_map/ppermute | solution.py:317
  307.7 0.0 copy-start
  307.7 1.3 copy-done
  309.0 5.2 %pair_products.1 = f32[32,8,128]{2,1,0:T(8,128)} custom-call(s32[1]{0:T(128)} %bitcast.core_ref, bf16[16,2,72,896]{3,2,1,0:T(8,128)(2,1)} %bitcast.12.own_ref, bf16[16,72,896]{2,1,0:T(8,128)(2,1)} %copy-done), custom_call_target="tpu_custom_call" | custom-call | flops 1056964608 | bytes 4128768 | tf_op jit(solution)/shard_map/pair_products/pallas_call | solution.py:156
  314.3 13.2 %all_to_all.32 = f32[32,8,128]{2,1,0:T(8,128)S(1)} all-to-all(f32[32,8,128]{2,1,0:T(8,128)} %pair_products.1), channel_id=1, replica_groups=mesh['z'=16,'core'=2,'x'=4,'y'=4] {'core','x','y'}, dimensions={0} | all-to-all | bytes 262144 | tf_op jit(solution)/shard_map/all_to_all | solution.py:15
  327.6 0.6 broadcast_in_dim.11
  328.2 10.1 %all-to-all-start.5 = ((f32[16,8,128]{2,1,0:T(8,128)}), f32[16,8,128]{2,1,0:T(8,128)S(1)}, u32[]{:S(2)}, u32[]{:S(2)}) async-start(f32[16,8,128]{2,1,0:T(8,128)} %broadcast_in_dim.11), calls=%async_computation.5 | async-start | bytes 131072 | tf_op jit(solution)/shard_map/all_to_all | solution.py:15
  338.3 0.0 copy-done.7
  338.4 0.1 reshape.57
  338.4 0.1 copy.13
  338.5 0.7 reshape.58.neighbours_ref
  339.2 10.7 %all-to-all-done.5.parts_ref = f32[16,8,128]{2,1,0:T(8,128)S(1)} async-done(((f32[16,8,128]{2,1,0:T(8,128)}), f32[16,8,128]{2,1,0:T(8,128)S(1)}, u32[]{:S(2)}, u32[]{:S(2)}) %all-to-all-start.5) | async-done | bytes 65568 | tf_op jit(solution)/shard_map/all_to_all | solution.py:15
  349.9 0.6 copy-done.4
  350.5 4.7 %finish.1 = (f32[72,288]{1,0:T(8,128)}, f32[72,288]{1,0:T(8,128)}, f32[72,288]{1,0:T(8,128)}, f32[1,32]{1,0:T(1,128)}) custom-call(s32[1]{0:T(128)} %bitcast.core_ref, f32[16,8,128]{2,1,0:T(8,128)} %copy-done.4, s32[1,32]{1,0:T(1,128)} %reshape.58.neighbours_ref, bf16[16,2,72,896]{3,2,1,0:T(8,128)(2,1)} %bitcast.12.own_ref, bf16[16,72,896]{2,1,0:T(8,128)(2,1)} %copy-done), custom_call_target="tpu_custom_call" | custom-call | flops 4128768 | bytes 4377600 | tf_op jit(solution)/shard_map/finish/pallas_call | solution.py:248
  355.2 0.5 broadcast.53
  355.7 1.3 reduce.4
  357.0 0.1 reshape.59
  357.1 0.1 copy.14
  357.2 0.6 reshape.60
  (6 shorter events, 0.1 us)
Async XLA Ops:
  1.7 30.4 %copy-start.6 = (f32[2304]{0:T(1024)S(1)}, f32[2304]{0:T(1024)}, u32[]{:S(2)}) copy-start(f32[2304]{0:T(1024)} %param.9) | copy-start | bytes 27652
  41.9 25.3 %copy-start.5 = (bf16[1,384,144]{1,2,0:T(8,128)(2,1)S(1)}, bf16[1,384,144]{1,2,0:T(8,128)(2,1)}, u32[]{:S(2)}) copy-start(bf16[1,384,144]{1,2,0:T(8,128)(2,1)} %param.8) | copy-start | bytes 331780
  68.7 24.4 %copy-start.1 = (bf16[288,2304]{1,0:T(8,128)(2,1)S(1)}, bf16[288,2304]{1,0:T(8,128)(2,1)}, u32[]{:S(2)}) copy-start(bf16[288,2304]{1,0:T(8,128)(2,1)} %down_ref.1) | copy-start | bytes 3981316
  68.7 24.4 %copy-start.3 = (f32[288,384]{1,0:T(8,128)S(1)}, f32[288,384]{1,0:T(8,128)}, u32[]{:S(2)}) copy-start(f32[288,384]{1,0:T(8,128)} %get-tuple-element.14) | copy-start | bytes 1327108
  68.7 24.4 %all-to-all-start.2 = ((bf16[16,144,384]{2,1,0:T(8,128)(2,1)}), bf16[16,144,384]{2,1,0:T(8,128)(2,1)S(1)}, u32[]{:S(2)}, u32[]{:S(2)}) async-start(bf16[16,144,384]{2,1,0:T(8,128)(2,1)} %broadcast_in_dim.9), calls=%async_computation.2 | async-start | bytes 3538944 | tf_op jit(solution)/shard_map/all_to_all | solution.py:15
  93.1 2.0 copy-start.2
  93.1 2.0 copy-start.8
  101.0 197.9 %all-to-all-start.3 = ((bf16[16,144,896]{2,1,0:T(8,128)(2,1)}), bf16[16,144,896]{2,1,0:T(8,128)(2,1)}, u32[]{:S(2)}, u32[]{:S(2)}) async-start(bf16[16,144,896]{2,1,0:T(8,128)(2,1)} %bitcast.37), calls=%async_computation.3 | async-start | bytes 8257536 | tf_op jit(solution)/shard_map/all_to_all | solution.py:15
  300.7 7.0 %collective-permute-start = (bf16[16,72,896]{2,1,0:T(8,128)(2,1)S(1)}, bf16[16,72,896]{2,1,0:T(8,128)(2,1)S(1)}, u32[]{:S(2)}, u32[]{:S(2)}) collective-permute-start(bf16[16,72,896]{2,1,0:T(8,128)(2,1)S(1)} %dynamic-slice_bitcast_fusion), channel_id=1, source_target_pairs={{0,16},{16,0},{1,17},{17,1},{2,18},{18,2},{3,19},{19,3},{4,20},{20... | collective-permute-start | bytes 6193160 | tf_op jit(solution)/shard_map/ppermute | solution.py:317
  307.7 1.3 copy-start
  309.0 29.3 %copy-start.7 = (s32[32]{0:T(128)S(1)}, s32[32]{0:T(128)}, u32[]{:S(2)}) copy-start(s32[32]{0:T(128)} %param.13) | copy-start | bytes 388
  328.2 21.7 %all-to-all-start.5 = ((f32[16,8,128]{2,1,0:T(8,128)}), f32[16,8,128]{2,1,0:T(8,128)S(1)}, u32[]{:S(2)}, u32[]{:S(2)}) async-start(f32[16,8,128]{2,1,0:T(8,128)} %broadcast_in_dim.11), calls=%async_computation.5 | async-start | bytes 131072 | tf_op jit(solution)/shard_map/all_to_all | solution.py:15
  349.9 0.6 copy-start.4

commit v4 on v2

--- a/solution.py
+++ b/solution.py
@@ -125,14 +125,12 @@
     hidden_units = gate_weight.shape[1]
 
     own_inputs = inputs[0].T
-    met_inputs = swap_blocks(own_inputs, z_count, core_count)
-    met_inputs = lax.all_gather(met_inputs, "z", axis=0, tiled=True)
+    met_inputs = lax.all_gather(own_inputs, "z", axis=0, tiled=False)
     gathered = gather_rows(own_inputs, XY, param_count)
     normed = rms_normed(gathered, norm_gain)
     gate_value = contract(gate_weight, normed, 0, 0)
     up_value = contract(up_weight, normed, 0, 0)
-    activated, gelu_back = jax.vjp(gelu_tanh, gate_value)
-    hidden = (activated * up_value).astype(jnp.bfloat16)
+    hidden = (gelu_tanh(gate_value) * up_value).astype(jnp.bfloat16)
     partial_out = contract(down_weight, hidden, 0, 0).astype(jnp.bfloat16)
     parts = exchange(
         partial_out.reshape(param_count, features // param_count, token_count), XY
@@ -141,23 +139,54 @@
     own_residual = ((summed - targets[0].T.astype(jnp.float32)) * factor).astype(jnp.bfloat16)
     met_residual = swap_blocks(own_residual, z_count, core_count)
     met_residual = lax.all_gather(met_residual, "z", axis=0, tiled=True)
-    residual = gather_rows(own_residual, XY, param_count)
-    back_hidden = contract(down_weight, residual, 1, 0)
+
+    share = hidden_units // z_count
+    height = -(-3 * share // 8) * 8
+    first = lax.axis_index("z") * share
+    column = lax.axis_index("core") * (features // core_count)
+
+    def own_part(rows):
+        return lax.dynamic_slice(rows, (first, column), (share, features // core_count))
+
+    part = jnp.concatenate(
+        [
+            own_part(gate_weight.T),
+            own_part(up_weight.T),
+            own_part(down_weight),
+            jnp.zeros((height - 3 * share, features // core_count), jnp.bfloat16),
+        ],
+        axis=0,
+    )
+    part, own_residual = lax.optimization_barrier((part, own_residual))
+    part = gather_rows(part, XY, param_count)
+    part, met_inputs = lax.optimization_barrier((part, met_inputs))
+    weights_met = gather_rows(part[None], "core", core_count)
+    met_inputs = exchange(met_inputs, XY).reshape(features, token_count)
+    met_normed = rms_normed(met_inputs, norm_gain)
+
+    def times_weights(rows):
+        halves = rows.reshape(core_count, features // core_count, token_count)
+        total = sum(contract(weights_met[core], halves[core], 1, 0) for core in range(core_count))
+        return total.reshape(param_count, height, token_count)
+
+    values = times_weights(met_normed)
+    values, met_residual = lax.optimization_barrier((values, met_residual))
+    activated, gelu_back = jax.vjp(gelu_tanh, values[:, :share])
+    up_value = values[:, share : 2 * share]
+    hidden = (activated * up_value).astype(jnp.bfloat16)
+    back_hidden = times_weights(met_residual)[:, 2 * share : 3 * share]
     back_gate = gelu_back(back_hidden * up_value)[0].astype(jnp.bfloat16)
     back_up = (back_hidden * activated).astype(jnp.bfloat16)
-
-    height = -(-3 * hidden_units // (8 * z_count)) * 8
-    rest = jnp.zeros((height * z_count - 3 * hidden_units, token_count), jnp.bfloat16)
-    rows = jnp.concatenate([back_gate, back_up, hidden, rest], axis=0)
-    rows, met_inputs = lax.optimization_barrier((rows, met_inputs))
-    rows = exchange(rows.reshape(z_count, height, token_count), "z")
-    rows = exchange(rows, XY)
-    place = lax.axis_index("z") * height + lax.broadcasted_iota(jnp.int32, (1, height, 1), 1)
-    of_down = place >= 2 * hidden_units
+    rest = jnp.zeros((param_count, height - 3 * share, token_count), jnp.bfloat16)
+    none = jnp.zeros((param_count, share, token_count), jnp.bfloat16)
     left = jnp.concatenate(
-        [jnp.where(of_down, 0, rows), jnp.where(of_down, rows, 0)], axis=2
+        [
+            jnp.concatenate([back_gate, back_up, none, rest], axis=1),
+            jnp.concatenate([none, none, hidden, rest], axis=1),
+        ],
+        axis=2,
     ).reshape(param_count * height, 2 * token_count)
-    right = jnp.concatenate([rms_normed(met_inputs, norm_gain), met_residual], axis=1)
+    right = jnp.concatenate([met_normed, met_residual], axis=1)
     right = right.reshape(z_count, core_count, slice_rows, 2 * token_count)
     half = z_count * slice_rows
     deltas = [
@@ -174,11 +203,16 @@
     weights = krum_weights(gram, neighbours.reshape(z_count, core_count).T.reshape(-1))
     update = jnp.sum(weights[:, None, None] * owned.astype(jnp.float32), axis=0)
     update = update.astype(jnp.bfloat16).reshape(height, z_count, slice_rows).swapaxes(0, 1)
-    update = exchange(update, "z").reshape(z_count * height, slice_rows).T.astype(jnp.float32)
+    update = exchange(update, "z").astype(jnp.float32)
+
+    def placed(index):
+        rows = update[:, index * share : (index + 1) * share]
+        return rows.reshape(hidden_units, slice_rows).T
+
     return (
-        update[:, :hidden_units],
-        update[:, hidden_units : 2 * hidden_units],
-        update[:, 2 * hidden_units : 3 * hidden_units],
+        placed(0),
+        placed(1),
+        placed(2),
         client_count * weights.reshape(core_count, z_count).T.reshape(-1),
     )
 

time: 395 us -> 384 us (0.972)
  waiting for transfers between devices: 187 us -> 144 us
  starting transfers between devices: 36.5 us -> 48.5 us
  matrix products: 9.78 us -> 21 us
  local copies, waits for them, and re-layouts: 15.3 us -> 23 us
    all_to_all x6, waiting for transfers between devices: 112 us -> 66.3 us  [exchange(): return lax.all_to_all(blocks, axes, split_axis=0, concat_axis=0, tiled=True)]
    all_to_all x6, starting transfers between devices: 34.1 us -> 47.7 us  [exchange(): return lax.all_to_all(blocks, axes, split_axis=0, concat_axis=0, tiled=True)]
    dot_general x6 -> x8, matrix products: 9.78 us -> 21 us  [contract(): lax.dot_general(left, right, (((left_dim,), (right_dim,)), ((), ())), pre...]
    all_gather x1, waiting for transfers between devices: 34.3 us -> 44.2 us  [on_device(): met_inputs = lax.all_gather(own_inputs, 'z', axis=0, tiled=False)]
    all_gather x1, waiting for transfers between devices: 40.6 us -> 32.6 us  [on_device(): met_residual = lax.all_gather(met_residual, 'z', axis=0, tiled=True)]
  transfers between devices with their start and end apart: 10 -> 9, of which waited for: 7 -> 7; matrix products, arithmetic and copies ran while one was open for 3% -> 4% of each run, Pallas kernels for 0% -> 0%
where the time goes in v4:
time: 384 us; the launch traced here: 378 us
  waiting for transfers between devices  144 us (38%)
  blocking collectives  109 us (28%)
  starting transfers between devices  48.5 us (13%)
  local copies, waits for them, and re-layouts  23 us (6%)
  matrix products  21 us (5%)
  between operations  15 us (4%)
  other arithmetic  11.5 us (3%)
  Pallas kernels  5.85 us (2%)
    all_to_all x3, blocking collectives, exchange(): return lax.all_to_all(blocks, axes, split_axis=0, concat_axis=0, tiled=True)  109 us
    all_to_all x6, waiting for transfers between devices, exchange(): return lax.all_to_all(blocks, axes, split_axis=0, concat_axis=0, tiled=True)  66.3 us
    all_to_all x6, starting transfers between devices, exchange(): return lax.all_to_all(blocks, axes, split_axis=0, concat_axis=0, tiled=True)  47.7 us
    all_gather x1, waiting for transfers between devices, on_device(): met_inputs = lax.all_gather(own_inputs, 'z', axis=0, tiled=False)  44.2 us
    all_gather x1, waiting for transfers between devices, on_device(): met_residual = lax.all_gather(met_residual, 'z', axis=0, tiled=True)  32.6 us
    dot_general x8, matrix products, contract(): lax.dot_general(left, right, (((left_dim,), (right_dim,)), ((), ())), pre...  21 us
  transfers between devices with their start and end apart: 9, of which 7 were waited for; matrix products, arithmetic and copies ran while one was open for 4% of the time, Pallas kernels for 0%

profile of v4, /device:TPU:1, one launch (start us, length us, event | category | flops | bytes accessed | tf_op | source)
XLA Modules:
  0.0 377.6 jit_solution(9401618283965548654)
XLA Ops:
  7.2 1.1 broadcast_in_dim.29
  8.2 29.9 %all_to_all.45 = bf16[16,144,384]{2,1,0:T(8,128)(2,1)S(1)} all-to-all(bf16[16,144,384]{2,1,0:T(8,128)(2,1)S(1)} %broadcast_in_dim.29), channel_id=1, replica_groups=mesh['z'=16,'core'=2,'x'=4,'y'=4] {'x','y'}, dimensions={0} | all-to-all | bytes 3538944 | tf_op jit(solution)/shard_map/all_to_all | solution.py:20
  39.3 0.8 copy-done.7
  40.2 1.7 fusion.30
  41.9 3.8 %fusion = bf16[2304,384]{0,1:T(8,128)(2,1)S(1)} fusion(bf16[288,2304]{1,0:T(8,128)(2,1)} %param.12, f32[288,384]{1,0:T(8,128)} %fusion.30, bf16[2304,288]{0,1:T(8,128)(2,1)} %param.11, bf16[2304,384]{1,0:T(8,128)(2,1)S(1)} %fusion.4), kind=kOutput, calls=%fused_computation.5 | convolution fusion | flops 1020321792 | bytes 6635520 | tf_op jit(solution)/shard_map/dot_general | solution.py:29
  45.7 2.2 copy.43
  47.9 3.7 all-to-all-start.1
  51.7 0.7 all-gather.6.cloned.1.call-update
  52.4 1.0 dynamic_slice.11
  53.5 1.0 dynamic-slice_bitcast_fusion
  54.6 19.0 %all-to-all-done.1 = bf16[16,144,384]{2,1,0:T(8,128)(2,1)S(1)} async-done(((bf16[16,144,384]{2,1,0:T(8,128)(2,1)}), bf16[16,144,384]{2,1,0:T(8,128)(2,1)S(1)}, u32[]{:S(2)}, u32[]{:S(2)}) %all-to-all-start.1) | async-done | bytes 1769504 | tf_op jit(solution)/shard_map/all_to_all | solution.py:20
  73.9 1.5 broadcast_in_dim.30
  75.4 4.9 %all-to-all-start.2 = ((bf16[16,56,1152]{2,1,0:T(8,128)(2,1)}), bf16[16,56,1152]{2,1,0:T(8,128)(2,1)S(1)}, u32[]{:S(2)}, u32[]{:S(2)}) async-start(bf16[16,56,1152]{2,1,0:T(8,128)(2,1)} %broadcast_in_dim.30), calls=%async_computation.2 | async-start | bytes 4128768 | tf_op jit(solution)/shard_map/all_to_all | solution.py:20
  80.3 44.2 %all-gather.6.cloned.1.call-done = bf16[2304,384]{1,0:T(8,128)(2,1)} async-done(((bf16[144,384]{1,0:T(8,128)(2,1)}), bf16[2304,384]{1,0:T(8,128)(2,1)}) %all-gather.6.cloned.1.call-update) | async-done | bytes 1769488 | tf_op jit(solution)/shard_map/all_gather | solution.py:128
  124.5 1.3 copy-done
  125.8 6.3 %all-to-all-start.4 = ((bf16[16,144,384]{2,1,0:T(8,128)(2,1)}), bf16[16,144,384]{2,1,0:T(8,128)(2,1)S(1)}, u32[]{:S(2)}, u32[]{:S(2)}) async-start(bf16[16,144,384]{2,1,0:T(8,128)(2,1)} %bitcast.88), calls=%async_computation.4 | async-start | bytes 3538944 | tf_op jit(solution)/shard_map/all_to_all | solution.py:20
  132.2 0.7 collective-permute-start
  133.6 0.6 pad.8.clone
  134.2 0.6 pad.6.clone
  134.9 21.1 %all-to-all-done.4 = bf16[16,144,384]{2,1,0:T(8,128)(2,1)S(1)} async-done(((bf16[16,144,384]{2,1,0:T(8,128)(2,1)}), bf16[16,144,384]{2,1,0:T(8,128)(2,1)S(1)}, u32[]{:S(2)}, u32[]{:S(2)}) %all-to-all-start.4) | async-done | bytes 1769504 | tf_op jit(solution)/shard_map/all_to_all | solution.py:20
  156.0 3.8 %broadcast_in_dim.62 = bf16[2,1,896,1152]{3,2,1,0:T(8,128)(2,1)} broadcast(bf16[896,1152]{1,0:T(8,128)(2,1)} %bitcast.83), dimensions={2,3} | broadcast | bytes 6193152 | tf_op jit(solution)/shard_map/broadcast_in_dim | solution.py:24
  159.8 21.3 %all-to-all-start.3 = ((bf16[2,1,896,1152]{3,2,1,0:T(8,128)(2,1)}), bf16[2,1,896,1152]{3,2,1,0:T(8,128)(2,1)}, u32[]{:S(2)}, u32[]{:S(2)}) async-start(bf16[2,1,896,1152]{3,2,1,0:T(8,128)(2,1)} %broadcast_in_dim.62), calls=%async_computation.3 | async-start | bytes 8257536 | tf_op jit(solution)/shard_map/all_to_all | solution.py:20
  182.0 3.2 all-to-all-done.3
  185.2 2.9 fusion.6
  188.1 2.9 fusion.9
  191.0 32.6 %all-gather.4.cloned.1.call-done = bf16[2304,384]{1,0:T(8,128)(2,1)} async-done(((bf16[144,384]{1,0:T(8,128)(2,1)}), bf16[2304,384]{1,0:T(8,128)(2,1)}) %all-gather.4.cloned.1.call-update) | async-done | bytes 1769488 | tf_op jit(solution)/shard_map/all_gather | solution.py:141
  223.6 1.8 pad_maximum_fusion.1
  225.6 1.2 copy-done.1
  226.9 2.9 fusion.5
  229.7 2.9 fusion.10
  234.0 2.0 negate_convert_fusion
  236.0 2.0 negate_convert_fusion.1
  238.4 67.2 %all_to_all.46.block_ref = bf16[32,56,1152]{2,1,0:T(8,128)(2,1)} all-to-all(bf16[32,56,1152]{2,1,0:T(8,128)(2,1)S(1)} %pad_maximum_fusion), channel_id=1, replica_groups=mesh['z'=16,'core'=2,'x'=4,'y'=4] {'core','x','y'}, dimensions={0} | all-to-all | bytes 8257536 | tf_op jit(solution)/shard_map/all_to_all | solution.py:20
  305.6 5.8 %pair_products.1 = f32[32,32]{1,0:T(8,128)} custom-call(bf16[32,56,1152]{2,1,0:T(8,128)(2,1)} %all_to_all.46.block_ref), custom_call_target="tpu_custom_call" | custom-call | flops 1056964608 | bytes 4128768 | tf_op jit(solution)/shard_map/pair_products/pallas_call | solution.py:80
  311.4 0.8 broadcast_in_dim.65
  312.2 12.0 %all_to_all.47 = f32[32,8,128]{2,1,0:T(8,128)S(1)} all-to-all(f32[32,8,128]{2,1,0:T(8,128)S(1)} %broadcast_in_dim.66), channel_id=1, replica_groups=mesh['z'=16,'core'=2,'x'=4,'y'=4] {'core','x','y'}, dimensions={0} | all-to-all | bytes 262144 | tf_op jit(solution)/shard_map/all_to_all | solution.py:20
  324.2 0.6 broadcast_in_dim.67
  324.9 7.6 %all-to-all-start.7 = ((f32[16,8,128]{2,1,0:T(8,128)}), f32[16,8,128]{2,1,0:T(8,128)S(1)}, u32[]{:S(2)}, u32[]{:S(2)}) async-start(f32[16,8,128]{2,1,0:T(8,128)} %broadcast_in_dim.67), calls=%async_computation.7 | async-start | bytes 131072 | tf_op jit(solution)/shard_map/all_to_all | solution.py:20
  332.8 11.3 %all-to-all-done.7 = f32[16,8,128]{2,1,0:T(8,128)S(1)} async-done(((f32[16,8,128]{2,1,0:T(8,128)}), f32[16,8,128]{2,1,0:T(8,128)S(1)}, u32[]{:S(2)}, u32[]{:S(2)}) %all-to-all-start.7) | async-done | bytes 65568 | tf_op jit(solution)/shard_map/all_to_all | solution.py:20
  344.4 0.9 sort.15
  347.2 0.6 broadcast_multiply_fusion
  347.8 3.0 multiply_reduce_fusion
  351.3 0.7 copy.46
  352.0 3.8 %all-to-all-start.8 = ((bf16[16,56,72]{2,1,0:T(8,128)(2,1)}), bf16[16,56,72]{2,1,0:T(8,128)(2,1)S(1)}, u32[]{:S(2)}, u32[]{:S(2)}) async-start(bf16[16,56,72]{2,1,0:T(8,128)(2,1)} %copy.46), calls=%async_computation.8 | async-start | bytes 458752 | tf_op jit(solution)/shard_map/all_to_all | solution.py:20
  356.6 11.7 %all-to-all-done.8 = bf16[16,56,72]{2,1,0:T(8,128)(2,1)S(1)} async-done(((bf16[16,56,72]{2,1,0:T(8,128)(2,1)}), bf16[16,56,72]{2,1,0:T(8,128)(2,1)S(1)}, u32[]{:S(2)}, u32[]{:S(2)}) %all-to-all-start.8) | async-done | bytes 129056 | tf_op jit(solution)/shard_map/all_to_all | solution.py:20
  368.4 0.8 copy.48
  369.2 0.8 copy.49
  370.0 0.8 copy.50
  (59 shorter events, 8.4 us)
Async XLA Ops:
  38.1 0.7 copy-start.6
  38.9 1.3 copy-start.7
  47.9 25.7 %all-to-all-start.1 = ((bf16[16,144,384]{2,1,0:T(8,128)(2,1)}), bf16[16,144,384]{2,1,0:T(8,128)(2,1)S(1)}, u32[]{:S(2)}, u32[]{:S(2)}) async-start(bf16[16,144,384]{2,1,0:T(8,128)(2,1)} %bitcast.9), calls=%async_computation.1 | async-start | bytes 3538944 | tf_op jit(solution)/shard_map/all_to_all | solution.py:20
  51.6 22.2 %copy-start.4 = (bf16[1,384,144]{1,2,0:T(8,128)(2,1)S(1)}, bf16[1,384,144]{1,2,0:T(8,128)(2,1)}, u32[]{:S(2)}) copy-start(bf16[1,384,144]{1,2,0:T(8,128)(2,1)} %param.8) | copy-start | bytes 331780
  51.6 72.8 %all-gather.6.cloned.1.call-start = ((), (), s32[]{:S(2)}) async-start(), calls=%async_computation.10 | async-start | bytes 1880064 | tf_op jit(solution)/shard_map/all_gather | solution.py:128
  75.4 49.1 %all-to-all-start.2 = ((bf16[16,56,1152]{2,1,0:T(8,128)(2,1)}), bf16[16,56,1152]{2,1,0:T(8,128)(2,1)S(1)}, u32[]{:S(2)}, u32[]{:S(2)}) async-start(bf16[16,56,1152]{2,1,0:T(8,128)(2,1)} %broadcast_in_dim.30), calls=%async_computation.2 | async-start | bytes 4128768 | tf_op jit(solution)/shard_map/all_to_all | solution.py:20
  124.5 1.3 copy-start
  125.8 30.1 %all-to-all-start.4 = ((bf16[16,144,384]{2,1,0:T(8,128)(2,1)}), bf16[16,144,384]{2,1,0:T(8,128)(2,1)S(1)}, u32[]{:S(2)}, u32[]{:S(2)}) async-start(bf16[16,144,384]{2,1,0:T(8,128)(2,1)} %bitcast.88), calls=%async_computation.4 | async-start | bytes 3538944 | tf_op jit(solution)/shard_map/all_to_all | solution.py:20
  132.2 91.5 %all-gather.4.cloned.1.call-start = ((), (), s32[]{:S(2)}) async-start(), calls=%async_computation.9 | async-start | bytes 1880064 | tf_op jit(solution)/shard_map/all_gather | solution.py:141
  132.2 0.7 collective-permute-start
  132.9 0.6 copy-start.5
  159.8 25.4 %all-to-all-start.3 = ((bf16[2,1,896,1152]{3,2,1,0:T(8,128)(2,1)}), bf16[2,1,896,1152]{3,2,1,0:T(8,128)(2,1)}, u32[]{:S(2)}, u32[]{:S(2)}) async-start(bf16[2,1,896,1152]{3,2,1,0:T(8,128)(2,1)} %broadcast_in_dim.62), calls=%async_computation.3 | async-start | bytes 8257536 | tf_op jit(solution)/shard_map/all_to_all | solution.py:20
  225.4 1.5 copy-start.1
  232.6 0.9 copy-start.2
  232.6 0.9 copy-start.3
  305.6 27.0 %copy-start.8 = (s32[32]{0:T(128)S(1)}, s32[32]{0:T(128)}, u32[]{:S(2)}) copy-start(s32[32]{0:T(128)} %param.13) | copy-start | bytes 388
  324.9 19.2 %all-to-all-start.7 = ((f32[16,8,128]{2,1,0:T(8,128)}), f32[16,8,128]{2,1,0:T(8,128)S(1)}, u32[]{:S(2)}, u32[]{:S(2)}) async-start(f32[16,8,128]{2,1,0:T(8,128)} %broadcast_in_dim.67), calls=%async_computation.7 | async-start | bytes 131072 | tf_op jit(solution)/shard_map/all_to_all | solution.py:20
  352.0 16.3 %all-to-all-start.8 = ((bf16[16,56,72]{2,1,0:T(8,128)(2,1)}), bf16[16,56,72]{2,1,0:T(8,128)(2,1)S(1)}, u32[]{:S(2)}, u32[]{:S(2)}) async-start(bf16[16,56,72]{2,1,0:T(8,128)(2,1)} %copy.46), calls=%async_computation.8 | async-start | bytes 458752 | tf_op jit(solution)/shard_map/all_to_all | solution.py:20
Sparse Core Ops, SparseCore 0:
  54.5 69.9 all-gather.5
  135.6 87.9 all-gather.3

commit v5 on v4

v5 whole, which is shorter than its diff:
```python
import math

import jax
import jax.numpy as jnp
from jax import lax
from jax.experimental import pallas as pl
from jax.experimental.pallas import tpu as pltpu
from jax.sharding import Mesh, PartitionSpec as P


XY = ("x", "y")
ZC = ("z", "core")


def gelu_tanh(values):
    return jax.nn.gelu(values, approximate=True)


def exchange(blocks, axes):
    return lax.all_to_all(blocks, axes, split_axis=0, concat_axis=0, tiled=True)


def gather_rows(shard, axes, count):
    copies = jnp.broadcast_to(shard[None], (count,) + shard.shape)
    return exchange(copies, axes).reshape((count * shard.shape[0],) + shard.shape[1:])


def contract(left, right, left_dim, right_dim):
    return lax.dot_general(
        left, right, (((left_dim,), (right_dim,)), ((), ())), preferred_element_type=jnp.float32
    )


def exact_dot(left, right, left_dim, right_dim):
    return lax.dot_general(
        left, right, (((left_dim,), (right_dim,)), ((), ())),
        precision=lax.Precision.HIGHEST, preferred_element_type=jnp.float32,
    )


def lane_place(index, size, lanes):
    row = lax.broadcasted_iota(jnp.int32, (size, lanes), 0)
    column = lax.broadcasted_iota(jnp.int32, (size, lanes), 1)
    return (column == row + index * size).astype(jnp.float32)


def gram_kernel(block_ref, copies_ref, total_ref):
    clients, rows, columns = block_ref.shape
    tall = 8
    size = clients * tall
    total_ref[...] = jnp.zeros_like(total_ref)

    @pl.loop(0, rows // tall)
    def _(index):
        start = pl.multiple_of(index * tall, tall)
        tile = block_ref[:, pl.ds(start, tall), :].reshape(size, columns)
        total_ref[...] += contract(tile, tile, 1, 1)

    row_index = lax.broadcasted_iota(jnp.int32, (size, size), 0)
    col_index = lax.broadcasted_iota(jnp.int32, (size, size), 1)
    kept = jnp.where(row_index % tall == col_index % tall, total_ref[...], 0.0)
    pick_client = lax.broadcasted_iota(jnp.int32, (clients, size), 0)
    pick_row = lax.broadcasted_iota(jnp.int32, (clients, size), 1) // tall
    pick = (pick_row == pick_client).astype(jnp.float32)
    gram = exact_dot(exact_dot(pick, kept, 1, 0), pick, 1, 1)
    packed = jnp.zeros(copies_ref.shape[1:], jnp.float32)
    for index in range(clients // tall):
        packed += exact_dot(
            gram[index * tall : (index + 1) * tall],
            lane_place(index, clients, copies_ref.shape[2]), 1, 0,
        )
    copies_ref[...] = jnp.broadcast_to(packed[None], copies_ref.shape)


def pair_products(exchanged, copies):
    clients, rows, columns = exchanged.shape
    return pl.pallas_call(
        gram_kernel,
        out_shape=jax.ShapeDtypeStruct((copies, 8, 128), jnp.float32),
        in_specs=[pl.BlockSpec(memory_space=pltpu.VMEM)],
        out_specs=pl.BlockSpec(memory_space=pltpu.VMEM),
        scratch_shapes=[pltpu.VMEM((clients * 8, clients * 8), jnp.float32)],
        cost_estimate=pl.CostEstimate(
            flops=2 * rows * clients * clients * 8 * columns,
            bytes_accessed=2 * clients * rows * columns,
            transcendentals=0,
        ),
        name="pair_products",
    )(exchanged)


def finish_kernel(parts_ref, neighbours_ref, owned_ref, update_ref, relative_ref):
    clients, rows, columns = owned_ref.shape
    pieces, _, width = update_ref.shape
    tall = 8
    packed = jnp.sum(parts_ref[...], axis=0)
    gram = jnp.concatenate(
        [
            exact_dot(packed, lane_place(index, clients, packed.shape[1]), 1, 1)
            for index in range(clients // tall)
        ],
        axis=0,
    )
    row_index = lax.broadcasted_iota(jnp.int32, (clients, clients), 0)
    col_index = lax.broadcasted_iota(jnp.int32, (clients, clients), 1)
    same = row_index == col_index
    diagonal = jnp.where(same, gram, 0.0)
    distance = (
        jnp.sum(diagonal, axis=1, keepdims=True)
        + jnp.sum(diagonal, axis=0, keepdims=True)
        - 2.0 * gram
    )
    distance = jnp.where(same, 1e30, distance)
    rank = jnp.zeros((clients, clients), jnp.float32)
    for index in range(clients):
        rival = distance[:, index : index + 1]
        ahead = (rival < distance) | ((rival == distance) & (index < col_index))
        rank += jnp.where(ahead, 1.0, 0.0)
    count = jnp.sum(
        jnp.where(same, neighbours_ref[...].astype(jnp.float32), 0.0), axis=1, keepdims=True
    )
    scores = jnp.sum(jnp.where(rank < count, distance, 0.0), axis=1, keepdims=True)
    mean = jnp.sum(scores, axis=0, keepdims=True) / clients
    exponent = jnp.exp(-4.0 * (scores / mean))
    weights = exponent / jnp.sum(exponent, axis=0, keepdims=True)
    relative_ref[...] = clients * jnp.sum(jnp.where(same, weights, 0.0), axis=0, keepdims=True)
    for start in range(0, rows, tall):
        total = jnp.zeros((tall, columns), jnp.float32)
        for index in range(clients):
            total += weights[index : index + 1, :] * owned_ref[
                index, start : start + tall, :
            ].astype(jnp.float32)
        total = total.astype(update_ref.dtype)
        for piece in range(pieces):
            update_ref[piece, start : start + tall, :] = total[
                :, piece * width : (piece + 1) * width
            ]


def finish(parts, neighbours, owned, pieces):
    clients, rows, columns = owned.shape
    vmem = pl.BlockSpec(memory_space=pltpu.VMEM)
    return pl.pallas_call(
        finish_kernel,
        in_specs=[vmem] * 3,
        out_specs=[vmem] * 2,
        out_shape=[
            jax.ShapeDtypeStruct((pieces, rows, columns // pieces), jnp.bfloat16),
            jax.ShapeDtypeStruct((1, clients), jnp.float32),
        ],
        cost_estimate=pl.CostEstimate(
            flops=2 * clients * rows * columns,
            bytes_accessed=2 * clients * rows * columns + 2 * rows * columns,
            transcendentals=clients,
        ),
        name="finish",
    )(parts, neighbours, owned)


def delta_kernel(left_ref, other_left_ref, right_ref, other_right_ref, out_ref):
    planes, _, rows, tokens = right_ref.shape
    right = right_ref[...].reshape(planes * rows, tokens)
    other_right = other_right_ref[...].reshape(planes * rows, tokens)
    total = contract(left_ref[...], right, 1, 1) + contract(other_left_ref[...], other_right, 1, 1)
    out_ref[...] = (-total).astype(out_ref.dtype).reshape(out_ref.shape)


def make_deltas(left, other_left, right, other_right, height):
    planes, cores, rows, tokens = right.shape
    slices = left.shape[0] // height
    chunks = 2
    tall = left.shape[0] // chunks
    left_spec = pl.BlockSpec((tall, tokens), lambda core, chunk: (chunk, 0))
    right_spec = pl.BlockSpec((planes, 1, rows, tokens), lambda core, chunk: (0, core, 0, 0))
    return pl.pallas_call(
        delta_kernel,
        grid=(cores, chunks),
        in_specs=[left_spec, left_spec, right_spec, right_spec],
        out_specs=pl.BlockSpec(
            (slices // chunks, height, planes * rows), lambda core, chunk: (core * chunks + chunk, 0, 0)
        ),
        out_shape=jax.ShapeDtypeStruct((cores * slices, height, planes * rows), jnp.bfloat16),
        cost_estimate=pl.CostEstimate(
            flops=4 * left.shape[0] * planes * cores * rows * tokens,
            bytes_accessed=4 * (left.shape[0] + planes * cores * rows) * tokens
            + 2 * left.shape[0] * planes * cores * rows,
            transcendentals=0,
        ),
        name="make_deltas",
    )(left, other_left, right, other_right)


def rms_normed(raw, norm_gain):
    widened = raw.astype(jnp.float32)
    inverse_rms = lax.rsqrt(jnp.mean(widened * widened, axis=0, keepdims=True) + 1e-06)
    return (widened * inverse_rms * norm_gain[:, None]).astype(jnp.bfloat16)


def swap_blocks(shard, z_count, core_count):
    pairs = [
        ((z * core_count + core) * z_count + p, (p * core_count + core) * z_count + z)
        for z in range(z_count)
        for core in range(core_count)
        for p in range(z_count)
    ]
    return lax.ppermute(shard, ZC + XY, pairs)


def on_device(inputs, targets, norm_gain, gate_weight, up_weight, down_weight, neighbours):
    token_count = inputs.shape[1]
    param_count = lax.axis_size(XY)
    z_count = lax.axis_size("z")
    core_count = lax.axis_size("core")
    client_count = z_count * core_count
    factor = 1.0 / math.sqrt(token_count)
    features = param_count * inputs.shape[2]
    slice_rows = features // client_count
    hidden_units = gate_weight.shape[1]

    own_inputs = inputs[0].T
    met_inputs = lax.all_gather(own_inputs, "z", axis=0, tiled=False)
    gathered = gather_rows(own_inputs, XY, param_count)
    normed = rms_normed(gathered, norm_gain)
    gate_value = contract(gate_weight, normed, 0, 0)
    up_value = contract(up_weight, normed, 0, 0)
    hidden = (gelu_tanh(gate_value) * up_value).astype(jnp.bfloat16)
    partial_out = contract(down_weight, hidden, 0, 0).astype(jnp.bfloat16)
    parts = exchange(
        partial_out.reshape(param_count, features // param_count, token_count), XY
    )
    summed = jnp.sum(parts.astype(jnp.float32), axis=0)
    own_residual = ((summed - targets[0].T.astype(jnp.float32)) * factor).astype(jnp.bfloat16)
    met_residual = swap_blocks(own_residual, z_count, core_count)
    met_residual = lax.all_gather(met_residual, "z", axis=0, tiled=True)

    share = hidden_units // z_count
    height = -(-3 * share // 8) * 8
    first = lax.axis_index("z") * share
    column = lax.axis_index("core") * (features // core_count)

    def own_part(rows):
        return lax.dynamic_slice(rows, (first, column), (share, features // core_count))

    group = -(-share // 8) * 8
    fill = jnp.zeros((group - share, features // core_count), jnp.bfloat16)
    part = jnp.concatenate(
        [own_part(gate_weight.T), fill, own_part(up_weight.T), fill, own_part(down_weight), fill],
        axis=0,
    )
    part, own_residual = lax.optimization_barrier((part, own_residual))
    part = gather_rows(part, XY, param_count)
    part, met_inputs = lax.optimization_barrier((part, met_inputs))
    other = lax.ppermute(part, "core", [(0, 1), (1, 0)])
    met_inputs = exchange(met_inputs, XY).reshape(features, token_count)
    low = lax.axis_index("core") == 0
    met_weights = jnp.concatenate(
        [jnp.where(low, part, other), jnp.where(low, other, part)], axis=1
    ).reshape(param_count, 3 * group, features)
    ahead_weights = met_weights[:, : 2 * group].reshape(2 * param_count * group, features)
    back_weights = met_weights[:, 2 * group :].reshape(param_count * group, features)
    met_normed = rms_normed(met_inputs, norm_gain)
    values = contract(ahead_weights, met_normed, 1, 0)
    values, back_weights, met_residual = lax.optimization_barrier(
        (values, back_weights, met_residual)
    )
    values = values.reshape(param_count, 2 * group, token_count)
    activated, gelu_back = jax.vjp(gelu_tanh, values[:, :share])
    up_value = values[:, group : group + share]
    hidden = (activated * up_value).astype(jnp.bfloat16)
    back_hidden = contract(back_weights, met_residual, 1, 0)
    back_hidden = back_hidden.reshape(param_count, group, token_count)[:, :share]
    back_gate = gelu_back(back_hidden * up_value)[0].astype(jnp.bfloat16)
    back_up = (back_hidden * activated).astype(jnp.bfloat16)
    rest = jnp.zeros((param_count, height - 3 * share, token_count), jnp.bfloat16)
    none = jnp.zeros((param_count, share, token_count), jnp.bfloat16)
    flat = (param_count * height, token_count)
    by_plane = (z_count, core_count, slice_rows, token_count)
    deltas = make_deltas(
        jnp.concatenate([back_gate, back_up, none, rest], axis=1).reshape(flat),
        jnp.concatenate([none, none, hidden, rest], axis=1).reshape(flat),
        met_normed.reshape(by_plane),
        met_residual.reshape(by_plane),
        height,
    )
    owned = exchange(deltas, ("core",) + XY)

    gram = pair_products(owned, core_count * param_count)
    gram = jnp.sum(exchange(gram, ("core",) + XY), axis=0)
    gram = exchange(jnp.broadcast_to(gram[None], (z_count,) + gram.shape), "z")
    order = neighbours.reshape(z_count, core_count).T.reshape(1, -1)
    update, relative = finish(gram, order, owned, z_count)
    update = exchange(update, "z").astype(jnp.float32)

    def placed(index):
        rows = update[:, index * share : (index + 1) * share]
        return rows.reshape(hidden_units, slice_rows).T

    return (
        placed(0),
        placed(1),
        placed(2),
        relative.reshape(core_count, z_count).T.reshape(-1),
    )


def solution(mesh):
    torus = Mesh(mesh.devices.reshape(16, 2, 4, 4), ("z", "core", "x", "y"))
    in_specs = (
        P(ZC, None, XY),
        P(ZC, None, XY),
        P(),
        P(None, XY),
        P(None, XY),
        P(XY, None),
        P(),
    )
    out_specs = (P(ZC, XY), P(ZC, XY), P(ZC, XY), P())
    return jax.shard_map(
        on_device, mesh=torus, in_specs=in_specs, out_specs=out_specs, check_vma=False
    )
```

time: 384 us -> 392 us (1.021)
  waiting for transfers between devices: 144 us -> 164 us
  Pallas kernels: 5.85 us -> 19.4 us
  matrix products: 21 us -> 10 us
  starting transfers between devices: 48.5 us -> 39.8 us
  local copies, waits for them, and re-layouts: 23 us -> 18.1 us
    all_gather x1, waiting for transfers between devices: 32.6 us -> 77.6 us  [on_device(): met_residual = lax.all_gather(met_residual, 'z', axis=0, tiled=True)]
    all_to_all x6 -> x5, waiting for transfers between devices: 66.3 us -> 42 us  [exchange(): return lax.all_to_all(blocks, axes, split_axis=0, concat_axis=0, tiled=True)]
    all_to_all x6 -> x5, starting transfers between devices: 47.7 us -> 26.3 us  [exchange(): return lax.all_to_all(blocks, axes, split_axis=0, concat_axis=0, tiled=True)]
    pallas_call x1 -> x3, Pallas kernels: 5.85 us -> 19.4 us  [the longest x1 8.72 us: make_deltas(): pl.pallas_call(delta_kernel, grid=(cores, chunks), in_specs=[left_spec, l...]
    ppermute x0 -> x1, starting transfers between devices: none -> 12.5 us  [on_device(): other = lax.ppermute(part, 'core', [(0, 1), (1, 0)])]
    dot_general x8 -> x4, matrix products: 21 us -> 10 us  [contract(): lax.dot_general(left, right, (((left_dim,), (right_dim,)), ((), ())), pre...]
    reduce_sum x6 -> x1, other arithmetic: 4.35 us -> 0.04 us  [on_device(): gram = jnp.sum(exchange(gram, ('core',) + XY), axis=0)]
  transfers between devices with their start and end apart: 9 -> 9, of which waited for: 7 -> 6; matrix products, arithmetic and copies ran while one was open for 4% -> 4% of each run, Pallas kernels for 0% -> 0%
where the time goes in v5:
time: 392 us; the launch traced here: 386 us
  waiting for transfers between devices  164 us (42%)
  blocking collectives  110 us (28%)
  starting transfers between devices  39.8 us (10%)
  Pallas kernels  19.4 us (5%)
  local copies, waits for them, and re-layouts  18.1 us (5%)
  between operations  14.3 us (4%)
  matrix products  10 us (3%)
  other arithmetic  9.95 us (3%)
    all_to_all x3, blocking collectives, exchange(): return lax.all_to_all(blocks, axes, split_axis=0, concat_axis=0, tiled=True)  110 us
    all_gather x1, waiting for transfers between devices, on_device(): met_residual = lax.all_gather(met_residual, 'z', axis=0, tiled=True)  77.6 us
    all_gather x1, waiting for transfers between devices, on_device(): met_inputs = lax.all_gather(own_inputs, 'z', axis=0, tiled=False)  44.1 us
    all_to_all x5, waiting for transfers between devices, exchange(): return lax.all_to_all(blocks, axes, split_axis=0, concat_axis=0, tiled=True)  42 us
    all_to_all x5, starting transfers between devices, exchange(): return lax.all_to_all(blocks, axes, split_axis=0, concat_axis=0, tiled=True)  26.3 us
    ppermute x1, starting transfers between devices, on_device(): other = lax.ppermute(part, 'core', [(0, 1), (1, 0)])  12.5 us
    dot_general x4, matrix products, contract(): lax.dot_general(left, right, (((left_dim,), (right_dim,)), ((), ())), pre...  10 us
    pallas_call x1, Pallas kernels, make_deltas(): pl.pallas_call(delta_kernel, grid=(cores, chunks), in_specs=[left_spec, l...  8.72 us
  transfers between devices with their start and end apart: 9, of which 6 were waited for; matrix products, arithmetic and copies ran while one was open for 4% of the time, Pallas kernels for 0%

profile of v5, /device:TPU:1, one launch (start us, length us, event | category | flops | bytes accessed | tf_op | source)
XLA Modules:
  0.0 385.7 jit_solution(2606999489579612881)
XLA Ops:
  7.2 1.1 broadcast_in_dim.15
  8.2 29.9 %all_to_all.40 = bf16[16,144,384]{2,1,0:T(8,128)(2,1)S(1)} all-to-all(bf16[16,144,384]{2,1,0:T(8,128)(2,1)S(1)} %broadcast_in_dim.15), channel_id=1, replica_groups=mesh['z'=16,'core'=2,'x'=4,'y'=4] {'x','y'}, dimensions={0} | all-to-all | bytes 3538944 | tf_op jit(solution)/shard_map/all_to_all | solution.py:20
  38.9 0.5 fusion.2
  39.3 0.8 copy-done.6
  40.2 1.7 fusion.18
  41.9 3.8 fusion
  45.7 2.2 copy.22
  47.9 3.7 all-to-all-start.1
  51.7 0.7 all-gather.6.cloned.1.call-update
  52.4 1.0 dynamic_slice.11
  53.4 1.0 dynamic-slice_bitcast_fusion
  54.6 19.0 %all-to-all-done.1 = bf16[16,144,384]{2,1,0:T(8,128)(2,1)S(1)} async-done(((bf16[16,144,384]{2,1,0:T(8,128)(2,1)}), bf16[16,144,384]{2,1,0:T(8,128)(2,1)S(1)}, u32[]{:S(2)}, u32[]{:S(2)}) %all-to-all-start.1) | async-done | bytes 1769504 | tf_op jit(solution)/shard_map/all_to_all | solution.py:20
  73.9 1.7 broadcast_in_dim.16
  75.6 4.9 %all-to-all-start.2 = ((bf16[16,72,1152]{2,1,0:T(8,128)(2,1)}), bf16[16,72,1152]{2,1,0:T(8,128)(2,1)S(1)}, u32[]{:S(2)}, u32[]{:S(2)}) async-start(bf16[16,72,1152]{2,1,0:T(8,128)(2,1)} %broadcast_in_dim.16), calls=%async_computation.2 | async-start | bytes 5308416 | tf_op jit(solution)/shard_map/all_to_all | solution.py:20
  80.5 44.1 %all-gather.6.cloned.1.call-done = bf16[2304,384]{1,0:T(8,128)(2,1)} async-done(((bf16[144,384]{1,0:T(8,128)(2,1)}), bf16[2304,384]{1,0:T(8,128)(2,1)}) %all-gather.6.cloned.1.call-update) | async-done | bytes 1769488 | tf_op jit(solution)/shard_map/all_gather | solution.py:221
  124.6 1.5 copy-done
  126.1 6.2 %all-to-all-start.3 = ((bf16[16,144,384]{2,1,0:T(8,128)(2,1)}), bf16[16,144,384]{2,1,0:T(8,128)(2,1)S(1)}, u32[]{:S(2)}, u32[]{:S(2)}) async-start(bf16[16,144,384]{2,1,0:T(8,128)(2,1)} %bitcast.72), calls=%async_computation.3 | async-start | bytes 3538944 | tf_op jit(solution)/shard_map/all_to_all | solution.py:20
  132.5 12.5 %collective-permute-start = (bf16[1152,1152]{1,0:T(8,128)(2,1)}, bf16[1152,1152]{1,0:T(8,128)(2,1)}, u32[]{:S(2)}, u32[]{:S(2)}) collective-permute-start(bf16[1152,1152]{1,0:T(8,128)(2,1)} %bitcast.69), channel_id=1, source_target_pairs={{0,16},{16,0},{1,17},{17,1},{2,18},{18,2},{3,19},{19,3},{4,20},{20... | collective-permute-start | bytes 7962632 | tf_op jit(solution)/shard_map/ppermute | solution.py:253
  145.0 0.8 collective-permute-start.1
  146.2 0.6 copy-done.4
  146.9 2.2 all-to-all-done.3
  149.6 1.8 multiply_convert_fusion.right_ref
  151.4 0.5 multiply_convert_fusion.1
  151.9 1.3 copy-done.1
  153.1 2.2 broadcast_select_fusion.1
  156.1 2.0 fusion.23
  158.1 77.6 %all-gather.4.cloned.1.call-done = bf16[2304,384]{1,0:T(8,128)(2,1)} async-done(((bf16[144,384]{1,0:T(8,128)(2,1)}), bf16[2304,384]{1,0:T(8,128)(2,1)}) %all-gather.4.cloned.1.call-update) | async-done | bytes 1769488 | tf_op jit(solution)/shard_map/all_gather | solution.py:234
  235.7 2.5 fusion.24
  238.3 0.5 fusion.11
  238.8 1.5 maximum_maximum_fusion.1
  240.3 8.7 %make_deltas.1 = bf16[32,56,1152]{2,1,0:T(8,128)(2,1)} custom-call(bf16[896,384]{1,0:T(8,128)(2,1)} %bitcast.77, bf16[896,384]{1,0:T(8,128)(2,1)} %bitcast.76, bf16[16,2,72,384]{3,2,1,0:T(8,128)(2,1)} %multiply_convert_fusion.right_ref, bf16[16,2,72,384]{3,2,1,0:T(8,128)(2,1)} %bitcast.86), custom_call_target="tpu_custom_call" | custom-call | flops 3170893824 | bytes 9043968 | tf_op jit(solution)/shard_map/make_deltas/pallas_call | solution.py:175
  249.0 67.4 %all_to_all.41.block_ref.owned_ref = bf16[32,56,1152]{2,1,0:T(8,128)(2,1)} all-to-all(bf16[32,56,1152]{2,1,0:T(8,128)(2,1)} %make_deltas.1), channel_id=1, replica_groups=mesh['z'=16,'core'=2,'x'=4,'y'=4] {'core','x','y'}, dimensions={0} | all-to-all | bytes 8257536 | tf_op jit(solution)/shard_map/all_to_all | solution.py:20
  316.4 6.2 %pair_products.1 = f32[32,8,128]{2,1,0:T(8,128)} custom-call(bf16[32,56,1152]{2,1,0:T(8,128)(2,1)} %all_to_all.41.block_ref.owned_ref), custom_call_target="tpu_custom_call" | custom-call | flops 1056964608 | bytes 4128768 | tf_op jit(solution)/shard_map/pair_products/pallas_call | solution.py:77
  322.6 12.5 %all_to_all.42 = f32[32,8,128]{2,1,0:T(8,128)S(1)} all-to-all(f32[32,8,128]{2,1,0:T(8,128)} %pair_products.1), channel_id=1, replica_groups=mesh['z'=16,'core'=2,'x'=4,'y'=4] {'core','x','y'}, dimensions={0} | all-to-all | bytes 262144 | tf_op jit(solution)/shard_map/all_to_all | solution.py:20
  335.1 0.6 broadcast_in_dim.39
  335.8 7.6 %all-to-all-start.6 = ((f32[16,8,128]{2,1,0:T(8,128)}), f32[16,8,128]{2,1,0:T(8,128)S(1)}, u32[]{:S(2)}, u32[]{:S(2)}) async-start(f32[16,8,128]{2,1,0:T(8,128)} %broadcast_in_dim.39), calls=%async_computation.6 | async-start | bytes 131072 | tf_op jit(solution)/shard_map/all_to_all | solution.py:20
  343.6 0.6 reshape.119.neighbours_ref
  344.2 10.8 %all-to-all-done.6.parts_ref = f32[16,8,128]{2,1,0:T(8,128)S(1)} async-done(((f32[16,8,128]{2,1,0:T(8,128)}), f32[16,8,128]{2,1,0:T(8,128)S(1)}, u32[]{:S(2)}, u32[]{:S(2)}) %all-to-all-start.6) | async-done | bytes 65568 | tf_op jit(solution)/shard_map/all_to_all | solution.py:20
  355.0 0.6 copy-done.2
  355.6 4.5 %finish.1 = (bf16[16,56,72]{2,1,0:T(8,128)(2,1)}, f32[1,32]{1,0:T(1,128)}) custom-call(f32[16,8,128]{2,1,0:T(8,128)} %copy-done.2, s32[1,32]{1,0:T(1,128)} %reshape.119.neighbours_ref, bf16[32,56,1152]{2,1,0:T(8,128)(2,1)} %all_to_all.41.block_ref.owned_ref), custom_call_target="tpu_custom_call" | custom-call | flops 4128768 | bytes 4257792 | tf_op jit(solution)/shard_map/finish/pallas_call | solution.py:143
  360.1 3.8 all-to-all-start.7
  363.9 0.5 broadcast.101
  364.5 1.3 reduce.5
  366.0 0.6 reshape.124
  366.6 9.9 %all-to-all-done.7 = bf16[16,56,72]{2,1,0:T(8,128)(2,1)S(1)} async-done(((bf16[16,56,72]{2,1,0:T(8,128)(2,1)}), bf16[16,56,72]{2,1,0:T(8,128)(2,1)S(1)}, u32[]{:S(2)}, u32[]{:S(2)}) %all-to-all-start.7) | async-done | bytes 129056 | tf_op jit(solution)/shard_map/all_to_all | solution.py:20
  376.5 0.8 copy.25
  377.3 0.8 copy.26
  378.1 0.8 copy.27
  (45 shorter events, 3.2 us)
Async XLA Ops:
  38.1 0.7 copy-start.5
  38.9 1.3 copy-start.6
  47.9 25.7 %all-to-all-start.1 = ((bf16[16,144,384]{2,1,0:T(8,128)(2,1)}), bf16[16,144,384]{2,1,0:T(8,128)(2,1)S(1)}, u32[]{:S(2)}, u32[]{:S(2)}) async-start(bf16[16,144,384]{2,1,0:T(8,128)(2,1)} %bitcast.8), calls=%async_computation.1 | async-start | bytes 3538944 | tf_op jit(solution)/shard_map/all_to_all | solution.py:20
  51.6 22.2 %copy-start.3 = (bf16[1,384,144]{1,2,0:T(8,128)(2,1)S(1)}, bf16[1,384,144]{1,2,0:T(8,128)(2,1)}, u32[]{:S(2)}) copy-start(bf16[1,384,144]{1,2,0:T(8,128)(2,1)} %param.8) | copy-start | bytes 331780
  51.7 73.0 %all-gather.6.cloned.1.call-start = ((), (), s32[]{:S(2)}) async-start(), calls=%async_computation.9 | async-start | bytes 1880064 | tf_op jit(solution)/shard_map/all_gather | solution.py:221
  75.6 49.0 %all-to-all-start.2 = ((bf16[16,72,1152]{2,1,0:T(8,128)(2,1)}), bf16[16,72,1152]{2,1,0:T(8,128)(2,1)S(1)}, u32[]{:S(2)}, u32[]{:S(2)}) async-start(bf16[16,72,1152]{2,1,0:T(8,128)(2,1)} %broadcast_in_dim.16), calls=%async_computation.2 | async-start | bytes 5308416 | tf_op jit(solution)/shard_map/all_to_all | solution.py:20
  124.6 1.5 copy-start
  126.1 23.0 %all-to-all-start.3 = ((bf16[16,144,384]{2,1,0:T(8,128)(2,1)}), bf16[16,144,384]{2,1,0:T(8,128)(2,1)S(1)}, u32[]{:S(2)}, u32[]{:S(2)}) async-start(bf16[16,144,384]{2,1,0:T(8,128)(2,1)} %bitcast.72), calls=%async_computation.3 | async-start | bytes 3538944 | tf_op jit(solution)/shard_map/all_to_all | solution.py:20
  132.4 103.3 %all-gather.4.cloned.1.call-start = ((), (), s32[]{:S(2)}) async-start(), calls=%async_computation.8 | async-start | bytes 1880064 | tf_op jit(solution)/shard_map/all_gather | solution.py:234
  132.5 19.4 %collective-permute-start = (bf16[1152,1152]{1,0:T(8,128)(2,1)}, bf16[1152,1152]{1,0:T(8,128)(2,1)}, u32[]{:S(2)}, u32[]{:S(2)}) collective-permute-start(bf16[1152,1152]{1,0:T(8,128)(2,1)} %bitcast.69), channel_id=1, source_target_pairs={{0,16},{16,0},{1,17},{17,1},{2,18},{18,2},{3,19},{19,3},{4,20},{20... | collective-permute-start | bytes 7962632 | tf_op jit(solution)/shard_map/ppermute | solution.py:253
  145.0 1.2 collective-permute-start.1
  146.2 0.6 copy-start.4
  151.4 1.7 copy-start.1
  316.4 27.0 %copy-start.7 = (s32[32]{0:T(128)S(1)}, s32[32]{0:T(128)}, u32[]{:S(2)}) copy-start(s32[32]{0:T(128)} %param.13) | copy-start | bytes 388
  335.8 19.2 %all-to-all-start.6 = ((f32[16,8,128]{2,1,0:T(8,128)}), f32[16,8,128]{2,1,0:T(8,128)S(1)}, u32[]{:S(2)}, u32[]{:S(2)}) async-start(f32[16,8,128]{2,1,0:T(8,128)} %broadcast_in_dim.39), calls=%async_computation.6 | async-start | bytes 131072 | tf_op jit(solution)/shard_map/all_to_all | solution.py:20
  355.0 0.6 copy-start.2
  360.1 16.3 %all-to-all-start.7 = ((bf16[16,56,72]{2,1,0:T(8,128)(2,1)}), bf16[16,56,72]{2,1,0:T(8,128)(2,1)S(1)}, u32[]{:S(2)}, u32[]{:S(2)}) async-start(bf16[16,56,72]{2,1,0:T(8,128)(2,1)} %get-tuple-element.18), calls=%async_computation.7 | async-start | bytes 458752 | tf_op jit(solution)/shard_map/all_to_all | solution.py:20
Sparse Core Ops, SparseCore 0:
  54.5 70.0 all-gather.5
  147.0 88.6 all-gather.3

commit v6 on v5

--- a/solution.py
+++ b/solution.py
@@ -157,37 +157,46 @@
     )(parts, neighbours, owned)
 
 
-def delta_kernel(left_ref, other_left_ref, right_ref, other_right_ref, out_ref):
-    planes, _, rows, tokens = right_ref.shape
-    right = right_ref[...].reshape(planes * rows, tokens)
-    other_right = other_right_ref[...].reshape(planes * rows, tokens)
-    total = contract(left_ref[...], right, 1, 1) + contract(other_left_ref[...], other_right, 1, 1)
-    out_ref[...] = (-total).astype(out_ref.dtype).reshape(out_ref.shape)
-
-
-def make_deltas(left, other_left, right, other_right, height):
-    planes, cores, rows, tokens = right.shape
-    slices = left.shape[0] // height
-    chunks = 2
-    tall = left.shape[0] // chunks
-    left_spec = pl.BlockSpec((tall, tokens), lambda core, chunk: (chunk, 0))
-    right_spec = pl.BlockSpec((planes, 1, rows, tokens), lambda core, chunk: (0, core, 0, 0))
+def delta_kernel(ahead_ref, back_ref, normed_ref, residual_ref, out_ref):
+    planes, _, rows, tokens = normed_ref.shape
+    slices, ahead_rows, _ = ahead_ref.shape
+    back_rows = back_ref.shape[1]
+    columns = planes * rows
+    shared = ahead_rows + back_rows - out_ref.shape[1]
+    ahead = contract(
+        ahead_ref[...].reshape(slices * ahead_rows, tokens),
+        normed_ref[...].reshape(columns, tokens), 1, 1,
+    ).reshape(slices, ahead_rows, columns)
+    back = contract(
+        back_ref[...].reshape(slices * back_rows, tokens),
+        residual_ref[...].reshape(columns, tokens), 1, 1,
+    ).reshape(slices, back_rows, columns)
+    first = ahead_rows - shared
+    out_ref[:, :first, :] = (-ahead[:, :first]).astype(out_ref.dtype)
+    both = ahead[:, first:] + back[:, :shared]
+    out_ref[:, first:ahead_rows, :] = (-both).astype(out_ref.dtype)
+    out_ref[:, ahead_rows:, :] = (-back[:, shared:]).astype(out_ref.dtype)
+
+
+def make_deltas(ahead, back, normed, residual, height):
+    planes, cores, rows, tokens = normed.shape
+    slices = ahead.shape[0]
+    whole = lambda left: pl.BlockSpec(left.shape, lambda core: (0, 0, 0))
+    right_spec = pl.BlockSpec((planes, 1, rows, tokens), lambda core: (0, core, 0, 0))
     return pl.pallas_call(
         delta_kernel,
-        grid=(cores, chunks),
-        in_specs=[left_spec, left_spec, right_spec, right_spec],
-        out_specs=pl.BlockSpec(
-            (slices // chunks, height, planes * rows), lambda core, chunk: (core * chunks + chunk, 0, 0)
-        ),
+        grid=(cores,),
+        in_specs=[whole(ahead), whole(back), right_spec, right_spec],
+        out_specs=pl.BlockSpec((slices, height, planes * rows), lambda core: (core, 0, 0)),
         out_shape=jax.ShapeDtypeStruct((cores * slices, height, planes * rows), jnp.bfloat16),
         cost_estimate=pl.CostEstimate(
-            flops=4 * left.shape[0] * planes * cores * rows * tokens,
-            bytes_accessed=4 * (left.shape[0] + planes * cores * rows) * tokens
-            + 2 * left.shape[0] * planes * cores * rows,
+            flops=2 * slices * (ahead.shape[1] + back.shape[1]) * planes * cores * rows * tokens,
+            bytes_accessed=4 * planes * cores * rows * tokens
+            + 2 * slices * height * planes * cores * rows,
             transcendentals=0,
         ),
         name="make_deltas",
-    )(left, other_left, right, other_right)
+    )(ahead, back, normed, residual)
 
 
 def rms_normed(raw, norm_gain):
@@ -241,10 +250,20 @@
     def own_part(rows):
         return lax.dynamic_slice(rows, (first, column), (share, features // core_count))
 
-    group = -(-share // 8) * 8
-    fill = jnp.zeros((group - share, features // core_count), jnp.bfloat16)
+    ahead_rows = -(-2 * share // 8) * 8
+    back_rows = -(-share // 8) * 8
+
+    def fill(rows):
+        return jnp.zeros((rows, features // core_count), jnp.bfloat16)
+
     part = jnp.concatenate(
-        [own_part(gate_weight.T), fill, own_part(up_weight.T), fill, own_part(down_weight), fill],
+        [
+            own_part(gate_weight.T),
+            own_part(up_weight.T),
+            fill(ahead_rows - 2 * share),
+            own_part(down_weight),
+            fill(back_rows - share),
+        ],
         axis=0,
     )
     part, own_residual = lax.optimization_barrier((part, own_residual))
@@ -255,29 +274,31 @@
     low = lax.axis_index("core") == 0
     met_weights = jnp.concatenate(
         [jnp.where(low, part, other), jnp.where(low, other, part)], axis=1
-    ).reshape(param_count, 3 * group, features)
-    ahead_weights = met_weights[:, : 2 * group].reshape(2 * param_count * group, features)
-    back_weights = met_weights[:, 2 * group :].reshape(param_count * group, features)
+    ).reshape(param_count, ahead_rows + back_rows, features)
+    ahead_weights = met_weights[:, :ahead_rows].reshape(param_count * ahead_rows, features)
+    back_weights = met_weights[:, ahead_rows:].reshape(param_count * back_rows, features)
     met_normed = rms_normed(met_inputs, norm_gain)
     values = contract(ahead_weights, met_normed, 1, 0)
     values, back_weights, met_residual = lax.optimization_barrier(
         (values, back_weights, met_residual)
     )
-    values = values.reshape(param_count, 2 * group, token_count)
+    values = values.reshape(param_count, ahead_rows, token_count)
     activated, gelu_back = jax.vjp(gelu_tanh, values[:, :share])
-    up_value = values[:, group : group + share]
+    up_value = values[:, share : 2 * share]
     hidden = (activated * up_value).astype(jnp.bfloat16)
     back_hidden = contract(back_weights, met_residual, 1, 0)
-    back_hidden = back_hidden.reshape(param_count, group, token_count)[:, :share]
+    back_hidden = back_hidden.reshape(param_count, back_rows, token_count)[:, :share]
     back_gate = gelu_back(back_hidden * up_value)[0].astype(jnp.bfloat16)
     back_up = (back_hidden * activated).astype(jnp.bfloat16)
-    rest = jnp.zeros((param_count, height - 3 * share, token_count), jnp.bfloat16)
-    none = jnp.zeros((param_count, share, token_count), jnp.bfloat16)
-    flat = (param_count * height, token_count)
+
+    def blank(rows):
+        return jnp.zeros((param_count, rows, token_count), jnp.bfloat16)
+
+    lead = 2 * share - (height - back_rows)
     by_plane = (z_count, core_count, slice_rows, token_count)
     deltas = make_deltas(
-        jnp.concatenate([back_gate, back_up, none, rest], axis=1).reshape(flat),
-        jnp.concatenate([none, none, hidden, rest], axis=1).reshape(flat),
+        jnp.concatenate([back_gate, back_up, blank(ahead_rows - 2 * share)], axis=1),
+        jnp.concatenate([blank(lead), hidden, blank(back_rows - share - lead)], axis=1),
         met_normed.reshape(by_plane),
         met_residual.reshape(by_plane),
         height,

time: 392 us -> 389 us (level)
  no operation moved by 1% of the time
where the time goes in v6:
time: 389 us; the launch traced here: 383 us
  waiting for transfers between devices  165 us (42%)
  blocking collectives  110 us (28%)
  starting transfers between devices  39.9 us (10%)
  local copies, waits for them, and re-layouts  18 us (5%)
  Pallas kernels  16.7 us (4%)
  between operations  14.3 us (4%)
  other arithmetic  10.2 us (3%)
  matrix products  9.72 us (2%)
    all_to_all x3, blocking collectives, exchange(): return lax.all_to_all(blocks, axes, split_axis=0, concat_axis=0, tiled=True)  110 us
    all_gather x1, waiting for transfers between devices, on_device(): met_residual = lax.all_gather(met_residual, 'z', axis=0, tiled=True)  78.2 us
    all_gather x1, waiting for transfers between devices, on_device(): met_inputs = lax.all_gather(own_inputs, 'z', axis=0, tiled=False)  43.7 us
    all_to_all x5, waiting for transfers between devices, exchange(): return lax.all_to_all(blocks, axes, split_axis=0, concat_axis=0, tiled=True)  42 us
    all_to_all x5, starting transfers between devices, exchange(): return lax.all_to_all(blocks, axes, split_axis=0, concat_axis=0, tiled=True)  26.7 us
    ppermute x1, starting transfers between devices, on_device(): other = lax.ppermute(part, 'core', [(0, 1), (1, 0)])  12.3 us
    dot_general x4, matrix products, contract(): lax.dot_general(left, right, (((left_dim,), (right_dim,)), ((), ())), pre...  9.72 us
  transfers between devices with their start and end apart: 9, of which 6 were waited for; matrix products, arithmetic and copies ran while one was open for 4% of the time, Pallas kernels for 0%

profile of v6, /device:TPU:1, one launch (start us, length us, event | category | flops | bytes accessed | tf_op | source)
XLA Modules:
  0.0 383.4 jit_solution(11362841140864051891)
XLA Ops:
  7.2 1.1 broadcast_in_dim.16
  8.2 29.9 %all_to_all.40 = bf16[16,144,384]{2,1,0:T(8,128)(2,1)S(1)} all-to-all(bf16[16,144,384]{2,1,0:T(8,128)(2,1)S(1)} %broadcast_in_dim.16), channel_id=1, replica_groups=mesh['z'=16,'core'=2,'x'=4,'y'=4] {'x','y'}, dimensions={0} | all-to-all | bytes 3538944 | tf_op jit(solution)/shard_map/all_to_all | solution.py:20
  38.9 0.5 fusion.2
  39.3 0.8 copy-done.6
  40.2 1.7 fusion.18
  41.9 3.8 fusion
  45.7 2.2 copy.22
  47.9 3.7 all-to-all-start.1
  51.7 0.7 all-gather.6.cloned.1.call-update
  52.4 1.0 dynamic_slice.11
  53.4 1.0 dynamic-slice_bitcast_fusion
  54.7 18.9 %all-to-all-done.1 = bf16[16,144,384]{2,1,0:T(8,128)(2,1)S(1)} async-done(((bf16[16,144,384]{2,1,0:T(8,128)(2,1)}), bf16[16,144,384]{2,1,0:T(8,128)(2,1)S(1)}, u32[]{:S(2)}, u32[]{:S(2)}) %all-to-all-start.1) | async-done | bytes 1769504 | tf_op jit(solution)/shard_map/all_to_all | solution.py:20
  73.9 1.8 broadcast_in_dim.17
  75.6 4.9 %all-to-all-start.2 = ((bf16[16,64,1152]{2,1,0:T(8,128)(2,1)}), bf16[16,64,1152]{2,1,0:T(8,128)(2,1)S(1)}, u32[]{:S(2)}, u32[]{:S(2)}) async-start(bf16[16,64,1152]{2,1,0:T(8,128)(2,1)} %broadcast_in_dim.17), calls=%async_computation.2 | async-start | bytes 4718592 | tf_op jit(solution)/shard_map/all_to_all | solution.py:20
  80.6 43.7 %all-gather.6.cloned.1.call-done = bf16[2304,384]{1,0:T(8,128)(2,1)} async-done(((bf16[144,384]{1,0:T(8,128)(2,1)}), bf16[2304,384]{1,0:T(8,128)(2,1)}) %all-gather.6.cloned.1.call-update) | async-done | bytes 1769488 | tf_op jit(solution)/shard_map/all_gather | solution.py:230
  124.3 1.4 copy-done
  125.8 6.6 %all-to-all-start.3 = ((bf16[16,144,384]{2,1,0:T(8,128)(2,1)}), bf16[16,144,384]{2,1,0:T(8,128)(2,1)S(1)}, u32[]{:S(2)}, u32[]{:S(2)}) async-start(bf16[16,144,384]{2,1,0:T(8,128)(2,1)} %bitcast.70), calls=%async_computation.3 | async-start | bytes 3538944 | tf_op jit(solution)/shard_map/all_to_all | solution.py:20
  132.4 12.3 %collective-permute-start = (bf16[1024,1152]{1,0:T(8,128)(2,1)}, bf16[1024,1152]{1,0:T(8,128)(2,1)}, u32[]{:S(2)}, u32[]{:S(2)}) collective-permute-start(bf16[1024,1152]{1,0:T(8,128)(2,1)} %bitcast.67), channel_id=1, source_target_pairs={{0,16},{16,0},{1,17},{17,1},{2,18},{18,2},{3,19},{19,3},{4,20},{20... | collective-permute-start | bytes 7077896 | tf_op jit(solution)/shard_map/ppermute | solution.py:272
  144.7 0.8 collective-permute-start.1
  145.6 0.6 copy-done.4
  146.5 2.5 all-to-all-done.3
  149.5 1.7 multiply_convert_fusion.normed_ref
  151.7 1.2 copy-done.1
  152.9 2.3 broadcast_select_fusion.1
  155.8 1.7 fusion.23
  157.5 78.2 %all-gather.4.cloned.1.call-done = bf16[2304,384]{1,0:T(8,128)(2,1)} async-done(((bf16[144,384]{1,0:T(8,128)(2,1)}), bf16[2304,384]{1,0:T(8,128)(2,1)}) %all-gather.4.cloned.1.call-update) | async-done | bytes 1769488 | tf_op jit(solution)/shard_map/all_gather | solution.py:243
  235.7 2.5 fusion.24
  238.3 0.6 fusion.11
  238.9 0.9 pad_maximum_fusion.1.ahead_ref
  239.8 0.9 maximum_maximum_fusion.back_ref
  240.7 6.0 %make_deltas.1 = bf16[32,56,1152]{2,1,0:T(8,128)(2,1)} custom-call(bf16[16,40,384]{2,1,0:T(8,128)(2,1)} %pad_maximum_fusion.1.ahead_ref, bf16[16,24,384]{2,1,0:T(8,128)(2,1)} %maximum_maximum_fusion.back_ref, bf16[16,2,72,384]{3,2,1,0:T(8,128)(2,1)} %multiply_convert_fusion.normed_ref, bf16[16,2,72,384]{3,2,1,0:T(8,128)(2,1)} %bitcast.73), custom_call_target="tpu_custom_call" | custom-call | flops 1811939328 | bytes 7667712 | tf_op jit(solution)/shard_map/make_deltas/pallas_call | solution.py:186
  246.7 67.4 %all_to_all.41.block_ref.owned_ref = bf16[32,56,1152]{2,1,0:T(8,128)(2,1)} all-to-all(bf16[32,56,1152]{2,1,0:T(8,128)(2,1)} %make_deltas.1), channel_id=1, replica_groups=mesh['z'=16,'core'=2,'x'=4,'y'=4] {'core','x','y'}, dimensions={0} | all-to-all | bytes 8257536 | tf_op jit(solution)/shard_map/all_to_all | solution.py:20
  314.1 6.2 %pair_products.1 = f32[32,8,128]{2,1,0:T(8,128)} custom-call(bf16[32,56,1152]{2,1,0:T(8,128)(2,1)} %all_to_all.41.block_ref.owned_ref), custom_call_target="tpu_custom_call" | custom-call | flops 1056964608 | bytes 4128768 | tf_op jit(solution)/shard_map/pair_products/pallas_call | solution.py:77
  320.3 12.5 %all_to_all.42 = f32[32,8,128]{2,1,0:T(8,128)S(1)} all-to-all(f32[32,8,128]{2,1,0:T(8,128)} %pair_products.1), channel_id=1, replica_groups=mesh['z'=16,'core'=2,'x'=4,'y'=4] {'core','x','y'}, dimensions={0} | all-to-all | bytes 262144 | tf_op jit(solution)/shard_map/all_to_all | solution.py:20
  332.8 0.6 broadcast_in_dim.39
  333.4 7.6 %all-to-all-start.6 = ((f32[16,8,128]{2,1,0:T(8,128)}), f32[16,8,128]{2,1,0:T(8,128)S(1)}, u32[]{:S(2)}, u32[]{:S(2)}) async-start(f32[16,8,128]{2,1,0:T(8,128)} %broadcast_in_dim.39), calls=%async_computation.6 | async-start | bytes 131072 | tf_op jit(solution)/shard_map/all_to_all | solution.py:20
  341.3 0.6 reshape.111.neighbours_ref
  341.9 10.8 %all-to-all-done.6.parts_ref = f32[16,8,128]{2,1,0:T(8,128)S(1)} async-done(((f32[16,8,128]{2,1,0:T(8,128)}), f32[16,8,128]{2,1,0:T(8,128)S(1)}, u32[]{:S(2)}, u32[]{:S(2)}) %all-to-all-start.6) | async-done | bytes 65568 | tf_op jit(solution)/shard_map/all_to_all | solution.py:20
  352.7 0.6 copy-done.2
  353.3 4.5 %finish.1 = (bf16[16,56,72]{2,1,0:T(8,128)(2,1)}, f32[1,32]{1,0:T(1,128)}) custom-call(f32[16,8,128]{2,1,0:T(8,128)} %copy-done.2, s32[1,32]{1,0:T(1,128)} %reshape.111.neighbours_ref, bf16[32,56,1152]{2,1,0:T(8,128)(2,1)} %all_to_all.41.block_ref.owned_ref), custom_call_target="tpu_custom_call" | custom-call | flops 4128768 | bytes 4257792 | tf_op jit(solution)/shard_map/finish/pallas_call | solution.py:143
  357.8 3.8 all-to-all-start.7
  361.6 0.5 broadcast.100
  362.1 1.3 reduce.5
  363.6 0.6 reshape.116
  364.2 9.9 %all-to-all-done.7 = bf16[16,56,72]{2,1,0:T(8,128)(2,1)S(1)} async-done(((bf16[16,56,72]{2,1,0:T(8,128)(2,1)}), bf16[16,56,72]{2,1,0:T(8,128)(2,1)S(1)}, u32[]{:S(2)}, u32[]{:S(2)}) %all-to-all-start.7) | async-done | bytes 129056 | tf_op jit(solution)/shard_map/all_to_all | solution.py:20
  374.2 0.8 copy.25
  375.0 0.8 copy.26
  375.8 0.8 copy.27
  (44 shorter events, 3.8 us)
Async XLA Ops:
  38.1 0.7 copy-start.5
  38.9 1.3 copy-start.6
  47.9 25.7 %all-to-all-start.1 = ((bf16[16,144,384]{2,1,0:T(8,128)(2,1)}), bf16[16,144,384]{2,1,0:T(8,128)(2,1)S(1)}, u32[]{:S(2)}, u32[]{:S(2)}) async-start(bf16[16,144,384]{2,1,0:T(8,128)(2,1)} %bitcast.8), calls=%async_computation.1 | async-start | bytes 3538944 | tf_op jit(solution)/shard_map/all_to_all | solution.py:20
  51.6 22.2 %copy-start.3 = (bf16[1,384,144]{1,2,0:T(8,128)(2,1)S(1)}, bf16[1,384,144]{1,2,0:T(8,128)(2,1)}, u32[]{:S(2)}) copy-start(bf16[1,384,144]{1,2,0:T(8,128)(2,1)} %param.8) | copy-start | bytes 331780
  51.6 72.7 %all-gather.6.cloned.1.call-start = ((), (), s32[]{:S(2)}) async-start(), calls=%async_computation.9 | async-start | bytes 1880064 | tf_op jit(solution)/shard_map/all_gather | solution.py:230
  75.6 48.7 %all-to-all-start.2 = ((bf16[16,64,1152]{2,1,0:T(8,128)(2,1)}), bf16[16,64,1152]{2,1,0:T(8,128)(2,1)S(1)}, u32[]{:S(2)}, u32[]{:S(2)}) async-start(bf16[16,64,1152]{2,1,0:T(8,128)(2,1)} %broadcast_in_dim.17), calls=%async_computation.2 | async-start | bytes 4718592 | tf_op jit(solution)/shard_map/all_to_all | solution.py:20
  124.3 1.4 copy-start
  125.8 23.3 %all-to-all-start.3 = ((bf16[16,144,384]{2,1,0:T(8,128)(2,1)}), bf16[16,144,384]{2,1,0:T(8,128)(2,1)S(1)}, u32[]{:S(2)}, u32[]{:S(2)}) async-start(bf16[16,144,384]{2,1,0:T(8,128)(2,1)} %bitcast.70), calls=%async_computation.3 | async-start | bytes 3538944 | tf_op jit(solution)/shard_map/all_to_all | solution.py:20
  132.3 103.4 %all-gather.4.cloned.1.call-start = ((), (), s32[]{:S(2)}) async-start(), calls=%async_computation.8 | async-start | bytes 1880064 | tf_op jit(solution)/shard_map/all_gather | solution.py:243
  132.4 19.3 %collective-permute-start = (bf16[1024,1152]{1,0:T(8,128)(2,1)}, bf16[1024,1152]{1,0:T(8,128)(2,1)}, u32[]{:S(2)}, u32[]{:S(2)}) collective-permute-start(bf16[1024,1152]{1,0:T(8,128)(2,1)} %bitcast.67), channel_id=1, source_target_pairs={{0,16},{16,0},{1,17},{17,1},{2,18},{18,2},{3,19},{19,3},{4,20},{20... | collective-permute-start | bytes 7077896 | tf_op jit(solution)/shard_map/ppermute | solution.py:272
  144.7 0.9 collective-permute-start.1
  145.6 0.6 copy-start.4
  151.2 1.7 copy-start.1
  314.1 27.0 %copy-start.7 = (s32[32]{0:T(128)S(1)}, s32[32]{0:T(128)}, u32[]{:S(2)}) copy-start(s32[32]{0:T(128)} %param.13) | copy-start | bytes 388
  333.4 19.2 %all-to-all-start.6 = ((f32[16,8,128]{2,1,0:T(8,128)}), f32[16,8,128]{2,1,0:T(8,128)S(1)}, u32[]{:S(2)}, u32[]{:S(2)}) async-start(f32[16,8,128]{2,1,0:T(8,128)} %broadcast_in_dim.39), calls=%async_computation.6 | async-start | bytes 131072 | tf_op jit(solution)/shard_map/all_to_all | solution.py:20
  352.6 0.6 copy-start.2
  357.8 16.3 %all-to-all-start.7 = ((bf16[16,56,72]{2,1,0:T(8,128)(2,1)}), bf16[16,56,72]{2,1,0:T(8,128)(2,1)S(1)}, u32[]{:S(2)}, u32[]{:S(2)}) async-start(bf16[16,56,72]{2,1,0:T(8,128)(2,1)} %get-tuple-element.18), calls=%async_computation.7 | async-start | bytes 458752 | tf_op jit(solution)/shard_map/all_to_all | solution.py:20
Sparse Core Ops, SparseCore 0:
  54.5 69.7 all-gather.5
  146.4 89.3 all-gather.3

commit v7 on v6

--- a/solution.py
+++ b/solution.py
@@ -155,6 +155,84 @@
         ),
         name="finish",
     )(parts, neighbours, owned)
+
+
+def down_kernel(hidden_ref, weight_ref, out_ref):
+    out_ref[...] = contract(weight_ref[...], hidden_ref[...], 0, 0).astype(out_ref.dtype)
+
+
+def project_down(hidden, weight):
+    units, tokens = hidden.shape
+    features = weight.shape[1]
+    chunks = 3
+    rows = features // chunks
+    return pl.pallas_call(
+        down_kernel,
+        grid=(chunks,),
+        in_specs=[
+            pl.BlockSpec((units, tokens), lambda chunk: (0, 0)),
+            pl.BlockSpec((units, rows), lambda chunk: (0, chunk)),
+        ],
+        out_specs=pl.BlockSpec((rows, tokens), lambda chunk: (chunk, 0)),
+        out_shape=jax.ShapeDtypeStruct((features, tokens), jnp.bfloat16),
+        cost_estimate=pl.CostEstimate(
+            flops=2 * units * tokens * features,
+            bytes_accessed=2 * (units * features + units * tokens + tokens * features),
+            transcendentals=0,
+        ),
+        name="project_down",
+    )(hidden, weight)
+
+
+def times_kernel(first, last, core_ref, own_ref, other_ref, near_ref, far_ref, out_ref):
+    slices, _, depth = own_ref.shape
+    step = pl.program_id(0)
+    flat = (slices * (last - first), depth)
+    total = contract(own_ref[:, first:last, :].reshape(flat), near_ref[...], 1, 0)
+    total += contract(other_ref[:, first:last, :].reshape(flat), far_ref[...], 1, 0)
+    total = total.reshape(out_ref.shape)
+
+    @pl.when(step == 0)
+    def _():
+        out_ref[...] = total
+
+    @pl.when(step > 0)
+    def _():
+        out_ref[...] += total
+
+
+def times_weights(core, own, other, rows, height, first, last):
+    slices, _, depth = own.shape
+    tokens = rows.shape[1]
+    pieces = other.shape[1] // height
+    weight_spec = pl.BlockSpec((slices, height, depth), lambda step, core_ref: (0, step, 0))
+    return pl.pallas_call(
+        lambda *refs: times_kernel(first, last, *refs),
+        grid_spec=pltpu.PrefetchScalarGridSpec(
+            num_scalar_prefetch=1,
+            grid=(pieces,),
+            in_specs=[
+                weight_spec,
+                weight_spec,
+                pl.BlockSpec(
+                    (depth, tokens), lambda step, core_ref: (core_ref[0] * pieces + step, 0)
+                ),
+                pl.BlockSpec(
+                    (depth, tokens), lambda step, core_ref: ((1 - core_ref[0]) * pieces + step, 0)
+                ),
+            ],
+            out_specs=pl.BlockSpec(
+                (slices, last - first, tokens), lambda step, core_ref: (0, 0, 0)
+            ),
+        ),
+        out_shape=jax.ShapeDtypeStruct((slices, last - first, tokens), jnp.float32),
+        cost_estimate=pl.CostEstimate(
+            flops=4 * slices * (last - first) * depth * pieces * tokens,
+            bytes_accessed=4 * slices * height * depth * pieces + 4 * depth * pieces * tokens,
+            transcendentals=0,
+        ),
+        name="times_weights",
+    )(core, own, other, rows, rows)
 
 
 def delta_kernel(ahead_ref, back_ref, normed_ref, residual_ref, out_ref):
@@ -233,7 +311,7 @@
     gate_value = contract(gate_weight, normed, 0, 0)
     up_value = contract(up_weight, normed, 0, 0)
     hidden = (gelu_tanh(gate_value) * up_value).astype(jnp.bfloat16)
-    partial_out = contract(down_weight, hidden, 0, 0).astype(jnp.bfloat16)
+    partial_out = project_down(hidden, down_weight)
     parts = exchange(
         partial_out.reshape(param_count, features // param_count, token_count), XY
     )
@@ -266,28 +344,25 @@
         ],
         axis=0,
     )
-    part, own_residual = lax.optimization_barrier((part, own_residual))
-    part = gather_rows(part, XY, param_count)
-    part, met_inputs = lax.optimization_barrier((part, met_inputs))
+    weight_rows = ahead_rows + back_rows
+    pieces = features // core_count // token_count
+    part = jnp.concatenate(jnp.split(part, pieces, axis=1), axis=0)
+    part, met_inputs, own_residual = lax.optimization_barrier((part, met_inputs, own_residual))
+    copies = jnp.broadcast_to(part[None], (param_count,) + part.shape)
+    both = exchange(jnp.concatenate([copies, met_inputs], axis=1), XY)
+    met_inputs = both[:, pieces * weight_rows :].reshape(features, token_count)
+    part = both[:, : pieces * weight_rows]
     other = lax.ppermute(part, "core", [(0, 1), (1, 0)])
-    met_inputs = exchange(met_inputs, XY).reshape(features, token_count)
-    low = lax.axis_index("core") == 0
-    met_weights = jnp.concatenate(
-        [jnp.where(low, part, other), jnp.where(low, other, part)], axis=1
-    ).reshape(param_count, ahead_rows + back_rows, features)
-    ahead_weights = met_weights[:, :ahead_rows].reshape(param_count * ahead_rows, features)
-    back_weights = met_weights[:, ahead_rows:].reshape(param_count * back_rows, features)
+    core = lax.axis_index("core").reshape(1)
     met_normed = rms_normed(met_inputs, norm_gain)
-    values = contract(ahead_weights, met_normed, 1, 0)
-    values, back_weights, met_residual = lax.optimization_barrier(
-        (values, back_weights, met_residual)
-    )
-    values = values.reshape(param_count, ahead_rows, token_count)
+    values = times_weights(core, both, other, met_normed, weight_rows, 0, ahead_rows)
+    values, met_residual = lax.optimization_barrier((values, met_residual))
     activated, gelu_back = jax.vjp(gelu_tanh, values[:, :share])
     up_value = values[:, share : 2 * share]
     hidden = (activated * up_value).astype(jnp.bfloat16)
-    back_hidden = contract(back_weights, met_residual, 1, 0)
-    back_hidden = back_hidden.reshape(param_count, back_rows, token_count)[:, :share]
+    back_hidden = times_weights(
+        core, both, other, met_residual, weight_rows, ahead_rows, weight_rows
+    )[:, :share]
     back_gate = gelu_back(back_hidden * up_value)[0].astype(jnp.bfloat16)
     back_up = (back_hidden * activated).astype(jnp.bfloat16)
 

time: 389 us -> 347 us (0.89)
  blocking collectives: 110 us -> 79.7 us
  waiting for transfers between devices: 165 us -> 137 us
  Pallas kernels: 16.7 us -> 31.7 us
  matrix products: 9.72 us -> 2.46 us
  other arithmetic: 10.2 us -> 15.4 us
    all_to_all x5, waiting for transfers between devices: 42 us -> 121 us  [exchange(): return lax.all_to_all(blocks, axes, split_axis=0, concat_axis=0, tiled=True)]
    all_gather x1, waiting for transfers between devices: 78.2 us -> 3.17 us  [on_device(): met_residual = lax.all_gather(met_residual, 'z', axis=0, tiled=True)]
    all_gather x1, waiting for transfers between devices: 43.7 us -> 11.8 us  [on_device(): met_inputs = lax.all_gather(own_inputs, 'z', axis=0, tiled=False)]
    all_to_all x3 -> x2, blocking collectives: 110 us -> 79.7 us  [exchange(): return lax.all_to_all(blocks, axes, split_axis=0, concat_axis=0, tiled=True)]
    pallas_call x0 -> x3, Pallas kernels: none -> 15 us  [the longest x2 10.7 us: times_weights(): pl.pallas_call(lambda *refs: times_kernel(first, last, *refs), grid_spec=...]
    dot_general x4 -> x2, matrix products: 9.72 us -> 2.46 us  [contract(): lax.dot_general(left, right, (((left_dim,), (right_dim,)), ((), ())), pre...]
    all_to_all x5, starting transfers between devices: 26.7 us -> 31.7 us  [exchange(): return lax.all_to_all(blocks, axes, split_axis=0, concat_axis=0, tiled=True)]
  transfers between devices with their start and end apart: 9 -> 9, of which waited for: 6 -> 7; matrix products, arithmetic and copies ran while one was open for 4% -> 6% of each run, Pallas kernels for 0% -> 3%
where the time goes in v7:
time: 347 us; the launch traced here: 342 us
  waiting for transfers between devices  137 us (39%)
  blocking collectives  79.7 us (23%)
  starting transfers between devices  43.4 us (13%)
  Pallas kernels  31.7 us (9%)
  local copies, waits for them, and re-layouts  17.9 us (5%)
  other arithmetic  15.4 us (4%)
  between operations  14.3 us (4%)
    all_to_all x5, waiting for transfers between devices, exchange(): return lax.all_to_all(blocks, axes, split_axis=0, concat_axis=0, tiled=True)  121 us
    all_to_all x2, blocking collectives, exchange(): return lax.all_to_all(blocks, axes, split_axis=0, concat_axis=0, tiled=True)  79.7 us
    all_to_all x5, starting transfers between devices, exchange(): return lax.all_to_all(blocks, axes, split_axis=0, concat_axis=0, tiled=True)  31.7 us
    all_gather x1, waiting for transfers between devices, on_device(): met_inputs = lax.all_gather(own_inputs, 'z', axis=0, tiled=False)  11.8 us
    ppermute x1, starting transfers between devices, on_device(): other = lax.ppermute(part, 'core', [(0, 1), (1, 0)])  11 us
    pallas_call x2, Pallas kernels, times_weights(): pl.pallas_call(lambda *refs: times_kernel(first, last, *refs), grid_spec=...  10.7 us
  transfers between devices with their start and end apart: 9, of which 7 were waited for; matrix products, arithmetic and copies ran while one was open for 6% of the time, Pallas kernels for 3%

profile of v7, /device:TPU:1, one launch (start us, length us, event | category | flops | bytes accessed | tf_op | source)
XLA Modules:
  0.0 341.6 jit_solution(13172712080621310548)
XLA Ops:
  7.2 2.4 broadcast_in_dim.14
  9.5 7.7 %all-to-all-start = ((bf16[16,144,384]{2,1,0:T(8,128)(2,1)}), bf16[16,144,384]{2,1,0:T(8,128)(2,1)S(1)}, u32[]{:S(2)}, u32[]{:S(2)}) async-start(bf16[16,144,384]{2,1,0:T(8,128)(2,1)} %broadcast_in_dim.14), calls=%async_computation | async-start | bytes 3538944 | tf_op jit(solution)/shard_map/all_to_all | solution.py:20
  17.3 0.7 all-gather.6.cloned.1.call-update
  18.0 21.3 %all-to-all-done = bf16[16,144,384]{2,1,0:T(8,128)(2,1)S(1)} async-done(((bf16[16,144,384]{2,1,0:T(8,128)(2,1)}), bf16[16,144,384]{2,1,0:T(8,128)(2,1)S(1)}, u32[]{:S(2)}, u32[]{:S(2)}) %all-to-all-start) | async-done | bytes 1769504 | tf_op jit(solution)/shard_map/all_to_all | solution.py:20
  40.6 0.9 fusion.19
  41.6 1.6 fusion.5.hidden_ref
  43.1 4.2 %project_down.1 = bf16[2304,384]{1,0:T(8,128)(2,1)} custom-call(bf16[288,384]{1,0:T(8,128)(2,1)} %fusion.5.hidden_ref, bf16[288,2304]{1,0:T(8,128)(2,1)} %weight_ref.1), custom_call_target="tpu_custom_call" | custom-call | flops 509607936 | bytes 3317760 | tf_op jit(solution)/shard_map/project_down/pallas_call | solution.py:169
  47.4 6.1 %all-to-all-start.1 = ((bf16[16,144,384]{2,1,0:T(8,128)(2,1)}), bf16[16,144,384]{2,1,0:T(8,128)(2,1)S(1)}, u32[]{:S(2)}, u32[]{:S(2)}) async-start(bf16[16,144,384]{2,1,0:T(8,128)(2,1)} %bitcast.56), calls=%async_computation.1 | async-start | bytes 3538944 | tf_op jit(solution)/shard_map/all_to_all | solution.py:20
  53.5 1.0 dynamic_slice.11
  54.7 1.0 dynamic-slice_bitcast_fusion.1
  55.6 0.6 broadcast_in_dim.13
  56.3 1.0 concatenate.15
  57.3 18.3 %all-to-all-done.1 = bf16[16,144,384]{2,1,0:T(8,128)(2,1)S(1)} async-done(((bf16[16,144,384]{2,1,0:T(8,128)(2,1)}), bf16[16,144,384]{2,1,0:T(8,128)(2,1)S(1)}, u32[]{:S(2)}, u32[]{:S(2)}) %all-to-all-start.1) | async-done | bytes 1769504 | tf_op jit(solution)/shard_map/all_to_all | solution.py:20
  75.9 11.8 %all-gather.6.cloned.1.call-done = bf16[2304,384]{1,0:T(8,128)(2,1)} async-done(((bf16[144,384]{1,0:T(8,128)(2,1)}), bf16[2304,384]{1,0:T(8,128)(2,1)}) %all-gather.6.cloned.1.call-update) | async-done | bytes 1769488 | tf_op jit(solution)/shard_map/all_gather | solution.py:308
  88.1 1.2 copy-done.2
  89.2 2.4 pad_maximum_fusion
  91.6 6.3 %all-to-all-start.2 = ((bf16[16,336,384]{2,1,0:T(8,128)(2,1)}), bf16[16,336,384]{2,1,0:T(8,128)(2,1)}, u32[]{:S(2)}, u32[]{:S(2)}) async-start(bf16[16,336,384]{2,1,0:T(8,128)(2,1)} %pad_maximum_fusion), calls=%async_computation.2 | async-start | bytes 8257536 | tf_op jit(solution)/shard_map/all_to_all | solution.py:20
  98.0 0.7 collective-permute-start.1
  98.7 0.6 copy-done.5
  99.3 60.7 %all-to-all-done.2.refs_1_ = bf16[16,336,384]{2,1,0:T(8,128)(2,1)} async-done(((bf16[16,336,384]{2,1,0:T(8,128)(2,1)}), bf16[16,336,384]{2,1,0:T(8,128)(2,1)}, u32[]{:S(2)}, u32[]{:S(2)}) %all-to-all-start.2) | async-done | bytes 4128800 | tf_op jit(solution)/shard_map/all_to_all | solution.py:20
  160.1 3.4 slice.32
  163.4 11.0 %collective-permute-start = (bf16[16,192,384]{2,1,0:T(8,128)(2,1)}, bf16[16,192,384]{2,1,0:T(8,128)(2,1)}, u32[]{:S(2)}, u32[]{:S(2)}) collective-permute-start(bf16[16,192,384]{2,1,0:T(8,128)(2,1)} %slice.32), channel_id=1, source_target_pairs={{0,16},{16,0},{1,17},{17,1},{2,18},{18,2},{3,19},{19,3},{4,20},{20... | collective-permute-start | bytes 7077896 | tf_op jit(solution)/shard_map/ppermute | solution.py:355
  174.6 1.9 multiply_reduce_fusion
  176.6 1.7 slice_convert_fusion
  178.3 1.6 multiply_convert_fusion.normed_ref
  179.9 1.7 fusion.1.refs_3_.refs_4_
  181.6 5.7 %times_weights.2 = f32[16,40,384]{2,1,0:T(8,128)} custom-call(s32[1]{0:T(128)} %bitcast.refs_0_, bf16[16,336,384]{2,1,0:T(8,128)(2,1)} %all-to-all-done.2.refs_1_, bf16[16,192,384]{2,1,0:T(8,128)(2,1)} %collective-permute-done.refs_2_, bf16[2304,384]{1,0:T(8,128)(2,1)} %fusion.1.refs_3_.refs_4_, bf16[2304,384]{1,0:T(8,128)(2,1)} %fusion.1.refs_3_.refs_4_), custom_call_target="tpu_custom_call" | custom-call | flops 1132462080 | bytes 6488064 | tf_op jit(solution)/shard_map/times_weights/pallas_call | solution.py:209
  187.3 3.2 all-gather.4.cloned.1.call-done.refs_3_.refs_4_
  190.5 5.0 %times_weights.3 = f32[16,24,384]{2,1,0:T(8,128)} custom-call(s32[1]{0:T(128)} %bitcast.refs_0_, bf16[16,336,384]{2,1,0:T(8,128)(2,1)} %all-to-all-done.2.refs_1_, bf16[16,192,384]{2,1,0:T(8,128)(2,1)} %collective-permute-done.refs_2_, bf16[2304,384]{1,0:T(8,128)(2,1)} %all-gather.4.cloned.1.call-done.refs_3_.refs_4_, ...), custom_call_target="tpu_custom_call" | custom-call | flops 679477248 | bytes 6488064 | tf_op jit(solution)/shard_map/times_weights/pallas_call | solution.py:209
  195.5 1.6 fusion.12
  197.1 0.9 pad_maximum_fusion.1.ahead_ref
  198.1 0.9 maximum_maximum_fusion.back_ref
  199.0 6.0 %make_deltas.1 = bf16[32,56,1152]{2,1,0:T(8,128)(2,1)} custom-call(bf16[16,40,384]{2,1,0:T(8,128)(2,1)} %pad_maximum_fusion.1.ahead_ref, bf16[16,24,384]{2,1,0:T(8,128)(2,1)} %maximum_maximum_fusion.back_ref, bf16[16,2,72,384]{3,2,1,0:T(8,128)(2,1)} %multiply_convert_fusion.normed_ref, bf16[16,2,72,384]{3,2,1,0:T(8,128)(2,1)} %bitcast.55), custom_call_target="tpu_custom_call" | custom-call | flops 1811939328 | bytes 7667712 | tf_op jit(solution)/shard_map/make_deltas/pallas_call | solution.py:264
  204.9 67.2 %all_to_all.35.block_ref.owned_ref = bf16[32,56,1152]{2,1,0:T(8,128)(2,1)} all-to-all(bf16[32,56,1152]{2,1,0:T(8,128)(2,1)} %make_deltas.1), channel_id=1, replica_groups=mesh['z'=16,'core'=2,'x'=4,'y'=4] {'core','x','y'}, dimensions={0} | all-to-all | bytes 8257536 | tf_op jit(solution)/shard_map/all_to_all | solution.py:20
  272.1 6.2 %pair_products.1 = f32[32,8,128]{2,1,0:T(8,128)} custom-call(bf16[32,56,1152]{2,1,0:T(8,128)(2,1)} %all_to_all.35.block_ref.owned_ref), custom_call_target="tpu_custom_call" | custom-call | flops 1056964608 | bytes 4128768 | tf_op jit(solution)/shard_map/pair_products/pallas_call | solution.py:77
  278.3 12.5 %all_to_all.36 = f32[32,8,128]{2,1,0:T(8,128)S(1)} all-to-all(f32[32,8,128]{2,1,0:T(8,128)} %pair_products.1), channel_id=1, replica_groups=mesh['z'=16,'core'=2,'x'=4,'y'=4] {'core','x','y'}, dimensions={0} | all-to-all | bytes 262144 | tf_op jit(solution)/shard_map/all_to_all | solution.py:20
  290.9 0.6 broadcast_in_dim.17
  291.5 7.8 %all-to-all-start.5 = ((f32[16,8,128]{2,1,0:T(8,128)}), f32[16,8,128]{2,1,0:T(8,128)S(1)}, u32[]{:S(2)}, u32[]{:S(2)}) async-start(f32[16,8,128]{2,1,0:T(8,128)} %broadcast_in_dim.17), calls=%async_computation.5 | async-start | bytes 131072 | tf_op jit(solution)/shard_map/all_to_all | solution.py:20
  299.5 0.6 reshape.83.neighbours_ref
  300.1 10.8 %all-to-all-done.5.parts_ref = f32[16,8,128]{2,1,0:T(8,128)S(1)} async-done(((f32[16,8,128]{2,1,0:T(8,128)}), f32[16,8,128]{2,1,0:T(8,128)S(1)}, u32[]{:S(2)}, u32[]{:S(2)}) %all-to-all-start.5) | async-done | bytes 65568 | tf_op jit(solution)/shard_map/all_to_all | solution.py:20
  310.9 0.6 copy-done.3
  311.5 4.5 %finish.1 = (bf16[16,56,72]{2,1,0:T(8,128)(2,1)}, f32[1,32]{1,0:T(1,128)}) custom-call(f32[16,8,128]{2,1,0:T(8,128)} %copy-done.3, s32[1,32]{1,0:T(1,128)} %reshape.83.neighbours_ref, bf16[32,56,1152]{2,1,0:T(8,128)(2,1)} %all_to_all.35.block_ref.owned_ref), custom_call_target="tpu_custom_call" | custom-call | flops 4128768 | bytes 4257792 | tf_op jit(solution)/shard_map/finish/pallas_call | solution.py:143
  316.0 3.8 %all-to-all-start.6 = ((bf16[16,56,72]{2,1,0:T(8,128)(2,1)}), bf16[16,56,72]{2,1,0:T(8,128)(2,1)S(1)}, u32[]{:S(2)}, u32[]{:S(2)}) async-start(bf16[16,56,72]{2,1,0:T(8,128)(2,1)} %get-tuple-element.14), calls=%async_computation.6 | async-start | bytes 458752 | tf_op jit(solution)/shard_map/all_to_all | solution.py:20
  320.3 1.3 reduce.5
  322.4 9.9 %all-to-all-done.6 = bf16[16,56,72]{2,1,0:T(8,128)(2,1)S(1)} async-done(((bf16[16,56,72]{2,1,0:T(8,128)(2,1)}), bf16[16,56,72]{2,1,0:T(8,128)(2,1)S(1)}, u32[]{:S(2)}, u32[]{:S(2)}) %all-to-all-start.6) | async-done | bytes 129056 | tf_op jit(solution)/shard_map/all_to_all | solution.py:20
  332.4 0.8 copy.18
  333.2 0.8 copy.19
  334.0 0.8 copy.20
  (46 shorter events, 3.9 us)
Async XLA Ops:
  7.2 34.4 %copy-start = (bf16[2304,288]{0,1:T(8,128)(2,1)S(1)}, bf16[2304,288]{0,1:T(8,128)(2,1)}, u32[]{:S(2)}) copy-start(bf16[2304,288]{0,1:T(8,128)(2,1)} %param.11) | copy-start | bytes 3981316
  9.5 30.2 %copy-start.6 = (f32[2304]{0:T(1024)S(1)}, f32[2304]{0:T(1024)}, u32[]{:S(2)}) copy-start(f32[2304]{0:T(1024)} %param.9) | copy-start | bytes 27652
  9.5 29.8 %all-to-all-start = ((bf16[16,144,384]{2,1,0:T(8,128)(2,1)}), bf16[16,144,384]{2,1,0:T(8,128)(2,1)S(1)}, u32[]{:S(2)}, u32[]{:S(2)}) async-start(bf16[16,144,384]{2,1,0:T(8,128)(2,1)} %broadcast_in_dim.14), calls=%async_computation | async-start | bytes 3538944 | tf_op jit(solution)/shard_map/all_to_all | solution.py:20
  17.2 70.5 %all-gather.6.cloned.1.call-start = ((), (), s32[]{:S(2)}) async-start(), calls=%async_computation.8 | async-start | bytes 1880064 | tf_op jit(solution)/shard_map/all_gather | solution.py:308
  39.3 1.3 copy-start.7
  47.4 28.3 %all-to-all-start.1 = ((bf16[16,144,384]{2,1,0:T(8,128)(2,1)}), bf16[16,144,384]{2,1,0:T(8,128)(2,1)S(1)}, u32[]{:S(2)}, u32[]{:S(2)}) async-start(bf16[16,144,384]{2,1,0:T(8,128)(2,1)} %bitcast.56), calls=%async_computation.1 | async-start | bytes 3538944 | tf_op jit(solution)/shard_map/all_to_all | solution.py:20
  53.5 22.4 %copy-start.4 = (bf16[1,384,144]{1,2,0:T(8,128)(2,1)S(1)}, bf16[1,384,144]{1,2,0:T(8,128)(2,1)}, u32[]{:S(2)}) copy-start(bf16[1,384,144]{1,2,0:T(8,128)(2,1)} %param.8) | copy-start | bytes 331780
  87.8 1.5 copy-start.2
  91.6 68.5 %all-to-all-start.2 = ((bf16[16,336,384]{2,1,0:T(8,128)(2,1)}), bf16[16,336,384]{2,1,0:T(8,128)(2,1)}, u32[]{:S(2)}, u32[]{:S(2)}) async-start(bf16[16,336,384]{2,1,0:T(8,128)(2,1)} %pad_maximum_fusion), calls=%async_computation.2 | async-start | bytes 8257536 | tf_op jit(solution)/shard_map/all_to_all | solution.py:20
  97.9 92.5 %all-gather.4.cloned.1.call-start = ((), (), s32[]{:S(2)}) async-start(), calls=%async_computation.7 | async-start | bytes 1880064 | tf_op jit(solution)/shard_map/all_gather | solution.py:321
  98.0 0.7 collective-permute-start.1
  98.7 0.6 copy-start.5
  163.4 18.1 %collective-permute-start = (bf16[16,192,384]{2,1,0:T(8,128)(2,1)}, bf16[16,192,384]{2,1,0:T(8,128)(2,1)}, u32[]{:S(2)}, u32[]{:S(2)}) collective-permute-start(bf16[16,192,384]{2,1,0:T(8,128)(2,1)} %slice.32), channel_id=1, source_target_pairs={{0,16},{16,0},{1,17},{17,1},{2,18},{18,2},{3,19},{19,3},{4,20},{20... | collective-permute-start | bytes 7077896 | tf_op jit(solution)/shard_map/ppermute | solution.py:355
  187.3 8.2 %copy-start.1 = (f32[16,40,384]{2,1,0:T(8,128)S(1)}, f32[16,40,384]{2,1,0:T(8,128)}, u32[]{:S(2)}) copy-start(f32[16,40,384]{2,1,0:T(8,128)} %times_weights.2) | copy-start | bytes 2949124
  272.1 27.1 %copy-start.8 = (s32[32]{0:T(128)S(1)}, s32[32]{0:T(128)}, u32[]{:S(2)}) copy-start(s32[32]{0:T(128)} %param.13) | copy-start | bytes 388
  291.5 19.3 %all-to-all-start.5 = ((f32[16,8,128]{2,1,0:T(8,128)}), f32[16,8,128]{2,1,0:T(8,128)S(1)}, u32[]{:S(2)}, u32[]{:S(2)}) async-start(f32[16,8,128]{2,1,0:T(8,128)} %broadcast_in_dim.17), calls=%async_computation.5 | async-start | bytes 131072 | tf_op jit(solution)/shard_map/all_to_all | solution.py:20
  310.8 0.6 copy-start.3
  316.0 16.3 %all-to-all-start.6 = ((bf16[16,56,72]{2,1,0:T(8,128)(2,1)}), bf16[16,56,72]{2,1,0:T(8,128)(2,1)S(1)}, u32[]{:S(2)}, u32[]{:S(2)}) async-start(bf16[16,56,72]{2,1,0:T(8,128)(2,1)} %get-tuple-element.14), calls=%async_computation.6 | async-start | bytes 458752 | tf_op jit(solution)/shard_map/all_to_all | solution.py:20
Sparse Core Ops, SparseCore 0:
  20.1 67.5 all-gather.5
  101.4 89.0 all-gather.3

commit v8 on v7

--- a/solution.py
+++ b/solution.py
@@ -45,43 +45,47 @@
 
 
 def gram_kernel(block_ref, copies_ref, total_ref):
-    clients, rows, columns = block_ref.shape
-    tall = 8
+    clients, tall, columns = block_ref.shape
     size = clients * tall
-    total_ref[...] = jnp.zeros_like(total_ref)
-
-    @pl.loop(0, rows // tall)
-    def _(index):
-        start = pl.multiple_of(index * tall, tall)
-        tile = block_ref[:, pl.ds(start, tall), :].reshape(size, columns)
-        total_ref[...] += contract(tile, tile, 1, 1)
-
-    row_index = lax.broadcasted_iota(jnp.int32, (size, size), 0)
-    col_index = lax.broadcasted_iota(jnp.int32, (size, size), 1)
-    kept = jnp.where(row_index % tall == col_index % tall, total_ref[...], 0.0)
-    pick_client = lax.broadcasted_iota(jnp.int32, (clients, size), 0)
-    pick_row = lax.broadcasted_iota(jnp.int32, (clients, size), 1) // tall
-    pick = (pick_row == pick_client).astype(jnp.float32)
-    gram = exact_dot(exact_dot(pick, kept, 1, 0), pick, 1, 1)
-    packed = jnp.zeros(copies_ref.shape[1:], jnp.float32)
-    for index in range(clients // tall):
-        packed += exact_dot(
-            gram[index * tall : (index + 1) * tall],
-            lane_place(index, clients, copies_ref.shape[2]), 1, 0,
-        )
-    copies_ref[...] = jnp.broadcast_to(packed[None], copies_ref.shape)
+    step = pl.program_id(0)
+    tile = block_ref[...].reshape(size, columns)
+
+    @pl.when(step == 0)
+    def _():
+        total_ref[...] = jnp.zeros_like(total_ref)
+
+    total_ref[...] += contract(tile, tile, 1, 1)
+
+    @pl.when(step == pl.num_programs(0) - 1)
+    def _():
+        row_index = lax.broadcasted_iota(jnp.int32, (size, size), 0)
+        col_index = lax.broadcasted_iota(jnp.int32, (size, size), 1)
+        kept = jnp.where(row_index % tall == col_index % tall, total_ref[...], 0.0)
+        pick_client = lax.broadcasted_iota(jnp.int32, (clients, size), 0)
+        pick_row = lax.broadcasted_iota(jnp.int32, (clients, size), 1) // tall
+        pick = (pick_row == pick_client).astype(jnp.float32)
+        gram = exact_dot(exact_dot(pick, kept, 1, 0), pick, 1, 1)
+        packed = jnp.zeros(copies_ref.shape[1:], jnp.float32)
+        for index in range(clients // tall):
+            packed += exact_dot(
+                gram[index * tall : (index + 1) * tall],
+                lane_place(index, clients, copies_ref.shape[2]), 1, 0,
+            )
+        copies_ref[...] = jnp.broadcast_to(packed[None], copies_ref.shape)
 
 
 def pair_products(exchanged, copies):
     clients, rows, columns = exchanged.shape
+    tall = 8
     return pl.pallas_call(
         gram_kernel,
+        grid=(rows // tall,),
+        in_specs=[pl.BlockSpec((clients, tall, columns), lambda step: (0, step, 0))],
+        out_specs=pl.BlockSpec((copies, 8, 128), lambda step: (0, 0, 0)),
         out_shape=jax.ShapeDtypeStruct((copies, 8, 128), jnp.float32),
-        in_specs=[pl.BlockSpec(memory_space=pltpu.VMEM)],
-        out_specs=pl.BlockSpec(memory_space=pltpu.VMEM),
-        scratch_shapes=[pltpu.VMEM((clients * 8, clients * 8), jnp.float32)],
+        scratch_shapes=[pltpu.VMEM((clients * tall, clients * tall), jnp.float32)],
         cost_estimate=pl.CostEstimate(
-            flops=2 * rows * clients * clients * 8 * columns,
+            flops=2 * rows * clients * clients * tall * columns,
             bytes_accessed=2 * clients * rows * columns,
             transcendentals=0,
         ),
@@ -184,12 +188,12 @@
     )(hidden, weight)
 
 
-def times_kernel(first, last, core_ref, own_ref, other_ref, near_ref, far_ref, out_ref):
-    slices, _, depth = own_ref.shape
+def times_kernel(core_ref, own_ref, other_ref, near_ref, far_ref, out_ref):
+    slices, height, depth = own_ref.shape
     step = pl.program_id(0)
-    flat = (slices * (last - first), depth)
-    total = contract(own_ref[:, first:last, :].reshape(flat), near_ref[...], 1, 0)
-    total += contract(other_ref[:, first:last, :].reshape(flat), far_ref[...], 1, 0)
+    flat = (slices * height, depth)
+    total = contract(own_ref[...].reshape(flat), near_ref[...], 1, 0)
+    total += contract(other_ref[...].reshape(flat), far_ref[...], 1, 0)
     total = total.reshape(out_ref.shape)
 
     @pl.when(step == 0)
@@ -201,13 +205,15 @@
         out_ref[...] += total
 
 
-def times_weights(core, own, other, rows, height, first, last):
+def times_weights(core, own, other, rows, pieces, start, height):
     slices, _, depth = own.shape
     tokens = rows.shape[1]
-    pieces = other.shape[1] // height
-    weight_spec = pl.BlockSpec((slices, height, depth), lambda step, core_ref: (0, step, 0))
+    if start % height:
+        raise ValueError("unaligned pieces")
+    first = start // height
+    weight_spec = pl.BlockSpec((slices, height, depth), lambda step, core_ref: (0, first + step, 0))
     return pl.pallas_call(
-        lambda *refs: times_kernel(first, last, *refs),
+        times_kernel,
         grid_spec=pltpu.PrefetchScalarGridSpec(
             num_scalar_prefetch=1,
             grid=(pieces,),
@@ -221,13 +227,11 @@
                     (depth, tokens), lambda step, core_ref: ((1 - core_ref[0]) * pieces + step, 0)
                 ),
             ],
-            out_specs=pl.BlockSpec(
-                (slices, last - first, tokens), lambda step, core_ref: (0, 0, 0)
-            ),
-        ),
-        out_shape=jax.ShapeDtypeStruct((slices, last - first, tokens), jnp.float32),
+            out_specs=pl.BlockSpec((slices, height, tokens), lambda step, core_ref: (0, 0, 0)),
+        ),
+        out_shape=jax.ShapeDtypeStruct((slices, height, tokens), jnp.float32),
         cost_estimate=pl.CostEstimate(
-            flops=4 * slices * (last - first) * depth * pieces * tokens,
+            flops=4 * slices * height * depth * pieces * tokens,
             bytes_accessed=4 * slices * height * depth * pieces + 4 * depth * pieces * tokens,
             transcendentals=0,
         ),
@@ -346,7 +350,10 @@
     )
     weight_rows = ahead_rows + back_rows
     pieces = features // core_count // token_count
-    part = jnp.concatenate(jnp.split(part, pieces, axis=1), axis=0)
+    part = jnp.concatenate(
+        jnp.split(part[:ahead_rows], pieces, axis=1) + jnp.split(part[ahead_rows:], pieces, axis=1),
+        axis=0,
+    )
     part, met_inputs, own_residual = lax.optimization_barrier((part, met_inputs, own_residual))
     copies = jnp.broadcast_to(part[None], (param_count,) + part.shape)
     both = exchange(jnp.concatenate([copies, met_inputs], axis=1), XY)
@@ -355,13 +362,13 @@
     other = lax.ppermute(part, "core", [(0, 1), (1, 0)])
     core = lax.axis_index("core").reshape(1)
     met_normed = rms_normed(met_inputs, norm_gain)
-    values = times_weights(core, both, other, met_normed, weight_rows, 0, ahead_rows)
+    values = times_weights(core, both, other, met_normed, pieces, 0, ahead_rows)
     values, met_residual = lax.optimization_barrier((values, met_residual))
     activated, gelu_back = jax.vjp(gelu_tanh, values[:, :share])
     up_value = values[:, share : 2 * share]
     hidden = (activated * up_value).astype(jnp.bfloat16)
     back_hidden = times_weights(
-        core, both, other, met_residual, weight_rows, ahead_rows, weight_rows
+        core, both, other, met_residual, pieces, pieces * ahead_rows, back_rows
     )[:, :share]
     back_gate = gelu_back(back_hidden * up_value)[0].astype(jnp.bfloat16)
     back_up = (back_hidden * activated).astype(jnp.bfloat16)

time: 347 us -> 348 us (level)
  no operation moved by 1% of the time
where the time goes in v8:
time: 348 us; the launch traced here: 342 us
  waiting for transfers between devices  139 us (40%)
  blocking collectives  79.3 us (23%)
  starting transfers between devices  43.6 us (13%)
  Pallas kernels  31.8 us (9%)
  local copies, waits for them, and re-layouts  16.4 us (5%)
  other arithmetic  15.4 us (4%)
  between operations  14.3 us (4%)
    all_to_all x5, waiting for transfers between devices, exchange(): return lax.all_to_all(blocks, axes, split_axis=0, concat_axis=0, tiled=True)  123 us
    all_to_all x2, blocking collectives, exchange(): return lax.all_to_all(blocks, axes, split_axis=0, concat_axis=0, tiled=True)  79.3 us
    all_to_all x5, starting transfers between devices, exchange(): return lax.all_to_all(blocks, axes, split_axis=0, concat_axis=0, tiled=True)  31.9 us
    all_gather x1, waiting for transfers between devices, on_device(): met_inputs = lax.all_gather(own_inputs, 'z', axis=0, tiled=False)  11.7 us
    ppermute x1, starting transfers between devices, on_device(): other = lax.ppermute(part, 'core', [(0, 1), (1, 0)])  11 us
    pallas_call x2, Pallas kernels, times_weights(): pl.pallas_call(times_kernel, grid_spec=pltpu.PrefetchScalarGridSpec(num_s...  9.74 us
    pallas_call x1, Pallas kernels, pair_products(): pl.pallas_call(gram_kernel, grid=(rows // tall,), in_specs=[pl.BlockSpec(...  7.38 us
  transfers between devices with their start and end apart: 9, of which 7 were waited for; matrix products, arithmetic and copies ran while one was open for 6% of the time, Pallas kernels for 3%

profile of v8, /device:TPU:1, one launch (start us, length us, event | category | flops | bytes accessed | tf_op | source)
XLA Modules:
  0.0 342.3 jit_solution(3648790461690860219)
XLA Ops:
  7.2 2.4 broadcast_in_dim.11
  9.5 7.7 %all-to-all-start = ((bf16[16,144,384]{2,1,0:T(8,128)(2,1)}), bf16[16,144,384]{2,1,0:T(8,128)(2,1)S(1)}, u32[]{:S(2)}, u32[]{:S(2)}) async-start(bf16[16,144,384]{2,1,0:T(8,128)(2,1)} %broadcast_in_dim.11), calls=%async_computation | async-start | bytes 3538944 | tf_op jit(solution)/shard_map/all_to_all | solution.py:20
  17.3 0.7 all-gather.6.cloned.1.call-update
  18.1 1.0 dynamic_slice.11
  19.2 20.1 %all-to-all-done = bf16[16,144,384]{2,1,0:T(8,128)(2,1)S(1)} async-done(((bf16[16,144,384]{2,1,0:T(8,128)(2,1)}), bf16[16,144,384]{2,1,0:T(8,128)(2,1)S(1)}, u32[]{:S(2)}, u32[]{:S(2)}) %all-to-all-start) | async-done | bytes 1769504 | tf_op jit(solution)/shard_map/all_to_all | solution.py:20
  40.6 0.9 fusion.19
  41.6 1.5 fusion.5.hidden_ref
  43.1 4.2 %project_down.1 = bf16[2304,384]{1,0:T(8,128)(2,1)} custom-call(bf16[288,384]{1,0:T(8,128)(2,1)} %fusion.5.hidden_ref, bf16[288,2304]{1,0:T(8,128)(2,1)} %weight_ref.1), custom_call_target="tpu_custom_call" | custom-call | flops 509607936 | bytes 3317760 | tf_op jit(solution)/shard_map/project_down/pallas_call | solution.py:173
  47.3 6.3 %all-to-all-start.1 = ((bf16[16,144,384]{2,1,0:T(8,128)(2,1)}), bf16[16,144,384]{2,1,0:T(8,128)(2,1)S(1)}, u32[]{:S(2)}, u32[]{:S(2)}) async-start(bf16[16,144,384]{2,1,0:T(8,128)(2,1)} %bitcast.56), calls=%async_computation.1 | async-start | bytes 3538944 | tf_op jit(solution)/shard_map/all_to_all | solution.py:20
  53.6 1.0 dynamic-slice_bitcast_fusion.1
  54.8 21.0 %all-to-all-done.1 = bf16[16,144,384]{2,1,0:T(8,128)(2,1)S(1)} async-done(((bf16[16,144,384]{2,1,0:T(8,128)(2,1)}), bf16[16,144,384]{2,1,0:T(8,128)(2,1)S(1)}, u32[]{:S(2)}, u32[]{:S(2)}) %all-to-all-start.1) | async-done | bytes 1769504 | tf_op jit(solution)/shard_map/all_to_all | solution.py:20
  76.0 11.7 %all-gather.6.cloned.1.call-done = bf16[2304,384]{1,0:T(8,128)(2,1)} async-done(((bf16[144,384]{1,0:T(8,128)(2,1)}), bf16[2304,384]{1,0:T(8,128)(2,1)}) %all-gather.6.cloned.1.call-update) | async-done | bytes 1769488 | tf_op jit(solution)/shard_map/all_gather | solution.py:312
  88.1 1.2 copy-done.2
  89.2 2.4 pad_maximum_fusion
  91.6 6.3 %all-to-all-start.2 = ((bf16[16,336,384]{2,1,0:T(8,128)(2,1)}), bf16[16,336,384]{2,1,0:T(8,128)(2,1)}, u32[]{:S(2)}, u32[]{:S(2)}) async-start(bf16[16,336,384]{2,1,0:T(8,128)(2,1)} %pad_maximum_fusion), calls=%async_computation.2 | async-start | bytes 8257536 | tf_op jit(solution)/shard_map/all_to_all | solution.py:20
  98.0 0.7 collective-permute-start.1
  98.7 0.6 copy-done.5
  99.4 60.7 %all-to-all-done.2.own_ref = bf16[16,336,384]{2,1,0:T(8,128)(2,1)} async-done(((bf16[16,336,384]{2,1,0:T(8,128)(2,1)}), bf16[16,336,384]{2,1,0:T(8,128)(2,1)}, u32[]{:S(2)}, u32[]{:S(2)}) %all-to-all-start.2) | async-done | bytes 4128800 | tf_op jit(solution)/shard_map/all_to_all | solution.py:20
  160.1 3.4 slice.38
  163.5 11.0 %collective-permute-start = (bf16[16,192,384]{2,1,0:T(8,128)(2,1)}, bf16[16,192,384]{2,1,0:T(8,128)(2,1)}, u32[]{:S(2)}, u32[]{:S(2)}) collective-permute-start(bf16[16,192,384]{2,1,0:T(8,128)(2,1)} %slice.38), channel_id=1, source_target_pairs={{0,16},{16,0},{1,17},{17,1},{2,18},{18,2},{3,19},{19,3},{4,20},{20... | collective-permute-start | bytes 7077896 | tf_op jit(solution)/shard_map/ppermute | solution.py:362
  174.6 1.9 multiply_reduce_fusion
  176.6 1.7 slice_convert_fusion
  178.3 1.6 multiply_convert_fusion.normed_ref
  180.0 1.6 fusion.1.near_ref.far_ref
  181.6 5.3 %times_weights.2 = f32[16,40,384]{2,1,0:T(8,128)} custom-call(s32[1]{0:T(128)} %bitcast.core_ref, bf16[16,336,384]{2,1,0:T(8,128)(2,1)} %all-to-all-done.2.own_ref, bf16[16,192,384]{2,1,0:T(8,128)(2,1)} %collective-permute-done.other_ref, bf16[2304,384]{1,0:T(8,128)(2,1)} %fusion.1.near_ref.far_ref, bf16[2304,384]{1,0:T(8,128)(2,1)} %fusion.1.near_ref.far_ref), custom_call_target="tpu_custom_call" | custom-call | flops 1132462080 | bytes 4718592 | tf_op jit(solution)/shard_map/times_weights/pallas_call | solution.py:215
  187.0 4.1 %all-gather.4.cloned.1.call-done.near_ref.far_ref = bf16[2304,384]{1,0:T(8,128)(2,1)} async-done(((bf16[144,384]{1,0:T(8,128)(2,1)}), bf16[2304,384]{1,0:T(8,128)(2,1)}) %all-gather.4.cloned.1.call-update) | async-done | bytes 1769488 | tf_op jit(solution)/shard_map/all_gather | solution.py:325
  191.1 4.4 %times_weights.3 = f32[16,24,384]{2,1,0:T(8,128)} custom-call(s32[1]{0:T(128)} %bitcast.core_ref, bf16[16,336,384]{2,1,0:T(8,128)(2,1)} %all-to-all-done.2.own_ref, bf16[16,192,384]{2,1,0:T(8,128)(2,1)} %collective-permute-done.other_ref, bf16[2304,384]{1,0:T(8,128)(2,1)} %all-gather.4.cloned.1.call-done.near_ref.far_ref, ...), custom_call_target="tpu_custom_call" | custom-call | flops 679477248 | bytes 3538944 | tf_op jit(solution)/shard_map/times_weights/pallas_call | solution.py:215
  195.5 1.6 fusion.12
  197.1 0.9 pad_maximum_fusion.1.ahead_ref
  198.1 0.9 maximum_maximum_fusion.back_ref
  199.0 6.0 %make_deltas.1 = bf16[32,56,1152]{2,1,0:T(8,128)(2,1)} custom-call(bf16[16,40,384]{2,1,0:T(8,128)(2,1)} %pad_maximum_fusion.1.ahead_ref, bf16[16,24,384]{2,1,0:T(8,128)(2,1)} %maximum_maximum_fusion.back_ref, bf16[16,2,72,384]{3,2,1,0:T(8,128)(2,1)} %multiply_convert_fusion.normed_ref, bf16[16,2,72,384]{3,2,1,0:T(8,128)(2,1)} %bitcast.55), custom_call_target="tpu_custom_call" | custom-call | flops 1811939328 | bytes 7667712 | tf_op jit(solution)/shard_map/make_deltas/pallas_call | solution.py:268
  204.9 66.6 %all_to_all.35.block_ref.owned_ref = bf16[32,56,1152]{2,1,0:T(8,128)(2,1)} all-to-all(bf16[32,56,1152]{2,1,0:T(8,128)(2,1)} %make_deltas.1), channel_id=1, replica_groups=mesh['z'=16,'core'=2,'x'=4,'y'=4] {'core','x','y'}, dimensions={0} | all-to-all | bytes 8257536 | tf_op jit(solution)/shard_map/all_to_all | solution.py:20
  271.5 7.4 %pair_products.1 = f32[32,8,128]{2,1,0:T(8,128)} custom-call(bf16[32,56,1152]{2,1,0:T(8,128)(2,1)} %all_to_all.35.block_ref.owned_ref), custom_call_target="tpu_custom_call" | custom-call | flops 1056964608 | bytes 4128768 | tf_op jit(solution)/shard_map/pair_products/pallas_call | solution.py:80
  278.9 12.7 %all_to_all.36 = f32[32,8,128]{2,1,0:T(8,128)S(1)} all-to-all(f32[32,8,128]{2,1,0:T(8,128)} %pair_products.1), channel_id=1, replica_groups=mesh['z'=16,'core'=2,'x'=4,'y'=4] {'core','x','y'}, dimensions={0} | all-to-all | bytes 262144 | tf_op jit(solution)/shard_map/all_to_all | solution.py:20
  291.6 0.6 broadcast_in_dim.14
  292.3 7.8 %all-to-all-start.5 = ((f32[16,8,128]{2,1,0:T(8,128)}), f32[16,8,128]{2,1,0:T(8,128)S(1)}, u32[]{:S(2)}, u32[]{:S(2)}) async-start(f32[16,8,128]{2,1,0:T(8,128)} %broadcast_in_dim.14), calls=%async_computation.5 | async-start | bytes 131072 | tf_op jit(solution)/shard_map/all_to_all | solution.py:20
  300.2 0.6 reshape.83.neighbours_ref
  300.8 10.8 %all-to-all-done.5.parts_ref = f32[16,8,128]{2,1,0:T(8,128)S(1)} async-done(((f32[16,8,128]{2,1,0:T(8,128)}), f32[16,8,128]{2,1,0:T(8,128)S(1)}, u32[]{:S(2)}, u32[]{:S(2)}) %all-to-all-start.5) | async-done | bytes 65568 | tf_op jit(solution)/shard_map/all_to_all | solution.py:20
  311.6 0.6 copy-done.3
  312.2 4.5 %finish.1 = (bf16[16,56,72]{2,1,0:T(8,128)(2,1)}, f32[1,32]{1,0:T(1,128)}) custom-call(f32[16,8,128]{2,1,0:T(8,128)} %copy-done.3, s32[1,32]{1,0:T(1,128)} %reshape.83.neighbours_ref, bf16[32,56,1152]{2,1,0:T(8,128)(2,1)} %all_to_all.35.block_ref.owned_ref), custom_call_target="tpu_custom_call" | custom-call | flops 4128768 | bytes 4257792 | tf_op jit(solution)/shard_map/finish/pallas_call | solution.py:147
  316.7 3.8 %all-to-all-start.6 = ((bf16[16,56,72]{2,1,0:T(8,128)(2,1)}), bf16[16,56,72]{2,1,0:T(8,128)(2,1)S(1)}, u32[]{:S(2)}, u32[]{:S(2)}) async-start(bf16[16,56,72]{2,1,0:T(8,128)(2,1)} %get-tuple-element.14), calls=%async_computation.6 | async-start | bytes 458752 | tf_op jit(solution)/shard_map/all_to_all | solution.py:20
  320.5 0.5 broadcast.98
  321.1 1.3 reduce.5
  322.5 0.6 reshape.88
  323.2 9.9 %all-to-all-done.6 = bf16[16,56,72]{2,1,0:T(8,128)(2,1)S(1)} async-done(((bf16[16,56,72]{2,1,0:T(8,128)(2,1)}), bf16[16,56,72]{2,1,0:T(8,128)(2,1)S(1)}, u32[]{:S(2)}, u32[]{:S(2)}) %all-to-all-start.6) | async-done | bytes 129056 | tf_op jit(solution)/shard_map/all_to_all | solution.py:20
  333.1 0.8 copy.18
  333.9 0.8 copy.19
  334.7 0.8 copy.20
  (50 shorter events, 3.0 us)
Async XLA Ops:
  7.2 11.9 %copy-start = (bf16[2304,288]{0,1:T(8,128)(2,1)S(1)}, bf16[2304,288]{0,1:T(8,128)(2,1)}, u32[]{:S(2)}) copy-start(bf16[2304,288]{0,1:T(8,128)(2,1)} %param.11) | copy-start | bytes 3981316
  9.5 30.2 %copy-start.6 = (f32[2304]{0:T(1024)S(1)}, f32[2304]{0:T(1024)}, u32[]{:S(2)}) copy-start(f32[2304]{0:T(1024)} %param.9) | copy-start | bytes 27652
  9.5 29.8 %all-to-all-start = ((bf16[16,144,384]{2,1,0:T(8,128)(2,1)}), bf16[16,144,384]{2,1,0:T(8,128)(2,1)S(1)}, u32[]{:S(2)}, u32[]{:S(2)}) async-start(bf16[16,144,384]{2,1,0:T(8,128)(2,1)} %broadcast_in_dim.11), calls=%async_computation | async-start | bytes 3538944 | tf_op jit(solution)/shard_map/all_to_all | solution.py:20
  17.3 70.5 %all-gather.6.cloned.1.call-start = ((), (), s32[]{:S(2)}) async-start(), calls=%async_computation.8 | async-start | bytes 1880064 | tf_op jit(solution)/shard_map/all_gather | solution.py:312
  39.3 1.3 copy-start.7
  47.3 28.7 %copy-start.4 = (bf16[1,384,144]{1,2,0:T(8,128)(2,1)S(1)}, bf16[1,384,144]{1,2,0:T(8,128)(2,1)}, u32[]{:S(2)}) copy-start(bf16[1,384,144]{1,2,0:T(8,128)(2,1)} %param.8) | copy-start | bytes 331780
  47.3 28.4 %all-to-all-start.1 = ((bf16[16,144,384]{2,1,0:T(8,128)(2,1)}), bf16[16,144,384]{2,1,0:T(8,128)(2,1)S(1)}, u32[]{:S(2)}, u32[]{:S(2)}) async-start(bf16[16,144,384]{2,1,0:T(8,128)(2,1)} %bitcast.56), calls=%async_computation.1 | async-start | bytes 3538944 | tf_op jit(solution)/shard_map/all_to_all | solution.py:20
  87.8 1.5 copy-start.2
  91.6 68.5 %all-to-all-start.2 = ((bf16[16,336,384]{2,1,0:T(8,128)(2,1)}), bf16[16,336,384]{2,1,0:T(8,128)(2,1)}, u32[]{:S(2)}, u32[]{:S(2)}) async-start(bf16[16,336,384]{2,1,0:T(8,128)(2,1)} %pad_maximum_fusion), calls=%async_computation.2 | async-start | bytes 8257536 | tf_op jit(solution)/shard_map/all_to_all | solution.py:20
  98.0 93.1 %all-gather.4.cloned.1.call-start = ((), (), s32[]{:S(2)}) async-start(), calls=%async_computation.7 | async-start | bytes 1880064 | tf_op jit(solution)/shard_map/all_gather | solution.py:325
  98.0 0.7 collective-permute-start.1
  98.7 0.6 copy-start.5
  163.5 18.1 %collective-permute-start = (bf16[16,192,384]{2,1,0:T(8,128)(2,1)}, bf16[16,192,384]{2,1,0:T(8,128)(2,1)}, u32[]{:S(2)}, u32[]{:S(2)}) collective-permute-start(bf16[16,192,384]{2,1,0:T(8,128)(2,1)} %slice.38), channel_id=1, source_target_pairs={{0,16},{16,0},{1,17},{17,1},{2,18},{18,2},{3,19},{19,3},{4,20},{20... | collective-permute-start | bytes 7077896 | tf_op jit(solution)/shard_map/ppermute | solution.py:362
  187.0 8.5 %copy-start.1 = (f32[16,40,384]{2,1,0:T(8,128)S(1)}, f32[16,40,384]{2,1,0:T(8,128)}, u32[]{:S(2)}) copy-start(f32[16,40,384]{2,1,0:T(8,128)} %times_weights.2) | copy-start | bytes 2949124
  271.5 28.5 %copy-start.8 = (s32[32]{0:T(128)S(1)}, s32[32]{0:T(128)}, u32[]{:S(2)}) copy-start(s32[32]{0:T(128)} %param.13) | copy-start | bytes 388
  292.3 19.3 %all-to-all-start.5 = ((f32[16,8,128]{2,1,0:T(8,128)}), f32[16,8,128]{2,1,0:T(8,128)S(1)}, u32[]{:S(2)}, u32[]{:S(2)}) async-start(f32[16,8,128]{2,1,0:T(8,128)} %broadcast_in_dim.14), calls=%async_computation.5 | async-start | bytes 131072 | tf_op jit(solution)/shard_map/all_to_all | solution.py:20
  311.6 0.6 copy-start.3
  316.7 16.3 %all-to-all-start.6 = ((bf16[16,56,72]{2,1,0:T(8,128)(2,1)}), bf16[16,56,72]{2,1,0:T(8,128)(2,1)S(1)}, u32[]{:S(2)}, u32[]{:S(2)}) async-start(bf16[16,56,72]{2,1,0:T(8,128)(2,1)} %get-tuple-element.14), calls=%async_computation.6 | async-start | bytes 458752 | tf_op jit(solution)/shard_map/all_to_all | solution.py:20
Sparse Core Ops, SparseCore 0:
  20.1 67.5 all-gather.5
  101.4 89.6 all-gather.3

commit v9 on v7

--- a/solution.py
+++ b/solution.py
@@ -184,12 +184,12 @@
     )(hidden, weight)
 
 
-def times_kernel(first, last, core_ref, own_ref, other_ref, near_ref, far_ref, out_ref):
-    slices, _, depth = own_ref.shape
+def times_kernel(core_ref, own_ref, other_ref, near_ref, far_ref, out_ref):
+    slices, height, depth = own_ref.shape
     step = pl.program_id(0)
-    flat = (slices * (last - first), depth)
-    total = contract(own_ref[:, first:last, :].reshape(flat), near_ref[...], 1, 0)
-    total += contract(other_ref[:, first:last, :].reshape(flat), far_ref[...], 1, 0)
+    flat = (slices * height, depth)
+    total = contract(own_ref[...].reshape(flat), near_ref[...], 1, 0)
+    total += contract(other_ref[...].reshape(flat), far_ref[...], 1, 0)
     total = total.reshape(out_ref.shape)
 
     @pl.when(step == 0)
@@ -201,13 +201,15 @@
         out_ref[...] += total
 
 
-def times_weights(core, own, other, rows, height, first, last):
+def times_weights(core, own, other, rows, pieces, start, height):
     slices, _, depth = own.shape
     tokens = rows.shape[1]
-    pieces = other.shape[1] // height
-    weight_spec = pl.BlockSpec((slices, height, depth), lambda step, core_ref: (0, step, 0))
+    if start % height:
+        raise ValueError("unaligned pieces")
+    first = start // height
+    weight_spec = pl.BlockSpec((slices, height, depth), lambda step, core_ref: (0, first + step, 0))
     return pl.pallas_call(
-        lambda *refs: times_kernel(first, last, *refs),
+        times_kernel,
         grid_spec=pltpu.PrefetchScalarGridSpec(
             num_scalar_prefetch=1,
             grid=(pieces,),
@@ -221,13 +223,11 @@
                     (depth, tokens), lambda step, core_ref: ((1 - core_ref[0]) * pieces + step, 0)
                 ),
             ],
-            out_specs=pl.BlockSpec(
-                (slices, last - first, tokens), lambda step, core_ref: (0, 0, 0)
-            ),
-        ),
-        out_shape=jax.ShapeDtypeStruct((slices, last - first, tokens), jnp.float32),
+            out_specs=pl.BlockSpec((slices, height, tokens), lambda step, core_ref: (0, 0, 0)),
+        ),
+        out_shape=jax.ShapeDtypeStruct((slices, height, tokens), jnp.float32),
         cost_estimate=pl.CostEstimate(
-            flops=4 * slices * (last - first) * depth * pieces * tokens,
+            flops=4 * slices * height * depth * pieces * tokens,
             bytes_accessed=4 * slices * height * depth * pieces + 4 * depth * pieces * tokens,
             transcendentals=0,
         ),
@@ -346,7 +346,10 @@
     )
     weight_rows = ahead_rows + back_rows
     pieces = features // core_count // token_count
-    part = jnp.concatenate(jnp.split(part, pieces, axis=1), axis=0)
+    part = jnp.concatenate(
+        jnp.split(part[:ahead_rows], pieces, axis=1) + jnp.split(part[ahead_rows:], pieces, axis=1),
+        axis=0,
+    )
     part, met_inputs, own_residual = lax.optimization_barrier((part, met_inputs, own_residual))
     copies = jnp.broadcast_to(part[None], (param_count,) + part.shape)
     both = exchange(jnp.concatenate([copies, met_inputs], axis=1), XY)
@@ -354,14 +357,14 @@
     part = both[:, : pieces * weight_rows]
     other = lax.ppermute(part, "core", [(0, 1), (1, 0)])
     core = lax.axis_index("core").reshape(1)
-    met_normed = rms_normed(met_inputs, norm_gain)
-    values = times_weights(core, both, other, met_normed, weight_rows, 0, ahead_rows)
+    met_normed = lax.optimization_barrier(rms_normed(met_inputs, norm_gain))
+    values = times_weights(core, both, other, met_normed, pieces, 0, ahead_rows)
     values, met_residual = lax.optimization_barrier((values, met_residual))
     activated, gelu_back = jax.vjp(gelu_tanh, values[:, :share])
     up_value = values[:, share : 2 * share]
     hidden = (activated * up_value).astype(jnp.bfloat16)
     back_hidden = times_weights(
-        core, both, other, met_residual, weight_rows, ahead_rows, weight_rows
+        core, both, other, met_residual, pieces, pieces * ahead_rows, back_rows
     )[:, :share]
     back_gate = gelu_back(back_hidden * up_value)[0].astype(jnp.bfloat16)
     back_up = (back_hidden * activated).astype(jnp.bfloat16)

time: 347 us -> 347 us (level)
  waiting for transfers between devices: 137 us -> 142 us
    all_gather x1, waiting for transfers between devices: 3.17 us -> 6.98 us  [on_device(): met_residual = lax.all_gather(met_residual, 'z', axis=0, tiled=True)]
  transfers between devices with their start and end apart: 9 -> 9, of which waited for: 7 -> 7; matrix products, arithmetic and copies ran while one was open for 6% -> 5% of each run, Pallas kernels for 3% -> 3%
where the time goes in v9:
time: 347 us; the launch traced here: 341 us
  waiting for transfers between devices  142 us (41%)
  blocking collectives  79.5 us (23%)
  starting transfers between devices  43.6 us (13%)
  Pallas kernels  30.6 us (9%)
  local copies, waits for them, and re-layouts  14.8 us (4%)
  between operations  14.3 us (4%)
  other arithmetic  13.8 us (4%)
    all_to_all x5, waiting for transfers between devices, exchange(): return lax.all_to_all(blocks, axes, split_axis=0, concat_axis=0, tiled=True)  122 us
    all_to_all x2, blocking collectives, exchange(): return lax.all_to_all(blocks, axes, split_axis=0, concat_axis=0, tiled=True)  79.5 us
    all_to_all x5, starting transfers between devices, exchange(): return lax.all_to_all(blocks, axes, split_axis=0, concat_axis=0, tiled=True)  31.8 us
    all_gather x1, waiting for transfers between devices, on_device(): met_inputs = lax.all_gather(own_inputs, 'z', axis=0, tiled=False)  11.7 us
    ppermute x1, starting transfers between devices, on_device(): other = lax.ppermute(part, 'core', [(0, 1), (1, 0)])  11 us
    pallas_call x2, Pallas kernels, times_weights(): pl.pallas_call(times_kernel, grid_spec=pltpu.PrefetchScalarGridSpec(num_s...  9.73 us
    all_gather x1, waiting for transfers between devices, on_device(): met_residual = lax.all_gather(met_residual, 'z', axis=0, tiled=True)  6.98 us
  transfers between devices with their start and end apart: 9, of which 7 were waited for; matrix products, arithmetic and copies ran while one was open for 5% of the time, Pallas kernels for 3%

profile of v9, /device:TPU:1, one launch (start us, length us, event | category | flops | bytes accessed | tf_op | source)
XLA Modules:
  0.0 340.9 jit_solution(3057420467869831291)
XLA Ops:
  7.2 2.4 broadcast_in_dim.11
  9.5 7.7 %all-to-all-start = ((bf16[16,144,384]{2,1,0:T(8,128)(2,1)}), bf16[16,144,384]{2,1,0:T(8,128)(2,1)S(1)}, u32[]{:S(2)}, u32[]{:S(2)}) async-start(bf16[16,144,384]{2,1,0:T(8,128)(2,1)} %broadcast_in_dim.11), calls=%async_computation | async-start | bytes 3538944 | tf_op jit(solution)/shard_map/all_to_all | solution.py:20
  17.3 0.7 all-gather.6.cloned.1.call-update
  18.1 1.0 dynamic_slice.11
  19.2 20.1 %all-to-all-done = bf16[16,144,384]{2,1,0:T(8,128)(2,1)S(1)} async-done(((bf16[16,144,384]{2,1,0:T(8,128)(2,1)}), bf16[16,144,384]{2,1,0:T(8,128)(2,1)S(1)}, u32[]{:S(2)}, u32[]{:S(2)}) %all-to-all-start) | async-done | bytes 1769504 | tf_op jit(solution)/shard_map/all_to_all | solution.py:20
  39.8 0.5 fusion.3
  40.6 0.9 fusion.19
  41.6 1.5 fusion.5.hidden_ref
  43.1 4.2 %project_down.1 = bf16[2304,384]{1,0:T(8,128)(2,1)} custom-call(bf16[288,384]{1,0:T(8,128)(2,1)} %fusion.5.hidden_ref, bf16[288,2304]{1,0:T(8,128)(2,1)} %weight_ref.1), custom_call_target="tpu_custom_call" | custom-call | flops 509607936 | bytes 3317760 | tf_op jit(solution)/shard_map/project_down/pallas_call | solution.py:169
  47.3 6.3 %all-to-all-start.1 = ((bf16[16,144,384]{2,1,0:T(8,128)(2,1)}), bf16[16,144,384]{2,1,0:T(8,128)(2,1)S(1)}, u32[]{:S(2)}, u32[]{:S(2)}) async-start(bf16[16,144,384]{2,1,0:T(8,128)(2,1)} %bitcast.56), calls=%async_computation.1 | async-start | bytes 3538944 | tf_op jit(solution)/shard_map/all_to_all | solution.py:20
  53.6 1.0 dynamic-slice_bitcast_fusion.1
  54.8 21.0 %all-to-all-done.1 = bf16[16,144,384]{2,1,0:T(8,128)(2,1)S(1)} async-done(((bf16[16,144,384]{2,1,0:T(8,128)(2,1)}), bf16[16,144,384]{2,1,0:T(8,128)(2,1)S(1)}, u32[]{:S(2)}, u32[]{:S(2)}) %all-to-all-start.1) | async-done | bytes 1769504 | tf_op jit(solution)/shard_map/all_to_all | solution.py:20
  76.0 11.7 %all-gather.6.cloned.1.call-done = bf16[2304,384]{1,0:T(8,128)(2,1)} async-done(((bf16[144,384]{1,0:T(8,128)(2,1)}), bf16[2304,384]{1,0:T(8,128)(2,1)}) %all-gather.6.cloned.1.call-update) | async-done | bytes 1769488 | tf_op jit(solution)/shard_map/all_gather | solution.py:308
  88.1 1.2 copy-done.2
  89.2 2.4 pad_maximum_fusion
  91.6 6.3 %all-to-all-start.2 = ((bf16[16,336,384]{2,1,0:T(8,128)(2,1)}), bf16[16,336,384]{2,1,0:T(8,128)(2,1)}, u32[]{:S(2)}, u32[]{:S(2)}) async-start(bf16[16,336,384]{2,1,0:T(8,128)(2,1)} %pad_maximum_fusion), calls=%async_computation.2 | async-start | bytes 8257536 | tf_op jit(solution)/shard_map/all_to_all | solution.py:20
  98.0 0.7 collective-permute-start.1
  98.7 0.6 copy-done.5
  99.4 60.7 %all-to-all-done.2.own_ref = bf16[16,336,384]{2,1,0:T(8,128)(2,1)} async-done(((bf16[16,336,384]{2,1,0:T(8,128)(2,1)}), bf16[16,336,384]{2,1,0:T(8,128)(2,1)}, u32[]{:S(2)}, u32[]{:S(2)}) %all-to-all-start.2) | async-done | bytes 4128800 | tf_op jit(solution)/shard_map/all_to_all | solution.py:20
  160.1 1.9 slice.38
  162.0 11.0 %collective-permute-start = (bf16[16,192,384]{2,1,0:T(8,128)(2,1)S(1)}, bf16[16,192,384]{2,1,0:T(8,128)(2,1)}, u32[]{:S(2)}, u32[]{:S(2)}) collective-permute-start(bf16[16,192,384]{2,1,0:T(8,128)(2,1)S(1)} %slice.38), channel_id=1, source_target_pairs={{0,16},{16,0},{1,17},{17,1},{2,18},{18,2},{3,19},{19,3},{4,20},{20... | collective-permute-start | bytes 7077896 | tf_op jit(solution)/shard_map/ppermute | solution.py:358
  173.1 2.0 multiply_reduce_fusion
  175.0 1.7 slice_convert_fusion
  176.8 1.6 fusion.1.near_ref.far_ref
  178.4 5.3 %times_weights.2 = f32[16,40,384]{2,1,0:T(8,128)} custom-call(s32[1]{0:T(128)} %bitcast.core_ref, bf16[16,336,384]{2,1,0:T(8,128)(2,1)} %all-to-all-done.2.own_ref, bf16[16,192,384]{2,1,0:T(8,128)(2,1)} %collective-permute-done.other_ref, bf16[2304,384]{1,0:T(8,128)(2,1)} %fusion.1.near_ref.far_ref, bf16[2304,384]{1,0:T(8,128)(2,1)} %fusion.1.near_ref.far_ref), custom_call_target="tpu_custom_call" | custom-call | flops 1132462080 | bytes 4718592 | tf_op jit(solution)/shard_map/times_weights/pallas_call | solution.py:211
  183.7 7.0 %all-gather.4.cloned.1.call-done.near_ref.far_ref = bf16[2304,384]{1,0:T(8,128)(2,1)} async-done(((bf16[144,384]{1,0:T(8,128)(2,1)}), bf16[2304,384]{1,0:T(8,128)(2,1)}) %all-gather.4.cloned.1.call-update) | async-done | bytes 1769488 | tf_op jit(solution)/shard_map/all_gather | solution.py:321
  190.7 4.4 %times_weights.3 = f32[16,24,384]{2,1,0:T(8,128)} custom-call(s32[1]{0:T(128)} %bitcast.core_ref, bf16[16,336,384]{2,1,0:T(8,128)(2,1)} %all-to-all-done.2.own_ref, bf16[16,192,384]{2,1,0:T(8,128)(2,1)} %collective-permute-done.other_ref, bf16[2304,384]{1,0:T(8,128)(2,1)} %all-gather.4.cloned.1.call-done.near_ref.far_ref, ...), custom_call_target="tpu_custom_call" | custom-call | flops 679477248 | bytes 3538944 | tf_op jit(solution)/shard_map/times_weights/pallas_call | solution.py:211
  195.1 1.6 fusion.12
  196.7 0.9 pad_maximum_fusion.1.ahead_ref
  197.7 0.9 maximum_maximum_fusion.back_ref
  198.6 6.0 %make_deltas.1 = bf16[32,56,1152]{2,1,0:T(8,128)(2,1)} custom-call(bf16[16,40,384]{2,1,0:T(8,128)(2,1)} %pad_maximum_fusion.1.ahead_ref, bf16[16,24,384]{2,1,0:T(8,128)(2,1)} %maximum_maximum_fusion.back_ref, bf16[16,2,72,384]{3,2,1,0:T(8,128)(2,1)} %bitcast.54, bf16[16,2,72,384]{3,2,1,0:T(8,128)(2,1)} %bitcast.55), custom_call_target="tpu_custom_call" | custom-call | flops 1811939328 | bytes 7667712 | tf_op jit(solution)/shard_map/make_deltas/pallas_call | solution.py:264
  204.5 67.0 %all_to_all.35.block_ref.owned_ref = bf16[32,56,1152]{2,1,0:T(8,128)(2,1)} all-to-all(bf16[32,56,1152]{2,1,0:T(8,128)(2,1)} %make_deltas.1), channel_id=1, replica_groups=mesh['z'=16,'core'=2,'x'=4,'y'=4] {'core','x','y'}, dimensions={0} | all-to-all | bytes 8257536 | tf_op jit(solution)/shard_map/all_to_all | solution.py:20
  271.5 6.2 %pair_products.1 = f32[32,8,128]{2,1,0:T(8,128)} custom-call(bf16[32,56,1152]{2,1,0:T(8,128)(2,1)} %all_to_all.35.block_ref.owned_ref), custom_call_target="tpu_custom_call" | custom-call | flops 1056964608 | bytes 4128768 | tf_op jit(solution)/shard_map/pair_products/pallas_call | solution.py:77
  277.7 12.5 %all_to_all.36 = f32[32,8,128]{2,1,0:T(8,128)S(1)} all-to-all(f32[32,8,128]{2,1,0:T(8,128)} %pair_products.1), channel_id=1, replica_groups=mesh['z'=16,'core'=2,'x'=4,'y'=4] {'core','x','y'}, dimensions={0} | all-to-all | bytes 262144 | tf_op jit(solution)/shard_map/all_to_all | solution.py:20
  290.2 0.6 broadcast_in_dim.14
  290.9 7.7 %all-to-all-start.5 = ((f32[16,8,128]{2,1,0:T(8,128)}), f32[16,8,128]{2,1,0:T(8,128)S(1)}, u32[]{:S(2)}, u32[]{:S(2)}) async-start(f32[16,8,128]{2,1,0:T(8,128)} %broadcast_in_dim.14), calls=%async_computation.5 | async-start | bytes 131072 | tf_op jit(solution)/shard_map/all_to_all | solution.py:20
  298.8 0.6 reshape.74.neighbours_ref
  299.4 10.8 %all-to-all-done.5.parts_ref = f32[16,8,128]{2,1,0:T(8,128)S(1)} async-done(((f32[16,8,128]{2,1,0:T(8,128)}), f32[16,8,128]{2,1,0:T(8,128)S(1)}, u32[]{:S(2)}, u32[]{:S(2)}) %all-to-all-start.5) | async-done | bytes 65568 | tf_op jit(solution)/shard_map/all_to_all | solution.py:20
  310.2 0.6 copy-done.3
  310.8 4.5 %finish.1 = (bf16[16,56,72]{2,1,0:T(8,128)(2,1)}, f32[1,32]{1,0:T(1,128)}) custom-call(f32[16,8,128]{2,1,0:T(8,128)} %copy-done.3, s32[1,32]{1,0:T(1,128)} %reshape.74.neighbours_ref, bf16[32,56,1152]{2,1,0:T(8,128)(2,1)} %all_to_all.35.block_ref.owned_ref), custom_call_target="tpu_custom_call" | custom-call | flops 4128768 | bytes 4257792 | tf_op jit(solution)/shard_map/finish/pallas_call | solution.py:143
  315.3 3.8 %all-to-all-start.6 = ((bf16[16,56,72]{2,1,0:T(8,128)(2,1)}), bf16[16,56,72]{2,1,0:T(8,128)(2,1)S(1)}, u32[]{:S(2)}, u32[]{:S(2)}) async-start(bf16[16,56,72]{2,1,0:T(8,128)(2,1)} %get-tuple-element.14), calls=%async_computation.6 | async-start | bytes 458752 | tf_op jit(solution)/shard_map/all_to_all | solution.py:20
  319.1 0.5 broadcast.92
  319.6 1.3 reduce.5
  321.1 0.6 reshape.79
  321.7 9.9 %all-to-all-done.6 = bf16[16,56,72]{2,1,0:T(8,128)(2,1)S(1)} async-done(((bf16[16,56,72]{2,1,0:T(8,128)(2,1)}), bf16[16,56,72]{2,1,0:T(8,128)(2,1)S(1)}, u32[]{:S(2)}, u32[]{:S(2)}) %all-to-all-start.6) | async-done | bytes 129056 | tf_op jit(solution)/shard_map/all_to_all | solution.py:20
  331.7 0.8 copy.18
  332.5 0.8 copy.19
  333.3 0.8 copy.20
  (48 shorter events, 2.5 us)
Async XLA Ops:
  7.2 11.9 %copy-start = (bf16[2304,288]{0,1:T(8,128)(2,1)S(1)}, bf16[2304,288]{0,1:T(8,128)(2,1)}, u32[]{:S(2)}) copy-start(bf16[2304,288]{0,1:T(8,128)(2,1)} %param.11) | copy-start | bytes 3981316
  9.5 30.2 %copy-start.6 = (f32[2304]{0:T(1024)S(1)}, f32[2304]{0:T(1024)}, u32[]{:S(2)}) copy-start(f32[2304]{0:T(1024)} %param.9) | copy-start | bytes 27652
  9.5 29.8 %all-to-all-start = ((bf16[16,144,384]{2,1,0:T(8,128)(2,1)}), bf16[16,144,384]{2,1,0:T(8,128)(2,1)S(1)}, u32[]{:S(2)}, u32[]{:S(2)}) async-start(bf16[16,144,384]{2,1,0:T(8,128)(2,1)} %broadcast_in_dim.11), calls=%async_computation | async-start | bytes 3538944 | tf_op jit(solution)/shard_map/all_to_all | solution.py:20
  17.3 70.5 %all-gather.6.cloned.1.call-start = ((), (), s32[]{:S(2)}) async-start(), calls=%async_computation.8 | async-start | bytes 1880064 | tf_op jit(solution)/shard_map/all_gather | solution.py:308
  39.3 1.3 copy-start.7
  47.3 28.7 %copy-start.4 = (bf16[1,384,144]{1,2,0:T(8,128)(2,1)S(1)}, bf16[1,384,144]{1,2,0:T(8,128)(2,1)}, u32[]{:S(2)}) copy-start(bf16[1,384,144]{1,2,0:T(8,128)(2,1)} %param.8) | copy-start | bytes 331780
  47.3 28.4 %all-to-all-start.1 = ((bf16[16,144,384]{2,1,0:T(8,128)(2,1)}), bf16[16,144,384]{2,1,0:T(8,128)(2,1)S(1)}, u32[]{:S(2)}, u32[]{:S(2)}) async-start(bf16[16,144,384]{2,1,0:T(8,128)(2,1)} %bitcast.56), calls=%async_computation.1 | async-start | bytes 3538944 | tf_op jit(solution)/shard_map/all_to_all | solution.py:20
  87.8 1.5 copy-start.2
  91.6 68.5 %all-to-all-start.2 = ((bf16[16,336,384]{2,1,0:T(8,128)(2,1)}), bf16[16,336,384]{2,1,0:T(8,128)(2,1)}, u32[]{:S(2)}, u32[]{:S(2)}) async-start(bf16[16,336,384]{2,1,0:T(8,128)(2,1)} %pad_maximum_fusion), calls=%async_computation.2 | async-start | bytes 8257536 | tf_op jit(solution)/shard_map/all_to_all | solution.py:20
  98.0 92.7 %all-gather.4.cloned.1.call-start = ((), (), s32[]{:S(2)}) async-start(), calls=%async_computation.7 | async-start | bytes 1880064 | tf_op jit(solution)/shard_map/all_gather | solution.py:321
  98.0 0.7 collective-permute-start.1
  98.7 0.6 copy-start.5
  162.0 16.4 %collective-permute-start = (bf16[16,192,384]{2,1,0:T(8,128)(2,1)S(1)}, bf16[16,192,384]{2,1,0:T(8,128)(2,1)}, u32[]{:S(2)}, u32[]{:S(2)}) collective-permute-start(bf16[16,192,384]{2,1,0:T(8,128)(2,1)S(1)} %slice.38), channel_id=1, source_target_pairs={{0,16},{16,0},{1,17},{17,1},{2,18},{18,2},{3,19},{19,3},{4,20},{20... | collective-permute-start | bytes 7077896 | tf_op jit(solution)/shard_map/ppermute | solution.py:358
  183.7 11.4 %copy-start.1 = (f32[16,40,384]{2,1,0:T(8,128)S(1)}, f32[16,40,384]{2,1,0:T(8,128)}, u32[]{:S(2)}) copy-start(f32[16,40,384]{2,1,0:T(8,128)} %times_weights.2) | copy-start | bytes 2949124
  271.5 27.1 %copy-start.8 = (s32[32]{0:T(128)S(1)}, s32[32]{0:T(128)}, u32[]{:S(2)}) copy-start(s32[32]{0:T(128)} %param.13) | copy-start | bytes 388
  290.9 19.3 %all-to-all-start.5 = ((f32[16,8,128]{2,1,0:T(8,128)}), f32[16,8,128]{2,1,0:T(8,128)S(1)}, u32[]{:S(2)}, u32[]{:S(2)}) async-start(f32[16,8,128]{2,1,0:T(8,128)} %broadcast_in_dim.14), calls=%async_computation.5 | async-start | bytes 131072 | tf_op jit(solution)/shard_map/all_to_all | solution.py:20
  310.2 0.6 copy-start.3
  315.3 16.3 %all-to-all-start.6 = ((bf16[16,56,72]{2,1,0:T(8,128)(2,1)}), bf16[16,56,72]{2,1,0:T(8,128)(2,1)S(1)}, u32[]{:S(2)}, u32[]{:S(2)}) async-start(bf16[16,56,72]{2,1,0:T(8,128)(2,1)} %get-tuple-element.14), calls=%async_computation.6 | async-start | bytes 458752 | tf_op jit(solution)/shard_map/all_to_all | solution.py:20
Sparse Core Ops, SparseCore 0:
  20.1 67.5 all-gather.5
  101.4 89.2 all-gather.3
